TPU v7x, 32 devices: a whole 2x2x4 slice. The times are simulated.
32 devices in a mesh: ctx: 32 (over z, y, x, core).
Axes of the slice: x: 2, y: 2, z: 4, core: 2. Of those that a mesh axis runs over, the one named last changes fastest.
Arguments:
- tokens: bfloat16 [16384, 1536], P('ctx'), may hold values from -6 to 6
- cotangent: bfloat16 [16384, 1536], P('ctx'), may hold values from -6 to 6
- doc_lengths: int32 [8], replicated, may hold values from 1 to 8192, 16384 in all
- adapter_ids: int32 [8], replicated, may hold values from 0 to 7
- w_query: bfloat16 [1536, 1536], P('ctx'), may hold values from -0.15625 to 0.15625
- w_keyval: bfloat16 [1536, 256], P('ctx'), may hold values from -0.15625 to 0.15625
- w_output: bfloat16 [1536, 1536], P('ctx'), may hold values from -2.5 to 2.5
- w_gateup: bfloat16 [1536, 9216], P('ctx'), may hold values from -0.15625 to 0.15625
- w_down: bfloat16 [4608, 1536], P('ctx'), may hold values from -0.09375 to 0.09375
- gain_attn: float32 [1536], replicated, may hold values from 0.25 to 1.75
- gain_mlp: float32 [1536], replicated, may hold values from 0.25 to 1.75
- query_a: bfloat16 [1536, 128], replicated, may hold values from -0.15625 to 0.15625
- query_b: bfloat16 [128, 1536], replicated, may hold values from -0.75 to 0.75
- keyval_a: bfloat16 [1536, 128], replicated, may hold values from -0.15625 to 0.15625
- keyval_b: bfloat16 [128, 256], replicated, may hold values from -0.75 to 0.75
- output_a: bfloat16 [1536, 128], replicated, may hold values from -0.15625 to 0.15625
- output_b: bfloat16 [128, 1536], replicated, may hold values from -0.75 to 0.75
- gateup_a: bfloat16 [1536, 128], replicated, may hold values from -0.15625 to 0.15625
- gateup_b: bfloat16 [128, 9216], replicated, may hold values from -0.75 to 0.75
- down_a: bfloat16 [4608, 128], replicated, may hold values from -0.09375 to 0.09375
- down_b: bfloat16 [128, 1536], replicated, may hold values from -0.75 to 0.75
Outputs:
- out: bfloat16 [16384, 1536], P('ctx')
- grad_tokens: bfloat16 [16384, 1536], P('ctx')
- grad_query_a: float32 [1536, 128], replicated
- grad_query_b: float32 [128, 1536], replicated
- grad_keyval_a: float32 [1536, 128], replicated
- grad_keyval_b: float32 [128, 256], replicated
- grad_output_a: float32 [1536, 128], replicated
- grad_output_b: float32 [128, 1536], replicated
- grad_gateup_a: float32 [1536, 128], replicated
- grad_gateup_b: float32 [128, 9216], replicated
- grad_down_a: float32 [4608, 128], replicated
- grad_down_b: float32 [128, 1536], replicated
Inputs may be any that keep to these rules, and one draw needn't show every extreme that they name: `doc_lengths`: the documents follow one another over all 16384 positions; the longest has exactly 8192 tokens.
All inputs are finite; a program needn't handle non-finite values.
Results may differ from a plain program's by a relative error of at most 0.015.
Values may be sent and summed in bfloat16 or wider, within the bound.
A program may use at most 320 MiB of HBM per device.

v0:
```python
import jax
import jax.numpy as jnp
from jax import lax
from jax.sharding import PartitionSpec as P

HEADS = 12
HD = 128
FF = 4608
WINDOW = 1024
RANK = 16
ADAPTERS = 8


NORM_EPS = 1e-06
MASKED = -1e30


def shifted(x, axis, by):
    size = lax.axis_size(axis)
    pairs = [(i, i + by) for i in range(size) if 0 <= i + by < size]
    return lax.ppermute(x, axis, pairs)


def segment_of(doc_lengths, positions):
    starts = jnp.cumsum(doc_lengths) - doc_lengths
    return jnp.sum((starts[None, :] <= positions[:, None]).astype(jnp.int32), axis=1) - 1


def adapter_mask(doc_lengths, adapter_ids, positions):
    segment = segment_of(doc_lengths, positions)
    owner = segment[:, None] == jnp.arange(doc_lengths.shape[0], dtype=jnp.int32)[None, :]
    chosen = jnp.sum(jnp.where(owner, adapter_ids[None, :], 0), axis=1)
    columns = jnp.arange(ADAPTERS * RANK, dtype=jnp.int32) // RANK
    return (segment, (columns[None, :] == chosen[:, None]).astype(jnp.float32))


def rms_scale(values, gain):
    return values * lax.rsqrt(jnp.mean(values * values, axis=-1, keepdims=True) + NORM_EPS) * gain


def by_rows(left, right):
    return lax.dot_general(
        left, right, (((0,), (0,)), ((), ())), preferred_element_type=jnp.float32
    )


def by_cols(left, right):
    return lax.dot_general(
        left, right, (((1,), (1,)), ((), ())), preferred_element_type=jnp.float32
    )


def adapted(inputs, weight, down_part, up_part, mask):
    inner = (jnp.dot(inputs, down_part, preferred_element_type=jnp.float32) * mask).astype(
        jnp.bfloat16
    )
    return (
        jnp.dot(inputs, weight, preferred_element_type=jnp.float32)
        + jnp.dot(inner, up_part, preferred_element_type=jnp.float32),
        inner,
    )


def adapter_back(grad_out, inputs, inner, up_part, mask):
    grad_up = by_rows(inner, grad_out)
    grad_inner = (by_cols(grad_out, up_part) * mask).astype(jnp.bfloat16)
    return (by_rows(inputs, grad_inner), grad_up, grad_inner)


def owner_of(block, count, width):
    device_of = jnp.where(block < count, block, 2 * count - 1 - block)
    return (device_of, jnp.where(block < count, 0, width))


def key_block(table, first_device, block, count, width):
    device_of, row_in = owner_of(block, count, width)
    piece = lax.dynamic_slice(
        table, (device_of - first_device, row_in, jnp.int32(0)), (1, width, table.shape[2])
    )
    return piece[0]


def block_scores(query, keys, allowed):
    rows = query.shape[0]
    heads = query.reshape(rows, HEADS, HD)
    raw = jnp.einsum(
        "rhd,kd->rhk", heads, keys[:, :HD], preferred_element_type=jnp.float32
    ) * HD ** (-0.5)
    return jnp.where(allowed[:, None, :], raw, MASKED)


def attend_forward(query, keys, allowed):
    scores = block_scores(query, keys, allowed)
    top = jnp.max(scores, axis=-1, keepdims=True)
    total = jnp.sum(jnp.exp(scores - top), axis=-1, keepdims=True)
    log_total = top + jnp.log(total)
    weights = jnp.exp(scores - log_total).astype(jnp.bfloat16)
    mixed = jnp.einsum("rhk,kd->rhd", weights, keys[:, HD:], preferred_element_type=jnp.float32)
    return (mixed.reshape(query.shape[0], -1), log_total)


def attend_backward(query, keys, allowed, log_total, grad_out):
    rows = query.shape[0]
    prob = jnp.exp(block_scores(query, keys, allowed) - log_total)
    grad_heads = grad_out.reshape(rows, HEADS, HD)
    grad_prob = jnp.einsum(
        "rhd,kd->rhk", grad_heads, keys[:, HD:], preferred_element_type=jnp.float32
    )
    delta = jnp.sum(prob * grad_prob, axis=-1, keepdims=True)
    grad_scores = (prob * (grad_prob - delta)).astype(jnp.bfloat16)
    scale = HD ** (-0.5)
    grad_query = (
        jnp.einsum("rhk,kd->rhd", grad_scores, keys[:, :HD], preferred_element_type=jnp.float32)
        * scale
    )
    grad_key = (
        jnp.einsum(
            "rhk,rhd->kd",
            grad_scores,
            query.reshape(rows, HEADS, HD),
            preferred_element_type=jnp.float32,
        )
        * scale
    )
    grad_value = jnp.einsum(
        "rhk,rhd->kd", prob.astype(jnp.bfloat16), grad_heads, preferred_element_type=jnp.float32
    )
    return (grad_query.reshape(rows, -1), jnp.concatenate([grad_key, grad_value], axis=1))


def local(
    tokens,
    cotangent,
    doc_lengths,
    adapter_ids,
    w_query,
    w_keyval,
    w_output,
    w_gateup,
    w_down,
    gain_attn,
    gain_mlp,
    query_a,
    query_b,
    keyval_a,
    keyval_b,
    output_a,
    output_b,
    gateup_a,
    gateup_b,
    down_a,
    down_b,
):
    count = lax.axis_size("ctx")
    device = lax.axis_index("ctx")
    local_rows = tokens.shape[0]
    width = local_rows // 2
    reach = (WINDOW + width - 1) // width
    key_width = w_keyval.shape[1]
    half_rows = jnp.arange(width, dtype=jnp.int32)
    own_blocks = (device, 2 * count - 1 - device)
    positions = jnp.concatenate(
        [own_blocks[0] * width + half_rows, own_blocks[1] * width + half_rows]
    )
    segment, mask = adapter_mask(doc_lengths, adapter_ids, positions)
    resid = tokens.astype(jnp.float32)
    act_one = rms_scale(resid, gain_attn).astype(jnp.bfloat16)
    full_query, full_keyval, full_output, full_gateup = (
        lax.all_gather(w_query, "ctx", axis=0, tiled=True),
        lax.all_gather(w_keyval, "ctx", axis=0, tiled=True),
        lax.all_gather(w_output, "ctx", axis=0, tiled=True),
        lax.all_gather(w_gateup, "ctx", axis=0, tiled=True),
    )
    query_full, inner_query = adapted(act_one, full_query, query_a, query_b, mask)
    keyval_full, inner_keyval = adapted(act_one, full_keyval, keyval_a, keyval_b, mask)
    query = query_full.astype(jnp.bfloat16)
    keyval = keyval_full.astype(jnp.bfloat16)
    stacked = [keyval]
    for offset in range(1, reach + 1):
        later = shifted(keyval, "ctx", -offset)
        prior = shifted(keyval, "ctx", offset)
        stacked = [prior] + stacked + [later]
    table = jnp.stack(stacked)
    first_device = device - reach
    kept = []
    mixed_parts = []
    for which in range(2):
        block = own_blocks[which]
        key_blocks = [block - reach + step for step in range(reach + 1)]
        keys = jnp.concatenate(
            [key_block(table, first_device, entry, count, width) for entry in key_blocks], axis=0
        )
        key_pos = jnp.concatenate([entry * width + half_rows for entry in key_blocks])
        key_seg = segment_of(doc_lengths, key_pos)
        query_pos = positions[which * width : (which + 1) * width]
        query_seg = segment[which * width : (which + 1) * width]
        allowed = (
            (key_pos[None, :] <= query_pos[:, None])
            & (query_pos[:, None] - key_pos[None, :] < WINDOW)
            & (key_seg[None, :] == query_seg[:, None])
        )
        mixed, log_total = attend_forward(query[which * width : (which + 1) * width], keys, allowed)
        kept.append((key_blocks, keys, allowed, log_total))
        mixed_parts.append(mixed)
    attention = jnp.concatenate(mixed_parts, axis=0).astype(jnp.bfloat16)
    branch_one, inner_output = adapted(attention, full_output, output_a, output_b, mask)
    middle = resid + branch_one
    act_two = rms_scale(middle, gain_mlp).astype(jnp.bfloat16)
    gate_up, inner_gateup = adapted(act_two, full_gateup, gateup_a, gateup_b, mask)
    gate = gate_up[:, :FF]
    upper = gate_up[:, FF:]
    hidden = (jax.nn.gelu(gate) * upper).astype(jnp.bfloat16)
    down_main = jnp.dot(
        hidden,
        lax.all_gather(w_down, "ctx", axis=0, tiled=True),
        preferred_element_type=jnp.float32,
    )
    inner_down = (jnp.dot(hidden, down_a, preferred_element_type=jnp.float32) * mask).astype(
        jnp.bfloat16
    )
    result = middle + (down_main + jnp.dot(inner_down, down_b, preferred_element_type=jnp.float32))
    grad_down_a, grad_down_b, d_inner_down = adapter_back(
        cotangent, hidden, inner_down, down_b, mask
    )
    grad_hidden = by_cols(cotangent, lax.all_gather(w_down, "ctx", axis=0, tiled=True)) + by_cols(
        d_inner_down, down_a
    )

    def gated(gate_part, up_part):
        return jax.nn.gelu(gate_part) * up_part

    unused, pull_glu = jax.vjp(gated, gate, upper)
    grad_gate, grad_up = pull_glu(grad_hidden)
    grad_gateup = jnp.concatenate([grad_gate, grad_up], axis=1).astype(jnp.bfloat16)
    grad_gateup_a, grad_gateup_b, d_inner_gateup = adapter_back(
        grad_gateup, act_two, inner_gateup, gateup_b, mask
    )
    grad_act_two = by_cols(grad_gateup, full_gateup) + by_cols(d_inner_gateup, gateup_a)
    unused, pull_two = jax.vjp(lambda values: rms_scale(values, gain_mlp), middle)
    grad_middle = cotangent.astype(jnp.float32) + pull_two(grad_act_two)[0]
    grad_branch = grad_middle.astype(jnp.bfloat16)
    grad_output_a, grad_output_b, d_inner_output = adapter_back(
        grad_branch, attention, inner_output, output_b, mask
    )
    grad_attention = (by_cols(grad_branch, full_output) + by_cols(d_inner_output, output_a)).astype(
        jnp.bfloat16
    )
    query_grads = []
    key_grads = []
    for which in range(2):
        key_blocks, keys, allowed, log_total = kept[which]
        rows_query = query[which * width : (which + 1) * width]
        rows_grad = grad_attention[which * width : (which + 1) * width]
        grad_rows, grad_keys = attend_backward(rows_query, keys, allowed, log_total, rows_grad)
        query_grads.append(grad_rows)
        for step, entry in enumerate(key_blocks):
            key_grads.append((entry, grad_keys[step * width : (step + 1) * width]))
    grad_query = jnp.concatenate(query_grads, axis=0).astype(jnp.bfloat16)
    slots = jnp.zeros((2 * reach + 1, local_rows, key_width), jnp.float32)
    for entry, piece in key_grads:
        device_of, row_in = owner_of(entry, count, width)
        slot = device_of - first_device
        current = lax.dynamic_slice(slots, (slot, row_in, jnp.int32(0)), (1, width, key_width))
        slots = lax.dynamic_update_slice(slots, current + piece[None], (slot, row_in, jnp.int32(0)))
    grad_keyval_full = slots[reach]
    for offset in range(1, reach + 1):
        from_lower = shifted(slots[reach + offset].astype(jnp.bfloat16), "ctx", offset).astype(
            jnp.float32
        )
        from_upper = shifted(slots[reach - offset].astype(jnp.bfloat16), "ctx", -offset).astype(
            jnp.float32
        )
        grad_keyval_full = grad_keyval_full + from_lower + from_upper
    grad_keyval = grad_keyval_full.astype(jnp.bfloat16)
    grad_query_a, grad_query_b, d_inner_query = adapter_back(
        grad_query, act_one, inner_query, query_b, mask
    )
    grad_keyval_a, grad_keyval_b, d_inner_keyval = adapter_back(
        grad_keyval, act_one, inner_keyval, keyval_b, mask
    )
    grad_act_one = (
        by_cols(grad_query, full_query)
        + by_cols(grad_keyval, full_keyval)
        + by_cols(d_inner_query, query_a)
        + by_cols(d_inner_keyval, keyval_a)
    )
    unused, pull_one = jax.vjp(lambda values: rms_scale(values, gain_attn), resid)
    grad_tokens = (grad_middle + pull_one(grad_act_one)[0]).astype(jnp.bfloat16)
    sums = lax.psum(
        (
            grad_query_a,
            grad_query_b,
            grad_keyval_a,
            grad_keyval_b,
            grad_output_a,
            grad_output_b,
            grad_gateup_a,
            grad_gateup_b,
            grad_down_a,
            grad_down_b,
        ),
        "ctx",
    )
    return (
        result.astype(jnp.bfloat16),
        grad_tokens,
        sums[0],
        sums[1],
        sums[2],
        sums[3],
        sums[4],
        sums[5],
        sums[6],
        sums[7],
        sums[8],
        sums[9],
    )


def solution(mesh):
    in_specs = (
        P("ctx", None),
        P("ctx", None),
        P(),
        P(),
        P("ctx", None),
        P("ctx", None),
        P("ctx", None),
        P("ctx", None),
        P("ctx", None),
        P(),
        P(),
        P(),
        P(),
        P(),
        P(),
        P(),
        P(),
        P(),
        P(),
        P(),
        P(),
    )
    out_specs = (P("ctx", None), P("ctx", None), P(), P(), P(), P(), P(), P(), P(), P(), P(), P())
    return jax.shard_map(local, mesh=mesh, in_specs=in_specs, out_specs=out_specs, check_vma=False)
```

profile of v0, /device:TPU:0, one launch (start us, length us, event | category | flops | bytes accessed | tf_op | source)
XLA Modules:
  0.0 927.8 jit_solution(5665380332954114076)
XLA Ops:
  12.4 1.8 fusion.17
  14.2 1.9 fusion.19
  16.8 46.3 %all_gather.17 = bf16[1536,256]{1,0:T(8,128)(2,1)S(1)} all-gather(bf16[48,256]{1,0:T(8,128)(2,1)S(1)} %copy-done.66), channel_id=1, replica_groups=mesh['ctx'=32] {'ctx'}, dimensions={0}, use_global_device_ids=true | all-gather | bytes 811008 | tf_op jit(solution)/shard_map/all_gather | solution.py:170
  64.2 2.0 collective-permute-start
  66.2 2.0 collective-permute-start.1
  68.2 2.3 collective-permute-start.2
  70.5 2.6 collective-permute-start.3
  74.8 2.6 fusion.35
  79.1 2.8 fusion.39
  81.8 2.5 collective-permute-done
  88.9 1.5 collective-permute-start.7
  93.4 2.0 collective-permute-done.5
  95.4 1.7 collective-permute-done.6
  97.1 4.3 collective-permute-done.7
  105.1 5.0 fusion.130
  114.3 4.8 fusion
  119.1 4.3 exponential_reduce_fusion.1
  124.6 4.1 fusion.1
  128.7 4.3 exponential_reduce_fusion
  133.1 8.4 convolution_convert_fusion.1
  141.6 5.1 convolution_convert_fusion
  148.2 12.7 %all-gather.7.cloned.1.call-done = bf16[1536,1536]{1,0:T(8,128)(2,1)} async-done(((bf16[48,1536]{1,0:T(8,128)(2,1)}), bf16[1536,1536]{1,0:T(8,128)(2,1)}) %all-gather.7.cloned.1.call-update) | async-done | bytes 4718608 | tf_op jit(solution)/shard_map/all_gather | solution.py:171
  160.9 5.1 fusion.57
  166.9 1.7 copy-done.4
  170.7 95.2 %all-gather.11.cloned.1.call-done = bf16[4608,1536]{1,0:T(8,128)(2,1)} async-done(((bf16[144,1536]{1,0:T(8,128)(2,1)}), bf16[4608,1536]{1,0:T(8,128)(2,1)}) %all-gather.11.cloned.1.call-update) | async-done | bytes 14155792 | tf_op jit(solution)/shard_map/all_gather | solution.py:215
  265.9 13.3 %fusion.134 = f32[512,4608]{1,0:T(8,128)} fusion(bf16[512,1536]{1,0:T(8,128)(2,1)} %param.22, bf16[4608,1536]{1,0:T(8,128)(2,1)} %all-gather.11.cloned.1.call-done), kind=kOutput, calls=%fused_computation.270 | convolution fusion | flops 7247757312 | bytes 25165824 | tf_op jit(solution)/shard_map/dot_general | solution.py:48
  279.2 157.3 %all-gather.9.cloned.1.call-done = bf16[1536,9216]{1,0:T(8,128)(2,1)} async-done(((bf16[48,9216]{1,0:T(8,128)(2,1)}), bf16[1536,9216]{1,0:T(8,128)(2,1)}) %all-gather.9.cloned.1.call-update) | async-done | bytes 28311568 | tf_op jit(solution)/shard_map/all_gather | solution.py:172
  436.5 23.3 %fusion.132 = f32[512,9216]{1,0:T(8,128)} fusion(bf16[512,1536]{1,0:T(8,128)(2,1)} %copy-done.25, bf16[1536,9216]{1,0:T(8,128)(2,1)} %all-gather.9.cloned.1.call-done), kind=kOutput, calls=%fused_computation.268 | convolution fusion | flops 14495514624 | bytes 48758784 | tf_op jit(solution)/shard_map/dot_general | solution.py:58
  459.8 12.3 %convolution_add_fusion = f32[512,9216]{1,0:T(8,128)} fusion(f32[512,9216]{1,0:T(8,128)} %fusion.132, bf16[512,128]{1,0:T(8,128)(2,1)S(1)} %fusion.38, bf16[128,9216]{1,0:T(8,128)(2,1)S(1)} %copy-done), kind=kOutput, calls=%fused_computation.10 | convolution fusion | flops 1212678144 | bytes 40239104 | tf_op jit(solution)/shard_map/dot_general | solution.py:59
  472.1 18.9 %fusion.8 = (bf16[512,4608]{1,0:T(8,128)(2,1)}, bf16[512,4608]{1,0:T(8,128)(2,1)}, bf16[512,4608]{1,0:T(8,128)(2,1)}) fusion(f32[512,9216]{1,0:T(8,128)} %convolution_add_fusion, f32[512,4608]{1,0:T(8,128)} %fusion.134, bf16[512,128]{1,0:T(8,128)(2,1)S(1)} %copy-done.58, bf16[4608,128]{1,0:T(8,128)(2,1)S(1)} %copy-done.71), kind=kOutput, calls=%fused_computation.21 | convolution fusion | flops 667680768 | bytes 43778048 | tf_op jit(solution)/shard_map/dot_general | solution.py:48
  491.0 7.6 fusion.24
  498.7 2.6 fusion.44
  501.3 21.7 %fusion.26 = f32[512,1536]{1,0:T(8,128)} fusion(bf16[1536,9216]{1,0:T(8,128)(2,1)} %all-gather.9.cloned.1.call-done, bf16[512,4608]{1,0:T(8,128)(2,1)} %get-tuple-element.25, bf16[512,4608]{1,0:T(8,128)(2,1)} %get-tuple-element.24), kind=kOutput, calls=%fused_computation.62 | convolution fusion | flops 14514388992 | bytes 40894464 | tf_op jit(solution)/shard_map/dot_general | solution.py:48
  523.0 3.7 multiply_reduce_fusion.2
  528.7 2.6 fusion.117
  533.2 12.1 %multiply_reduce_fusion = (f32[256,12]{0,1:T(8,128)S(1)}, f32[256,12,1280]{2,0,1:T(8,128)}) fusion(f32[256,12,1280]{2,0,1:T(8,128)} %copy-done.2, f32[256,12]{0,1:T(8,128)S(1)} %copy-done.55, pred[256,1280]{1,0:T(8,128)(4,1)S(1)} %copy-done.18, bf16[256,12,128]{0,2,1:T(8,128)(2,1)S(1)} %bitcast.271, bf16[1280,256]{1,0:T(8,128)(2,1)} %get-tuple-element.36), kind=kOutput, calls=%fused_computation.1 | convolution fusion | flops 1026290688 | bytes 32923648 | tf_op jit(solution)/shard_map/rhd,kd->rhk/dot_general | solution.py:106
  545.3 8.0 convolution_bitcast_fusion
  553.6 12.0 %multiply_reduce_fusion.1 = (f32[256,12]{0,1:T(8,128)S(1)}, f32[256,12,1280]{2,0,1:T(8,128)}) fusion(f32[256,12,1280]{2,0,1:T(8,128)} %copy-done.3, f32[256,12]{0,1:T(8,128)S(1)} %copy-done.57, pred[256,1280]{1,0:T(8,128)(4,1)S(1)} %copy-done.20, bf16[256,12,128]{0,2,1:T(8,128)(2,1)S(1)} %bitcast.273, bf16[1280,256]{1,0:T(8,128)(2,1)} %get-tuple-element.35), kind=kOutput, calls=%fused_computation.3 | convolution fusion | flops 1026290688 | bytes 32923648 | tf_op jit(solution)/shard_map/rhd,kd->rhk/dot_general | solution.py:106
  565.6 7.7 convolution_bitcast_fusion.2
  573.3 12.1 %multiply_convert_fusion.1 = bf16[256,12,1280]{2,0,1:T(8,128)(2,1)S(1)} fusion(f32[256,12,1280]{2,0,1:T(8,128)} %get-tuple-element.62, f32[256,12,1280]{2,0,1:T(8,128)} %copy-done.3, f32[256,12]{0,1:T(8,128)S(1)} %get-tuple-element.61, f32[256,12]{0,1:T(8,128)S(1)} %copy-done.57, pred[256,1280]{1,0:T(8,128)(4,1)S(1)} %copy-done.20), kind=kLoop, calls=%fused_computation.2 | loop fusion | flops 23592960 | bytes 39673856 | tf_op jit(solution)/shard_map/convert_element_type | solution.py:110
  585.5 4.4 multiply_convert_fusion.6
  591.1 8.3 multiply_convert_fusion
  599.4 3.8 multiply_convert_fusion.5
  607.4 1.5 fusion.138
  608.9 2.8 fusion.139
  613.8 1.5 fusion.135
  617.1 3.5 collective-permute-start.10
  621.9 3.8 collective-permute-start.12
  627.1 5.9 collective-permute-start.14
  635.6 2.3 collective-permute-start.8
  637.9 1.4 collective-permute-start.9
  639.4 1.5 fusion.54
  640.9 1.5 fusion.56
  642.4 9.9 %collective-permute-done.14 = bf16[512,256]{0,1:T(8,128)(2,1)S(1)} collective-permute-done((bf16[512,256]{0,1:T(8,128)(2,1)S(1)}, bf16[512,256]{0,1:T(8,128)(2,1)S(1)}, u32[]{:S(2)}, u32[]{:S(2)}) %collective-permute-start.14) | collective-permute-done | bytes 262176 | tf_op jit(solution)/shard_map/ppermute | solution.py:21
  653.8 1.5 fusion.136
  655.4 12.4 %fusion.133 = f32[512,1536]{1,0:T(8,128)S(1)} fusion(bf16[512,4608]{1,0:T(8,128)(2,1)} %get-tuple-element.26, bf16[4608,1536]{1,0:T(8,128)(2,1)} %all-gather.11.cloned.1.call-done), kind=kOutput, calls=%fused_computation.269 | convolution fusion | flops 7247757312 | bytes 22020096 | tf_op jit(solution)/shard_map/dot_general | solution.py:213
  667.8 1.7 fusion.21
  669.6 2.7 fusion.55
  676.7 1.9 fusion.16
  678.6 226.8 %all-reduce.3.cloned.1.call-done = (f32[1536,128]{1,0:T(8,128)}, f32[128,1536]{1,0:T(8,128)}, f32[1536,128]{1,0:T(8,128)}, f32[128,256]{1,0:T(8,128)}, f32[1536,...) async-done(((f32[1536,128]{1,0:T(8,128)}, f32[128,1536]{1,0:T(8,128)}, ...) | async-done | bytes 12714000 | tf_op jit(solution)/shard_map/psum | solution.py:289
  905.4 2.2 copy.127
  907.6 2.2 copy.128
  909.8 2.1 copy.129
  915.2 2.4 copy.134
  (302 shorter events, 62.2 us)
Async XLA Ops:
  7.2 452.6 %copy-start = (bf16[128,9216]{1,0:T(8,128)(2,1)S(1)}, bf16[128,9216]{1,0:T(8,128)(2,1)}, u32[]{:S(2)}) copy-start(bf16[128,9216]{1,0:T(8,128)(2,1)} %param.39) | copy-start | bytes 7077892
  7.2 8.9 copy-start.46
  7.2 97.9 %all-gather.5.cloned.1.call-start = ((), (), s32[]{:S(2)}) async-start(), calls=%async_computation | async-start | bytes 4866048 | tf_op jit(solution)/shard_map/all_gather | solution.py:169
  7.9 153.0 %all-gather.7.cloned.1.call-start = ((), (), s32[]{:S(2)}) async-start(), calls=%async_computation.1 | async-start | bytes 4866048 | tf_op jit(solution)/shard_map/all_gather | solution.py:171
  8.7 257.2 %all-gather.11.cloned.1.call-start = ((), (), s32[]{:S(2)}) async-start(), calls=%async_computation.3 | async-start | bytes 14598144 | tf_op jit(solution)/shard_map/all_gather | solution.py:215
  9.4 7.3 copy-start.66
  9.4 427.1 %all-gather.9.cloned.1.call-start = ((), (), s32[]{:S(2)}) async-start(), calls=%async_computation.2 | async-start | bytes 29196288 | tf_op jit(solution)/shard_map/all_gather | solution.py:172
  10.0 895.4 %all-reduce.3.cloned.1.call-start = ((), (), s32[]{:S(2)}) async-start(), calls=%async_computation.4 | async-start | bytes 25427968 | tf_op jit(solution)/shard_map/psum | solution.py:289
  14.2 49.5 %copy-start.69 = (f32[512]{0:T(512)}, f32[512]{0:T(512)S(1)}, u32[]{:S(2)}) copy-start(f32[512]{0:T(512)S(1)} %fusion.103) | copy-start | bytes 6148
  14.2 49.7 %copy-start.62 = (bf16[128,256]{1,0:T(8,128)(2,1)S(1)}, bf16[128,256]{1,0:T(8,128)(2,1)}, u32[]{:S(2)}) copy-start(bf16[128,256]{1,0:T(8,128)(2,1)} %param.35) | copy-start | bytes 196612
  16.1 47.0 %copy-start.12 = (bf16[512,1536]{1,0:T(8,128)(2,1)}, bf16[512,1536]{1,0:T(8,128)(2,1)S(1)}, u32[]{:S(2)}) copy-start(bf16[512,1536]{1,0:T(8,128)(2,1)S(1)} %fusion.19) | copy-start | bytes 4718596
  16.1 58.6 %copy-start.52 = (bf16[1536,128]{1,0:T(8,128)(2,1)S(1)}, bf16[1536,128]{1,0:T(8,128)(2,1)}, u32[]{:S(2)}) copy-start(bf16[1536,128]{1,0:T(8,128)(2,1)} %param.32) | copy-start | bytes 1179652
  16.7 53.8 %copy-start.41 = (bf16[512,128]{1,0:T(8,128)(2,1)}, bf16[512,128]{1,0:T(8,128)(2,1)S(1)}, u32[]{:S(2)}) copy-start(bf16[512,128]{1,0:T(8,128)(2,1)S(1)} %fusion.36) | copy-start | bytes 393220
  16.8 62.3 %copy-start.44 = (bf16[128,1536]{1,0:T(8,128)(2,1)S(1)}, bf16[128,1536]{1,0:T(8,128)(2,1)}, u32[]{:S(2)}) copy-start(bf16[128,1536]{1,0:T(8,128)(2,1)} %param.41) | copy-start | bytes 1179652
  64.2 20.1 %collective-permute-start = (bf16[512,256]{1,0:T(8,128)(2,1)S(1)}, bf16[512,256]{1,0:T(8,128)(2,1)}, u32[]{:S(2)}, u32[]{:S(2)}) collective-permute-start(bf16[512,256]{1,0:T(8,128)(2,1)S(1)} %fusion.33), channel_id=1, source_target_pairs={{0,4},{1,5},{2,6},{3,7},{4,8},{5,9},{6,10},{7,11},{8,12},{9,13},{1... | collective-permute-start | bytes 786440 | tf_op jit(solution)/shard_map/ppermute | solution.py:21
  66.2 20.4 %collective-permute-start.1 = (bf16[512,256]{1,0:T(8,128)(2,1)S(1)}, bf16[512,256]{1,0:T(8,128)(2,1)}, u32[]{:S(2)}, u32[]{:S(2)}) collective-permute-start(bf16[512,256]{1,0:T(8,128)(2,1)S(1)} %fusion.33), channel_id=1, source_target_pairs={{0,3},{1,4},{2,5},{3,6},{4,7},{5,8},{6,9},{7,10},{8,11},{9,12},{10... | collective-permute-start | bytes 786440 | tf_op jit(solution)/shard_map/ppermute | solution.py:21
  68.2 20.7 %collective-permute-start.2 = (bf16[512,256]{1,0:T(8,128)(2,1)S(1)}, bf16[512,256]{1,0:T(8,128)(2,1)}, u32[]{:S(2)}, u32[]{:S(2)}) collective-permute-start(bf16[512,256]{1,0:T(8,128)(2,1)S(1)} %fusion.33), channel_id=1, source_target_pairs={{0,2},{1,3},{2,4},{3,5},{4,6},{5,7},{6,8},{7,9},{8,10},{9,11},{10,... | collective-permute-start | bytes 786440 | tf_op jit(solution)/shard_map/ppermute | solution.py:21
  70.5 20.8 %collective-permute-start.3 = (bf16[512,256]{1,0:T(8,128)(2,1)S(1)}, bf16[512,256]{1,0:T(8,128)(2,1)}, u32[]{:S(2)}, u32[]{:S(2)}) collective-permute-start(bf16[512,256]{1,0:T(8,128)(2,1)S(1)} %fusion.33), channel_id=1, source_target_pairs={{0,1},{1,2},{2,3},{3,4},{4,5},{5,6},{6,7},{7,8},{8,9},{9,10},{10,1... | collective-permute-start | bytes 786440 | tf_op jit(solution)/shard_map/ppermute | solution.py:21
  73.1 19.2 %collective-permute-start.4 = (bf16[512,256]{1,0:T(8,128)(2,1)S(1)}, bf16[512,256]{1,0:T(8,128)(2,1)}, u32[]{:S(2)}, u32[]{:S(2)}) collective-permute-start(bf16[512,256]{1,0:T(8,128)(2,1)S(1)} %fusion.33), channel_id=1, source_target_pairs={{1,0},{2,1},{3,2},{4,3},{5,4},{6,5},{7,6},{8,7},{9,8},{10,9},{11,1... | collective-permute-start | bytes 786440 | tf_op jit(solution)/shard_map/ppermute | solution.py:21
  79.0 62.5 %copy-start.17 = (pred[256,1280]{1,0:T(8,128)(4,1)}, pred[256,1280]{1,0:T(8,128)(4,1)S(1)}, u32[]{:S(2)}) copy-start(pred[256,1280]{1,0:T(8,128)(4,1)S(1)} %fusion.32) | copy-start | bytes 983044
  84.3 11.1 %collective-permute-start.5 = (bf16[512,256]{1,0:T(8,128)(2,1)S(1)}, bf16[512,256]{1,0:T(8,128)(2,1)S(1)}, u32[]{:S(2)}, u32[]{:S(2)}) collective-permute-start(bf16[512,256]{1,0:T(8,128)(2,1)S(1)} %fusion.33), channel_id=1, source_target_pairs={{2,0},{3,1},{4,2},{5,3},{6,4},{7,5},{8,6},{9,7},{10,8},{11,9},{12,... | collective-permute-start | bytes 786440 | tf_op jit(solution)/shard_map/ppermute | solution.py:21
  86.6 10.5 %collective-permute-start.6 = (bf16[512,256]{1,0:T(8,128)(2,1)S(1)}, bf16[512,256]{1,0:T(8,128)(2,1)S(1)}, u32[]{:S(2)}, u32[]{:S(2)}) collective-permute-start(bf16[512,256]{1,0:T(8,128)(2,1)S(1)} %fusion.33), channel_id=1, source_target_pairs={{3,0},{4,1},{5,2},{6,3},{7,4},{8,5},{9,6},{10,7},{11,8},{12,9},{13... | collective-permute-start | bytes 786440 | tf_op jit(solution)/shard_map/ppermute | solution.py:21
  88.9 12.5 %collective-permute-start.7 = (bf16[512,256]{1,0:T(8,128)(2,1)S(1)}, bf16[512,256]{1,0:T(8,128)(2,1)S(1)}, u32[]{:S(2)}, u32[]{:S(2)}) collective-permute-start(bf16[512,256]{1,0:T(8,128)(2,1)S(1)} %fusion.33), channel_id=1, source_target_pairs={{4,0},{5,1},{6,2},{7,3},{8,4},{9,5},{10,6},{11,7},{12,8},{13,9},{1... | collective-permute-start | bytes 786440 | tf_op jit(solution)/shard_map/ppermute | solution.py:21
  114.3 10.3 %copy-start.14 = (bf16[256,1536]{0,1:T(8,128)(2,1)}, bf16[256,1536]{0,1:T(8,128)(2,1)S(1)}, u32[]{:S(2)}) copy-start(bf16[256,1536]{0,1:T(8,128)(2,1)S(1)} %copy.60) | copy-start | bytes 2359300
  124.6 8.5 copy-start.56
  128.7 12.8 %copy-start.2 = (f32[256,12,1280]{2,0,1:T(8,128)}, f32[256,12,1280]{2,0,1:T(8,128)S(1)}, u32[]{:S(2)}) copy-start(f32[256,12,1280]{2,0,1:T(8,128)S(1)} %get-tuple-element.52) | copy-start | bytes 47185924
  133.0 8.5 copy-start.54
  148.2 17.9 %copy-start.39 = (bf16[512,128]{1,0:T(8,128)(2,1)}, bf16[512,128]{1,0:T(8,128)(2,1)S(1)}, u32[]{:S(2)}) copy-start(bf16[512,128]{1,0:T(8,128)(2,1)S(1)} %fusion.37) | copy-start | bytes 393220
  148.2 17.9 %copy-start.30 = (bf16[128,1536]{1,0:T(8,128)(2,1)S(1)}, bf16[128,1536]{1,0:T(8,128)(2,1)}, u32[]{:S(2)}) copy-start(bf16[128,1536]{1,0:T(8,128)(2,1)} %param.37) | copy-start | bytes 1179652
  459.8 12.3 %copy-start.58 = (bf16[512,128]{1,0:T(8,128)(2,1)S(1)}, bf16[512,128]{1,0:T(8,128)(2,1)}, u32[]{:S(2)}) copy-start(bf16[512,128]{1,0:T(8,128)(2,1)} %fusion.39) | copy-start | bytes 393220
  459.8 12.3 %copy-start.71 = (bf16[4608,128]{1,0:T(8,128)(2,1)S(1)}, bf16[4608,128]{1,0:T(8,128)(2,1)}, u32[]{:S(2)}) copy-start(bf16[4608,128]{1,0:T(8,128)(2,1)} %param.40) | copy-start | bytes 3538948
  491.0 7.6 copy-start.77
  491.0 7.6 copy-start.78
  545.3 8.0 copy-start.28
  545.3 8.3 copy-start.20
  545.3 8.3 copy-start.57
  573.3 17.8 %slice-start = ((s8[15728640]{0:T(1024)(128)(4,1)}), s8[4194304]{0:T(1024)(128)(4,1)S(1)}, s32[]{:S(2)}) async-start(s8[15728640]{0:T(1024)(128)(4,1)} %bitcast.263), calls=%async_computation.5 | async-start | bytes 8388608
  573.3 17.8 %slice-start.1 = ((s8[15728640]{0:T(1024)(128)(4,1)}), s8[4194304]{0:T(1024)(128)(4,1)S(1)}, s32[]{:S(2)}) async-start(s8[15728640]{0:T(1024)(128)(4,1)} %bitcast.263), calls=%async_computation.6 | async-start | bytes 8388608
  573.3 17.8 %slice-start.2 = ((s8[15728640]{0:T(1024)(128)(4,1)}), s8[4194304]{0:T(1024)(128)(4,1)S(1)}, s32[]{:S(2)}) async-start(s8[15728640]{0:T(1024)(128)(4,1)} %bitcast.263), calls=%async_computation.7 | async-start | bytes 8388608
  589.8 49.5 %copy-start.31 = (bf16[256,12,128]{0,2,1:T(8,128)(2,1)}, bf16[256,12,128]{0,2,1:T(8,128)(2,1)S(1)}, u32[]{:S(2)}) copy-start(bf16[256,12,128]{0,2,1:T(8,128)(2,1)S(1)} %multiply_convert_fusion.6) | copy-start | bytes 2359300
  599.4 9.5 %slice-start.4 = ((s8[4718592]{0:T(1024)(128)(4,1)}), s8[524288]{0:T(1024)(128)(4,1)S(1)}, s32[]{:S(2)}) async-start(s8[4718592]{0:T(1024)(128)(4,1)} %bitcast.269), calls=%async_computation.9 | async-start | bytes 1048576
  603.2 36.2 %copy-start.33 = (bf16[256,12,128]{0,2,1:T(8,128)(2,1)}, bf16[256,12,128]{0,2,1:T(8,128)(2,1)S(1)}, u32[]{:S(2)}) copy-start(bf16[256,12,128]{0,2,1:T(8,128)(2,1)S(1)} %multiply_convert_fusion.5) | copy-start | bytes 2359300
  616.6 16.4 %copy-start.24 = (bf16[512,1536]{1,0:T(8,128)(2,1)S(1)}, bf16[512,1536]{1,0:T(8,128)(2,1)}, u32[]{:S(2)}) copy-start(bf16[512,1536]{1,0:T(8,128)(2,1)} %param.22) | copy-start | bytes 4718596
  617.0 22.4 %copy-start.60 = (bf16[512,128]{1,0:T(8,128)(2,1)S(1)}, bf16[512,128]{1,0:T(8,128)(2,1)}, u32[]{:S(2)}) copy-start(bf16[512,128]{1,0:T(8,128)(2,1)} %fusion.35) | copy-start | bytes 393220
  617.0 24.0 %copy-start.74 = (bf16[256,12,128]{0,2,1:T(8,128)(2,1)S(1)}, bf16[256,12,128]{0,2,1:T(8,128)(2,1)}, u32[]{:S(2)}) copy-start(bf16[256,12,128]{0,2,1:T(8,128)(2,1)} %copy-done.73) | copy-start | bytes 2359300
  617.0 24.0 %copy-start.76 = (bf16[256,12,128]{0,2,1:T(8,128)(2,1)S(1)}, bf16[256,12,128]{0,2,1:T(8,128)(2,1)}, u32[]{:S(2)}) copy-start(bf16[256,12,128]{0,2,1:T(8,128)(2,1)} %copy-done.75) | copy-start | bytes 2359300
  617.1 17.2 %collective-permute-start.10 = (bf16[512,256]{0,1:T(8,128)(2,1)S(1)}, bf16[512,256]{0,1:T(8,128)(2,1)S(1)}, u32[]{:S(2)}, u32[]{:S(2)}) collective-permute-start(bf16[512,256]{0,1:T(8,128)(2,1)S(1)} %get-tuple-element.33), channel_id=1, source_target_pairs={{0,2},{1,3},{2,4},{3,5},{4,6},{5,7},{6,8},{7,9},{8,10},{9,11},{10,... | collective-permute-start | bytes 786440 | tf_op jit(solution)/shard_map/ppermute | solution.py:21
  620.6 15.0 %collective-permute-start.11 = (bf16[512,256]{0,1:T(8,128)(2,1)S(1)}, bf16[512,256]{0,1:T(8,128)(2,1)S(1)}, u32[]{:S(2)}, u32[]{:S(2)}) collective-permute-start(bf16[512,256]{0,1:T(8,128)(2,1)S(1)} %get-tuple-element.32), channel_id=1, source_target_pairs={{2,0},{3,1},{4,2},{5,3},{6,4},{7,5},{8,6},{9,7},{10,8},{11,9},{12,... | collective-permute-start | bytes 786440 | tf_op jit(solution)/shard_map/ppermute | solution.py:21
  621.9 16.0 %collective-permute-start.12 = (bf16[512,256]{0,1:T(8,128)(2,1)S(1)}, bf16[512,256]{0,1:T(8,128)(2,1)S(1)}, u32[]{:S(2)}, u32[]{:S(2)}) collective-permute-start(bf16[512,256]{0,1:T(8,128)(2,1)S(1)} %get-tuple-element.31), channel_id=1, source_target_pairs={{0,3},{1,4},{2,5},{3,6},{4,7},{5,8},{6,9},{7,10},{8,11},{9,12},{10... | collective-permute-start | bytes 786440 | tf_op jit(solution)/shard_map/ppermute | solution.py:21
  625.8 16.6 %collective-permute-start.13 = (bf16[512,256]{0,1:T(8,128)(2,1)S(1)}, bf16[512,256]{0,1:T(8,128)(2,1)S(1)}, u32[]{:S(2)}, u32[]{:S(2)}) collective-permute-start(bf16[512,256]{0,1:T(8,128)(2,1)S(1)} %get-tuple-element.30), channel_id=1, source_target_pairs={{3,0},{4,1},{5,2},{6,3},{7,4},{8,5},{9,6},{10,7},{11,8},{12,9},{13... | collective-permute-start | bytes 786440 | tf_op jit(solution)/shard_map/ppermute | solution.py:21
  627.1 25.2 %collective-permute-start.14 = (bf16[512,256]{0,1:T(8,128)(2,1)S(1)}, bf16[512,256]{0,1:T(8,128)(2,1)S(1)}, u32[]{:S(2)}, u32[]{:S(2)}) collective-permute-start(bf16[512,256]{0,1:T(8,128)(2,1)S(1)} %get-tuple-element.29), channel_id=1, source_target_pairs={{0,4},{1,5},{2,6},{3,7},{4,8},{5,9},{6,10},{7,11},{8,12},{9,13},{1... | collective-permute-start | bytes 786440 | tf_op jit(solution)/shard_map/ppermute | solution.py:21
  634.3 17.9 %collective-permute-start.15 = (bf16[512,256]{0,1:T(8,128)(2,1)S(1)}, bf16[512,256]{0,1:T(8,128)(2,1)S(1)}, u32[]{:S(2)}, u32[]{:S(2)}) collective-permute-start(bf16[512,256]{0,1:T(8,128)(2,1)S(1)} %get-tuple-element.28), channel_id=1, source_target_pairs={{4,0},{5,1},{6,2},{7,3},{8,4},{9,5},{10,6},{11,7},{12,8},{13,9},{1... | collective-permute-start | bytes 786440 | tf_op jit(solution)/shard_map/ppermute | solution.py:21
  635.6 16.6 %collective-permute-start.8 = (bf16[512,256]{0,1:T(8,128)(2,1)S(1)}, bf16[512,256]{0,1:T(8,128)(2,1)S(1)}, u32[]{:S(2)}, u32[]{:S(2)}) collective-permute-start(bf16[512,256]{0,1:T(8,128)(2,1)S(1)} %get-tuple-element.27), channel_id=1, source_target_pairs={{0,1},{1,2},{2,3},{3,4},{4,5},{5,6},{6,7},{7,8},{8,9},{9,10},{10,1... | collective-permute-start | bytes 786440 | tf_op jit(solution)/shard_map/ppermute | solution.py:21
  637.9 14.7 %copy-start.63 = (bf16[128,256]{1,0:T(8,128)(2,1)S(1)}, bf16[128,256]{1,0:T(8,128)(2,1)}, u32[]{:S(2)}) copy-start(bf16[128,256]{1,0:T(8,128)(2,1)} %param.35) | copy-start | bytes 196612
  637.9 14.4 %collective-permute-start.9 = (bf16[512,256]{0,1:T(8,128)(2,1)S(1)}, bf16[512,256]{0,1:T(8,128)(2,1)S(1)}, u32[]{:S(2)}, u32[]{:S(2)}) collective-permute-start(bf16[512,256]{0,1:T(8,128)(2,1)S(1)} %get-tuple-element.34), channel_id=1, source_target_pairs={{1,0},{2,1},{3,2},{4,3},{5,4},{6,5},{7,6},{8,7},{9,8},{10,9},{11,1... | collective-permute-start | bytes 786440 | tf_op jit(solution)/shard_map/ppermute | solution.py:21
  640.9 12.0 %copy-start.42 = (bf16[512,128]{1,0:T(8,128)(2,1)S(1)}, bf16[512,128]{1,0:T(8,128)(2,1)}, u32[]{:S(2)}) copy-start(bf16[512,128]{1,0:T(8,128)(2,1)} %copy-done.41) | copy-start | bytes 393220
  655.3 14.3 %slice-start.6 = ((s8[4718592]{0:T(1024)(128)(4,1)}), s8[524288]{0:T(1024)(128)(4,1)S(1)}, s32[]{:S(2)}) async-start(s8[4718592]{0:T(1024)(128)(4,1)} %bitcast.281), calls=%async_computation.11 | async-start | bytes 1048576
  655.3 12.5 %copy-start.6 = (f32[512,1536]{1,0:T(8,128)S(1)}, f32[512,1536]{1,0:T(8,128)}, u32[]{:S(2)}) copy-start(f32[512,1536]{1,0:T(8,128)} %copy-done.4) | copy-start | bytes 9437188
  655.3 12.5 %copy-start.45 = (bf16[128,1536]{1,0:T(8,128)(2,1)S(1)}, bf16[128,1536]{1,0:T(8,128)(2,1)}, u32[]{:S(2)}) copy-start(bf16[128,1536]{1,0:T(8,128)(2,1)} %param.41) | copy-start | bytes 1179652
  655.3 14.2 %slice-start.7 = ((s8[4718592]{0:T(1024)(128)(4,1)}), s8[4194304]{0:T(1024)(128)(4,1)S(1)}, s32[]{:S(2)}) async-start(s8[4718592]{0:T(1024)(128)(4,1)} %bitcast.281), calls=%async_computation.12 | async-start | bytes 8388608
  905.4 7.2 copy-start.38
  905.4 8.0 copy-start.37
  905.4 8.9 copy-start.36
  907.6 7.6 copy-start.27
  (46 other events, 139.9 us)
Sparse Core Ops, SparseCore 0:
  10.9 78.0 all-gather.4
  92.0 68.8 all-gather.6
  163.8 102.0 all-gather.10
  268.6 167.8 all-gather.8
  655.4 249.8 all-reduce.2
where the time goes:
time: 933 us; the launch traced here: 928 us
  waiting for transfers between devices  515 us (55%)
  matrix products  234 us (25%)
  blocking collectives  46.3 us (5%)
  other arithmetic  41.2 us (4%)
  local copies, waits for them, and re-layouts  40.2 us (4%)
  starting transfers between devices  35.2 us (4%)
  between operations  15.5 us (2%)
    psum x1, waiting for transfers between devices, local(): lax.psum((grad_query_a, grad_query_b, grad_keyval_a, grad_keyval_b, grad_...  227 us
    all_gather x1, waiting for transfers between devices, local(): lax.all_gather(w_gateup, 'ctx', axis=0, tiled=True)  157 us
    all_gather x1, waiting for transfers between devices, local(): lax.all_gather(w_down, 'ctx', axis=0, tiled=True)  95.2 us
    dot_general x15, matrix products, by_cols(): lax.dot_general(left, right, (((1,), (1,)), ((), ())), preferred_element_...  72.4 us
    all_gather x1, blocking collectives, local(): lax.all_gather(w_keyval, 'ctx', axis=0, tiled=True)  46.3 us
    ppermute x16, starting transfers between devices, shifted(): return lax.ppermute(x, axis, pairs)  35 us
    dot_general x4, matrix products, adapted(): jnp.dot(inputs, weight, preferred_element_type=jnp.float32)  34 us
    unnamed x200, local copies, waits for them, and re-layouts  33.7 us
  transfers between devices with their start and end apart: 21, of which 9 were waited for; matrix products, arithmetic and copies ran while one was open for 12% of the time, Pallas kernels for 0%

commit v1 on v0

--- a/solution.py
+++ b/solution.py
@@ -1,6 +1,10 @@
+import functools
+
 import jax
 import jax.numpy as jnp
 from jax import lax
+from jax.experimental import pallas as pl
+from jax.experimental.pallas import tpu as pltpu
 from jax.sharding import PartitionSpec as P
 
 HEADS = 12
@@ -13,6 +17,185 @@
 
 NORM_EPS = 1e-06
 MASKED = -1e30
+MESH = pl.DeviceIdType.MESH
+
+ORD_A = (4, 3, 1, 2, 0)
+ORD_A2 = (4, 3, 2, 1, 0)
+ORD_B = (4, 1, 2, 3, 0)
+ORD_B2 = (4, 2, 1, 3, 0)
+ORD_C = (4, 2, 3, 1, 0)
+ORD_C2 = (4, 1, 3, 2, 0)
+LAGS = (0, 1, 2, 4, 6)
+
+
+def gather_units():
+    units = [
+        [(0, 0, 6, ORD_A), (0, 6, 5, ORD_C), (0, 11, 1, ORD_B), (1, 0, 2, ORD_B)],
+        [(2, 0, 5, ORD_A), (2, 5, 4, ORD_C), (2, 9, 3, ORD_B)],
+    ]
+    sets = ((ORD_A, ORD_C, ORD_B), (ORD_A2, ORD_C2, ORD_B2))
+    for i in range(3):
+        first, second, third = sets[i % 2]
+        units.append([(4, 4 * i, 2, first), (4, 4 * i + 2, 1, second), (4, 4 * i + 3, 1, third)])
+    for i in range(12):
+        first, second, third = sets[i % 2]
+        units.append(
+            [(3, 3 * i, 3, first), (3, 36 + 3 * i, 2, second), (3, 36 + 3 * i + 2, 1, third)]
+        )
+    return units
+
+
+def gather_kernel(parts, events, *refs):
+    count = 5
+    src, dst = refs[:count], refs[count : 2 * count]
+    send_sem, recv_sem, own_sem = refs[2 * count :]
+    me = lax.axis_index("ctx")
+    bits = [(me // (1 << b)) % 2 for b in range(5)]
+    barrier = pltpu.get_barrier_semaphore()
+    for b in range(5):
+        pl.semaphore_signal(barrier, 1, device_id=flip(me, bits, b), device_id_type=MESH)
+    pl.semaphore_wait(barrier, 5)
+    own = []
+    for w in range(count):
+        copy = pltpu.make_async_copy(
+            src[w], dst[w].at[bits[4], bits[3], bits[2], bits[1], bits[0]], own_sem.at[w]
+        )
+        copy.start()
+        own.append(copy)
+
+    def exchange(p, k):
+        w, tile, tiles, order = parts[p]
+        bit, have = order[k], order[:k]
+        where = tuple(pl.ds(0, 2) if b in have else bits[b] for b in (4, 3, 2, 1, 0))
+        cols = pl.ds(tile * 128, tiles * 128)
+        there = dst[w].at[where + (slice(None), cols)]
+        return pltpu.make_async_remote_copy(
+            there if k else src[w].at[:, cols],
+            there,
+            send_sem.at[p, k],
+            recv_sem.at[p, k],
+            device_id=flip(me, bits, bit),
+            device_id_type=MESH,
+        )
+
+    waited = set()
+    for p, k in events:
+        if k:
+            if parts[p][0] not in waited:
+                waited.add(parts[p][0])
+                own[parts[p][0]].wait()
+            exchange(p, k - 1).wait_recv()
+        exchange(p, k).start()
+    for p in range(len(parts)):
+        exchange(p, 4).wait_recv()
+    for p in range(len(parts)):
+        for k in range(5):
+            exchange(p, k).wait_send()
+
+
+def gather_weights(weights):
+    units = gather_units()
+    parts = [part for unit in units for part in unit]
+    unit_of = [i for i, unit in enumerate(units) for part in unit]
+    events = sorted(
+        ((unit_of[p] + LAGS[k], -k, p, k) for p in range(len(parts)) for k in range(5))
+    )
+    events = [(p, k) for _, _, p, k in events]
+    out = pl.pallas_call(
+        functools.partial(gather_kernel, parts, events),
+        out_shape=[jax.ShapeDtypeStruct((2,) * 5 + w.shape, w.dtype) for w in weights],
+        in_specs=[pl.BlockSpec(memory_space=pl.ANY)] * len(weights),
+        out_specs=[pl.BlockSpec(memory_space=pl.ANY)] * len(weights),
+        scratch_shapes=[
+            pltpu.SemaphoreType.DMA((len(parts), 5)),
+            pltpu.SemaphoreType.DMA((len(parts), 5)),
+            pltpu.SemaphoreType.DMA((len(weights),)),
+        ],
+        compiler_params=pltpu.CompilerParams(collective_id=0, has_side_effects=True),
+    )(*weights)
+    return [x.reshape(-1, x.shape[-1]) for x in out]
+
+
+def flip(me, bits, b):
+    return (me+(1-2*bits[b])*(1<<b),)
+def reduce_kernel(rows, in_ref, out_ref, r0, r1, r2, r3, r4, ssem, rsem):
+    rb=(r0,r1,r2,r3,r4)
+    me=lax.axis_index("ctx")
+    bits=[(me//(1<<b))%2 for b in range(5)]
+    bar=pltpu.get_barrier_semaphore()
+    for b in range(5):
+        pl.semaphore_signal(bar,1,device_id=flip(me,bits,b),device_id_type=MESH)
+    pl.semaphore_wait(bar,5)
+    t=rows//16
+    a=round(t*3/7); bb=round(t*3/14)
+    classes=[(0,a*16,ORD_A),(a*16,bb*16,ORD_B),((a+bb)*16,rows-(a+bb)*16,ORD_C)]
+    def rs(cl,s):
+        r0_,n,order=classes[cl]
+        red=order[::-1]
+        bit=red[s]; done=red[:s]
+        rem=[b for b in (4,3,2,1,0) if b not in done]
+        src=in_ref if s==0 else rb[s-1]
+        idx=tuple((1-bits[b]) if b==bit else slice(None) for b in rem)
+        return pltpu.make_async_remote_copy(src.at[idx+(pl.ds(r0_,n),)],rb[s].at[(slice(None),)*(4-s)+(pl.ds(r0_,n),)],ssem.at[cl,s],rsem.at[cl,s],device_id=flip(me,bits,bit),device_id_type=MESH)
+    def add(cl,s):
+        r0_,n,order=classes[cl]
+        red=order[::-1]
+        bit=red[s]; done=red[:s]
+        rem=[b for b in (4,3,2,1,0) if b not in done]
+        src=in_ref if s==0 else rb[s-1]
+        rs_=pl.ds(r0_,n)
+        nd=4-s
+        def body(j,_):
+            ds=[(j//(1<<(nd-1-i)))%2 for i in range(nd)]
+            it=iter(ds)
+            si=tuple(bits[b] if b==bit else next(it) for b in rem)
+            v=src[si+(rs_,)].astype(jnp.float32)+rb[s][tuple(ds)+(rs_,)].astype(jnp.float32)
+            rb[s][tuple(ds)+(rs_,)]=v.astype(jnp.bfloat16)
+            return 0
+        lax.fori_loop(0,1<<nd,body,0)
+    def ag(cl,k):
+        r0_,n,order=classes[cl]
+        bit=order[k]; have=order[:k]
+        idx=tuple(slice(None) if b in have else bits[b] for b in (4,3,2,1,0))+(pl.ds(r0_,n),)
+        src=out_ref.at[idx] if k else rb[4].at[pl.ds(r0_,n)]
+        return pltpu.make_async_remote_copy(src,out_ref.at[idx],ssem.at[cl,5+k],rsem.at[cl,5+k],device_id=flip(me,bits,bit),device_id_type=MESH)
+    for cl in range(3): rs(cl,0).start()
+    for s in range(5):
+        for cl in range(3):
+            rs(cl,s).wait_recv()
+            add(cl,s)
+            if s<4: rs(cl,s+1).start()
+            else:
+                ag(cl,0).start()
+                r0_,n,_=classes[cl]
+                out_ref[bits[4],bits[3],bits[2],bits[1],bits[0],pl.ds(r0_,n)]=rb[4][pl.ds(r0_,n)]
+    for k in range(1,5):
+        for cl in range(3):
+            ag(cl,k-1).wait_recv()
+            ag(cl,k).start()
+    for cl in range(3): ag(cl,4).wait_recv()
+    for cl in range(3):
+        for s in range(5):
+            rs(cl,s).wait_send(); ag(cl,s).wait_send()
+def reduce_packed(x, cid=1):
+    import functools
+    rows=x.shape[5]
+    return pl.pallas_call(functools.partial(reduce_kernel,rows),
+        out_shape=jax.ShapeDtypeStruct(x.shape,x.dtype),
+        in_specs=[pl.BlockSpec(memory_space=pltpu.VMEM)],out_specs=pl.BlockSpec(memory_space=pltpu.VMEM),
+        scratch_shapes=[pltpu.VMEM((2,)*(4-s)+(rows,128),jnp.bfloat16) for s in range(5)]+[pltpu.SemaphoreType.DMA((3,10)),pltpu.SemaphoreType.DMA((3,10))],
+        compiler_params=pltpu.CompilerParams(collective_id=cid,has_side_effects=True,vmem_limit_bytes=40<<20))(x)
+def pack(grads):
+    ps=[g.reshape(g.shape[0]//16,16,g.shape[1]//128,128).transpose(0,2,1,3).reshape(-1,128).astype(jnp.bfloat16) for g in grads]
+    n=sum(p.shape[0] for p in ps); tot=-(-n//512)*512
+    if tot>n: ps.append(jnp.zeros((tot-n,128),jnp.bfloat16))
+    return jnp.concatenate(ps,0).reshape((2,)*5+(tot//32,128))
+def unpack(x,shapes):
+    x=x.reshape(-1,128); out=[]; o=0
+    for r,c in shapes:
+        n=r*c//128
+        out.append(x[o:o+n].reshape(r//16,c//128,16,128).transpose(0,2,1,3).reshape(r,c).astype(jnp.float32)); o+=n
+    return out
 
 
 def shifted(x, axis, by):
@@ -165,12 +348,13 @@
     segment, mask = adapter_mask(doc_lengths, adapter_ids, positions)
     resid = tokens.astype(jnp.float32)
     act_one = rms_scale(resid, gain_attn).astype(jnp.bfloat16)
-    full_query, full_keyval, full_output, full_gateup = (
-        lax.all_gather(w_query, "ctx", axis=0, tiled=True),
-        lax.all_gather(w_keyval, "ctx", axis=0, tiled=True),
-        lax.all_gather(w_output, "ctx", axis=0, tiled=True),
-        lax.all_gather(w_gateup, "ctx", axis=0, tiled=True),
-    )
+    own = count == 32 and w_query.shape[0] % 16 == 0
+    weights = (w_query, w_keyval, w_output, w_gateup, w_down)
+    if own:
+        full = gather_weights(weights)
+    else:
+        full = [lax.all_gather(w, "ctx", axis=0, tiled=True) for w in weights]
+    full_query, full_keyval, full_output, full_gateup, full_down = full
     query_full, inner_query = adapted(act_one, full_query, query_a, query_b, mask)
     keyval_full, inner_keyval = adapted(act_one, full_keyval, keyval_a, keyval_b, mask)
     query = query_full.astype(jnp.bfloat16)
@@ -212,7 +396,7 @@
     hidden = (jax.nn.gelu(gate) * upper).astype(jnp.bfloat16)
     down_main = jnp.dot(
         hidden,
-        lax.all_gather(w_down, "ctx", axis=0, tiled=True),
+        full_down,
         preferred_element_type=jnp.float32,
     )
     inner_down = (jnp.dot(hidden, down_a, preferred_element_type=jnp.float32) * mask).astype(
@@ -222,7 +406,7 @@
     grad_down_a, grad_down_b, d_inner_down = adapter_back(
         cotangent, hidden, inner_down, down_b, mask
     )
-    grad_hidden = by_cols(cotangent, lax.all_gather(w_down, "ctx", axis=0, tiled=True)) + by_cols(
+    grad_hidden = by_cols(cotangent, full_down) + by_cols(
         d_inner_down, down_a
     )
 
@@ -286,9 +470,8 @@
     )
     unused, pull_one = jax.vjp(lambda values: rms_scale(values, gain_attn), resid)
     grad_tokens = (grad_middle + pull_one(grad_act_one)[0]).astype(jnp.bfloat16)
-    sums = lax.psum(
-        (
-            grad_query_a,
+    partial = (
+                        grad_query_a,
             grad_query_b,
             grad_keyval_a,
             grad_keyval_b,
@@ -298,9 +481,11 @@
             grad_gateup_b,
             grad_down_a,
             grad_down_b,
-        ),
-        "ctx",
-    )
+    )
+    if own:
+        sums = unpack(reduce_packed(pack(partial)), [g.shape for g in partial])
+    else:
+        sums = lax.psum(partial, "ctx")
     return (
         result.astype(jnp.bfloat16),
         grad_tokens,

time: 933 us -> 722 us (0.77)
  waiting for transfers between devices: 515 us -> 12.4 us
  Pallas kernels: 0 us -> 321 us
  blocking collectives: 46.3 us -> 0 us
  between operations: 15.5 us -> 3.06 us
  local copies, waits for them, and re-layouts: 40.2 us -> 52.2 us
  starting transfers between devices: 35.2 us -> 45.2 us
    pallas_call x0 -> x2, Pallas kernels: none -> 321 us  [the longest x1 234 us: gather_weights(): pl.pallas_call(functools.partial(gather_kernel, parts, events), out_shape...]
    all_gather x4 -> x0, waiting for transfers between devices: 265 us -> none  [the longest x1 157 us: local(): lax.all_gather(w_gateup, 'ctx', axis=0, tiled=True)]
    psum x1 -> x0, waiting for transfers between devices: 227 us -> none  [local(): lax.psum((grad_query_a, grad_query_b, grad_keyval_a, grad_keyval_b, grad_...]
    all_gather x1 -> x0, blocking collectives: 46.3 us -> none  [local(): lax.all_gather(w_keyval, 'ctx', axis=0, tiled=True)]
    ppermute x16, starting transfers between devices: 35 us -> 45.2 us  [shifted(): return lax.ppermute(x, axis, pairs)]
    unnamed x200 -> x239, local copies, waits for them, and re-layouts: 33.7 us -> 35.2 us
  transfers between devices with their start and end apart: 21 -> 16, of which waited for: 9 -> 4; matrix products, arithmetic and copies ran while one was open for 12% -> 6% of each run, Pallas kernels for 0% -> 0%
where the time goes in v1:
time: 722 us; the launch traced here: 710 us
  Pallas kernels  321 us (44%)
  matrix products  230 us (32%)
  local copies, waits for them, and re-layouts  52.2 us (7%)
  other arithmetic  45.9 us (6%)
  starting transfers between devices  45.2 us (6%)
  waiting for transfers between devices  12.4 us (2%)
    pallas_call x1, Pallas kernels, gather_weights(): pl.pallas_call(functools.partial(gather_kernel, parts, events), out_shape...  234 us
    pallas_call x1, Pallas kernels, reduce_packed(): pl.pallas_call(functools.partial(reduce_kernel, rows), out_shape=jax.Shap...  87.3 us
    dot_general x15, matrix products, by_cols(): lax.dot_general(left, right, (((1,), (1,)), ((), ())), preferred_element_...  70.1 us
    ppermute x16, starting transfers between devices, shifted(): return lax.ppermute(x, axis, pairs)  45.2 us
    unnamed x239, local copies, waits for them, and re-layouts  35.2 us
    dot_general x4, matrix products, adapted(): jnp.dot(inputs, weight, preferred_element_type=jnp.float32)  33.2 us
    dot_general x2, matrix products, attend_backward(): jnp.einsum('rhd,kd->rhk', grad_heads, keys[:, HD:], preferred_element_typ...  26.4 us
    convert_element_type x2, other arithmetic, attend_backward(): grad_scores = (prob * (grad_prob - delta)).astype(jnp.bfloat16)  21.2 us
  transfers between devices with their start and end apart: 16, of which 4 were waited for; matrix products, arithmetic and copies ran while one was open for 6% of the time, Pallas kernels for 0%

profile of v1, /device:TPU:0, one launch (start us, length us, event | category | flops | bytes accessed | tf_op | source)
XLA Modules:
  0.0 709.6 jit_solution(1443271672960212020)
XLA Ops:
  2.5 1.8 fusion.18
  5.5 234.0 %shard_map.292 = (bf16[2,2,2,2,2,48,1536]{6,5,4,3,2,1,0:T(8,128)(2,1)}, bf16[2,2,2,2,2,48,256]{6,5,4,3,2,1,0:T(8,128)(2,1)}, bf16[2,2,2,2,2,48,1536]{6,5,4,3,2,1...) custom-call(bf16[48,1536]{1,0:T(8,128)(2,1)} %refs_0_.1, ...), custom_call_target="tpu_custom_call" | custom-call | tf_op jit(solution)/shard_map/pallas_call | solution.py:104
  239.6 2.4 fusion.132
  244.3 3.1 collective-permute-start
  247.4 4.2 collective-permute-start.1
  251.6 4.4 collective-permute-start.2
  256.0 2.0 collective-permute-start.3
  259.5 2.0 fusion.40
  261.6 5.2 fusion.135
  270.4 9.8 %fusion.143 = f32[4608,512]{0,1:T(8,128)} fusion(bf16[4608,1536]{1,0:T(8,128)(2,1)S(1)} %bitcast.384, bf16[512,1536]{1,0:T(8,128)(2,1)S(1)} %copy-done.27), kind=kOutput, calls=%fused_computation.302 | convolution fusion | flops 7247757312 | bytes 25165824 | tf_op jit(solution)/shard_map/dot_general | solution.py:231
  282.9 2.6 copy.102
  290.1 1.5 collective-permute-start.7
  295.5 1.7 collective-permute-done.5
  297.2 2.6 collective-permute-done.6
  299.8 4.6 collective-permute-done.7
  304.6 3.2 fusion
  307.8 4.3 exponential_reduce_fusion.1
  313.3 3.9 convolution_convert_fusion.10
  317.2 3.2 fusion.1
  320.5 4.7 exponential_reduce_fusion
  325.2 2.0 copy-done.4
  327.2 3.9 convolution_convert_fusion.9
  331.8 2.6 fusion.60
  335.4 1.7 copy-done.7
  337.4 23.0 %fusion.141 = f32[512,9216]{1,0:T(8,128)} fusion(bf16[512,1536]{1,0:T(8,128)(2,1)S(1)} %multiply_convert_fusion.4, bf16[1536,9216]{1,0:T(8,128)(2,1)} %bitcast.379), kind=kOutput, calls=%fused_computation.300 | convolution fusion | flops 14495514624 | bytes 48758784 | tf_op jit(solution)/shard_map/dot_general | solution.py:241
  361.0 12.4 %convolution_add_fusion = f32[512,9216]{1,0:T(8,128)} fusion(f32[512,9216]{1,0:T(8,128)} %fusion.141, bf16[512,128]{1,0:T(8,128)(2,1)S(1)} %fusion.43, bf16[128,9216]{1,0:T(8,128)(2,1)S(1)} %copy-done), kind=kOutput, calls=%fused_computation.10 | convolution fusion | flops 1212678144 | bytes 40239104 | tf_op jit(solution)/shard_map/dot_general | solution.py:242
  373.4 18.9 %fusion.8 = (bf16[512,4608]{1,0:T(8,128)(2,1)}, bf16[512,4608]{1,0:T(8,128)(2,1)}, bf16[512,4608]{1,0:T(8,128)(2,1)}) fusion(f32[512,9216]{1,0:T(8,128)} %convolution_add_fusion, bf16[512,128]{1,0:T(8,128)(2,1)S(1)} %copy-done.67, bf16[4608,128]{1,0:T(8,128)(2,1)S(1)} %copy-done.80, f32[4608,512]{0,1:T(8,128)} %fusion.143), kind=kOutput, calls=%fused_computation.22 | convolution fusion | flops 667680768 | bytes 43778048 | tf_op jit(solution)/shard_map/dot_general | solution.py:231
  392.3 6.8 fusion.33
  399.1 2.6 fusion.49
  401.7 22.0 %fusion.26 = f32[512,1536]{1,0:T(8,128)} fusion(bf16[1536,9216]{1,0:T(8,128)(2,1)} %bitcast.380, bf16[512,4608]{1,0:T(8,128)(2,1)} %get-tuple-element.25, bf16[512,4608]{1,0:T(8,128)(2,1)} %get-tuple-element.24), kind=kOutput, calls=%fused_computation.66 | convolution fusion | flops 14514388992 | bytes 40894464 | tf_op jit(solution)/shard_map/dot_general | solution.py:231
  423.8 3.7 multiply_reduce_fusion.2
  429.6 2.6 fusion.119
  435.4 13.2 %multiply_reduce_fusion = (f32[256,12]{0,1:T(8,128)S(1)}, f32[256,12,1280]{2,0,1:T(8,128)}) fusion(f32[256,12,1280]{2,0,1:T(8,128)} %copy-done.4, f32[256,12]{0,1:T(8,128)S(1)} %log_add_fusion, pred[256,1280]{1,0:T(8,128)(4,1)S(1)} %copy-done.25, bf16[256,12,128]{0,2,1:T(8,128)(2,1)S(1)} %bitcast.350, bf16[1280,256]{1,0:T(8,128)(2,1)S(1)} %copy-done.37), kind=kOutput, calls=%fused_computation.1 | convolution fusion | flops 1026290688 | bytes 32927744 | tf_op jit(solution)/shard_map/rhd,kd->rhk/dot_general | solution.py:289
  448.6 9.4 %convolution_bitcast_fusion = f32[1280,128]{0,1:T(8,128)S(1)} fusion(bf16[256,12,128]{0,2,1:T(8,128)(2,1)S(1)} %bitcast.351, f32[256,12,1280]{2,0,1:T(8,128)} %copy-done.4, f32[256,12]{0,1:T(8,128)S(1)} %log_add_fusion, pred[256,1280]{1,0:T(8,128)(4,1)S(1)} %copy-done.26), kind=kOutput, calls=%fused_computation.67 | convolution fusion | flops 1022361600 | bytes 17510400 | tf_op jit(solution)/shard_map/rhk,rhd->kd/dot_general | solution.py:308
  458.1 10.7 %multiply_convert_fusion = bf16[256,12,1280]{2,0,1:T(8,128)(2,1)} fusion(f32[256,12,1280]{2,0,1:T(8,128)} %get-tuple-element.67, f32[256,12,1280]{2,0,1:T(8,128)S(1)} %bitcast.333, f32[256,12]{0,1:T(8,128)S(1)} %get-tuple-element.66, f32[256,12]{0,1:T(8,128)S(1)} %log_add_fusion, pred[256,1280]{1,0:T(8,128)(4,1)S(1)} %copy-done.26), kind=kLoop, calls=%fused_computation | loop fusion | flops 23592960 | bytes 39673856 | tf_op jit(solution)/shard_map/convert_element_type | solution.py:293
  468.8 7.0 multiply_convert_fusion.5
  478.5 13.2 %multiply_reduce_fusion.1 = (f32[256,12]{0,1:T(8,128)S(1)}, f32[256,12,1280]{2,0,1:T(8,128)}) fusion(f32[256,12,1280]{2,0,1:T(8,128)} %copy-done.3, f32[256,12]{0,1:T(8,128)S(1)} %copy-done.64, pred[256,1280]{1,0:T(8,128)(4,1)S(1)} %copy-done.24, bf16[256,12,128]{0,2,1:T(8,128)(2,1)S(1)} %bitcast.352, bf16[1280,256]{1,0:T(8,128)(2,1)} %copy-done.34), kind=kOutput, calls=%fused_computation.3 | convolution fusion | flops 1026290688 | bytes 32923648 | tf_op jit(solution)/shard_map/rhd,kd->rhk/dot_general | solution.py:289
  491.7 9.5 %convolution_bitcast_fusion.2 = f32[1280,128]{0,1:T(8,128)S(1)} fusion(bf16[256,12,128]{0,2,1:T(8,128)(2,1)S(1)} %bitcast.353, f32[256,12,1280]{2,0,1:T(8,128)} %copy-done.3, f32[256,12]{0,1:T(8,128)S(1)} %copy-done.64, pred[256,1280]{1,0:T(8,128)(4,1)S(1)} %copy-done.24), kind=kOutput, calls=%fused_computation.70 | convolution fusion | flops 1022361600 | bytes 17510400 | tf_op jit(solution)/shard_map/rhk,rhd->kd/dot_general | solution.py:308
  501.3 10.5 %multiply_convert_fusion.1 = bf16[256,12,1280]{2,0,1:T(8,128)(2,1)} fusion(f32[256,12,1280]{2,0,1:T(8,128)} %get-tuple-element.69, f32[256,12,1280]{2,0,1:T(8,128)S(1)} %bitcast.331, f32[256,12]{0,1:T(8,128)S(1)} %get-tuple-element.68, f32[256,12]{0,1:T(8,128)S(1)} %copy-done.64, pred[256,1280]{1,0:T(8,128)(4,1)S(1)} %copy-done.24), kind=kLoop, calls=%fused_computation.2 | loop fusion | flops 23592960 | bytes 39673856 | tf_op jit(solution)/shard_map/convert_element_type | solution.py:293
  511.8 6.1 multiply_convert_fusion.6
  520.9 4.3 fusion.59
  526.7 10.3 %fusion.142 = f32[512,1536]{1,0:T(8,128)S(1)} fusion(bf16[512,4608]{1,0:T(8,128)(2,1)S(1)} %bitcast.343, bf16[4608,1536]{1,0:T(8,128)(2,1)} %bitcast.381), kind=kOutput, calls=%fused_computation.301 | convolution fusion | flops 7247757312 | bytes 22020096 | tf_op jit(solution)/shard_map/dot_general | solution.py:397
  538.4 1.6 fusion.32
  542.7 1.6 copy-done.13
  544.4 6.9 collective-permute-start.10
  552.6 4.0 collective-permute-start.12
  557.9 8.0 %collective-permute-start.14 = (bf16[512,256]{0,1:T(8,128)(2,1)}, bf16[512,256]{0,1:T(8,128)(2,1)}, u32[]{:S(2)}, u32[]{:S(2)}) collective-permute-start(bf16[512,256]{0,1:T(8,128)(2,1)} %get-tuple-element.36), channel_id=1, source_target_pairs={{0,4},{1,5},{2,6},{3,7},{4,8},{5,9},{6,10},{7,11},{8,12},{9,13},{1... | collective-permute-start | bytes 786440 | tf_op jit(solution)/shard_map/ppermute | solution.py:204
  565.9 1.7 fusion.22
  569.3 2.1 collective-permute-start.8
  572.7 1.4 convolution_convert_fusion.7
  574.2 1.8 copy.115
  578.9 1.8 constant_dynamic-update-slice_fusion.7
  580.6 3.5 collective-permute-done.14
  584.2 2.0 fusion.58
  587.6 1.6 fusion.31
  589.8 3.0 fusion.30
  594.9 1.5 constant_dynamic-update-slice_fusion.4
  596.5 2.4 fusion.11
  600.4 2.8 copy-done.2
  603.2 87.3 %shard_map.293 = bf16[2,2,2,2,2,784,128]{6,5,4,3,2,1,0:T(8,128)(2,1)S(1)} custom-call(bf16[2,2,2,2,2,784,128]{6,5,4,3,2,1,0:T(8,128)(2,1)S(1)} %bitcast.329), custom_call_target="tpu_custom_call" | custom-call | tf_op jit(solution)/shard_map/pallas_call | solution.py:183
  690.7 1.7 fusion.137
  692.4 1.6 slice_convert_fusion
  695.8 3.0 copy.146
  707.3 1.9 fusion.17
  (352 shorter events, 66.0 us)
Async XLA Ops:
  0.6 360.3 %copy-start = (bf16[128,9216]{1,0:T(8,128)(2,1)S(1)}, bf16[128,9216]{1,0:T(8,128)(2,1)}, u32[]{:S(2)}) copy-start(bf16[128,9216]{1,0:T(8,128)(2,1)} %param.39) | copy-start | bytes 7077892
  0.7 241.4 %copy-start.75 = (f32[1536]{0:T(1024)S(1)}, f32[1536]{0:T(1024)}, u32[]{:S(2)}) copy-start(f32[1536]{0:T(1024)} %param.30) | copy-start | bytes 18436
  0.7 241.4 %copy-start.52 = (bf16[1536,128]{1,0:T(8,128)(2,1)S(1)}, bf16[1536,128]{1,0:T(8,128)(2,1)}, u32[]{:S(2)}) copy-start(bf16[1536,128]{1,0:T(8,128)(2,1)} %param.34) | copy-start | bytes 1179652
  0.7 524.6 %copy-start.79 = (s32[128]{0:T(128)}, s32[128]{0:T(128)S(1)}, u32[]{:S(2)}) copy-start(s32[128]{0:T(128)S(1)} %and_select_fusion) | copy-start | bytes 1540
  4.8 256.7 %copy-start.77 = (f32[512]{0:T(512)}, f32[512]{0:T(512)S(1)}, u32[]{:S(2)}) copy-start(f32[512]{0:T(512)S(1)} %fusion.106) | copy-start | bytes 6148
  239.6 19.9 %copy-start.58 = (bf16[1536,128]{1,0:T(8,128)(2,1)S(1)}, bf16[1536,128]{1,0:T(8,128)(2,1)}, u32[]{:S(2)}) copy-start(bf16[1536,128]{1,0:T(8,128)(2,1)} %param.32) | copy-start | bytes 1179652
  244.3 41.2 %collective-permute-start = (bf16[512,256]{1,0:T(8,128)(2,1)}, bf16[512,256]{1,0:T(8,128)(2,1)}, u32[]{:S(2)}, u32[]{:S(2)}) collective-permute-start(bf16[512,256]{1,0:T(8,128)(2,1)} %fusion.38), channel_id=1, source_target_pairs={{0,4},{1,5},{2,6},{3,7},{4,8},{5,9},{6,10},{7,11},{8,12},{9,13},{1... | collective-permute-start | bytes 786440 | tf_op jit(solution)/shard_map/ppermute | solution.py:204
  247.4 40.4 %collective-permute-start.1 = (bf16[512,256]{1,0:T(8,128)(2,1)}, bf16[512,256]{1,0:T(8,128)(2,1)}, u32[]{:S(2)}, u32[]{:S(2)}) collective-permute-start(bf16[512,256]{1,0:T(8,128)(2,1)} %fusion.38), channel_id=1, source_target_pairs={{0,3},{1,4},{2,5},{3,6},{4,7},{5,8},{6,9},{7,10},{8,11},{9,12},{10... | collective-permute-start | bytes 786440 | tf_op jit(solution)/shard_map/ppermute | solution.py:204
  251.6 38.5 %collective-permute-start.2 = (bf16[512,256]{1,0:T(8,128)(2,1)}, bf16[512,256]{1,0:T(8,128)(2,1)}, u32[]{:S(2)}, u32[]{:S(2)}) collective-permute-start(bf16[512,256]{1,0:T(8,128)(2,1)} %fusion.38), channel_id=1, source_target_pairs={{0,2},{1,3},{2,4},{3,5},{4,6},{5,7},{6,8},{7,9},{8,10},{9,11},{10,... | collective-permute-start | bytes 786440 | tf_op jit(solution)/shard_map/ppermute | solution.py:204
  256.0 36.6 %collective-permute-start.3 = (bf16[512,256]{1,0:T(8,128)(2,1)}, bf16[512,256]{1,0:T(8,128)(2,1)}, u32[]{:S(2)}, u32[]{:S(2)}) collective-permute-start(bf16[512,256]{1,0:T(8,128)(2,1)} %fusion.38), channel_id=1, source_target_pairs={{0,1},{1,2},{2,3},{3,4},{4,5},{5,6},{6,7},{7,8},{8,9},{9,10},{10,1... | collective-permute-start | bytes 786440 | tf_op jit(solution)/shard_map/ppermute | solution.py:204
  258.0 36.5 %collective-permute-start.4 = (bf16[512,256]{1,0:T(8,128)(2,1)}, bf16[512,256]{1,0:T(8,128)(2,1)}, u32[]{:S(2)}, u32[]{:S(2)}) collective-permute-start(bf16[512,256]{1,0:T(8,128)(2,1)} %fusion.38), channel_id=1, source_target_pairs={{1,0},{2,1},{3,2},{4,3},{5,4},{6,5},{7,6},{8,7},{9,8},{10,9},{11,1... | collective-permute-start | bytes 786440 | tf_op jit(solution)/shard_map/ppermute | solution.py:204
  261.6 8.8 %slice-start.12 = ((s8[14155776]{0:T(1024)(128)(4,1)}), s8[4194304]{0:T(1024)(128)(4,1)S(1)}, s32[]{:S(2)}) async-start(s8[14155776]{0:T(1024)(128)(4,1)} %bitcast.382), calls=%async_computation.12 | async-start | bytes 8388608
  261.6 8.8 %slice-start.13 = ((s8[14155776]{0:T(1024)(128)(4,1)}), s8[4194304]{0:T(1024)(128)(4,1)S(1)}, s32[]{:S(2)}) async-start(s8[14155776]{0:T(1024)(128)(4,1)} %bitcast.382), calls=%async_computation.13 | async-start | bytes 8388608
  261.6 8.8 %slice-start.14 = ((s8[14155776]{0:T(1024)(128)(4,1)}), s8[4194304]{0:T(1024)(128)(4,1)S(1)}, s32[]{:S(2)}) async-start(s8[14155776]{0:T(1024)(128)(4,1)} %bitcast.382), calls=%async_computation.14 | async-start | bytes 8388608
  269.2 42.9 %copy-start.23 = (pred[256,1280]{1,0:T(8,128)(4,1)}, pred[256,1280]{1,0:T(8,128)(4,1)S(1)}, u32[]{:S(2)}) copy-start(pred[256,1280]{1,0:T(8,128)(4,1)S(1)} %fusion.35) | copy-start | bytes 983044
  270.4 9.9 %copy-start.50 = (bf16[128,1536]{1,0:T(8,128)(2,1)S(1)}, bf16[128,1536]{1,0:T(8,128)(2,1)}, u32[]{:S(2)}) copy-start(bf16[128,1536]{1,0:T(8,128)(2,1)} %param.41) | copy-start | bytes 1179652
  282.9 21.7 %copy-start.18 = (bf16[256,1536]{0,1:T(8,128)(2,1)}, bf16[256,1536]{0,1:T(8,128)(2,1)S(1)}, u32[]{:S(2)}) copy-start(bf16[256,1536]{0,1:T(8,128)(2,1)S(1)} %copy.99) | copy-start | bytes 2359300
  285.5 11.7 %collective-permute-start.5 = (bf16[512,256]{1,0:T(8,128)(2,1)}, bf16[512,256]{1,0:T(8,128)(2,1)S(1)}, u32[]{:S(2)}, u32[]{:S(2)}) collective-permute-start(bf16[512,256]{1,0:T(8,128)(2,1)} %fusion.38), channel_id=1, source_target_pairs={{2,0},{3,1},{4,2},{5,3},{6,4},{7,5},{8,6},{9,7},{10,8},{11,9},{12,... | collective-permute-start | bytes 786440 | tf_op jit(solution)/shard_map/ppermute | solution.py:204
  287.8 12.0 %collective-permute-start.6 = (bf16[512,256]{1,0:T(8,128)(2,1)}, bf16[512,256]{1,0:T(8,128)(2,1)S(1)}, u32[]{:S(2)}, u32[]{:S(2)}) collective-permute-start(bf16[512,256]{1,0:T(8,128)(2,1)} %fusion.38), channel_id=1, source_target_pairs={{3,0},{4,1},{5,2},{6,3},{7,4},{8,5},{9,6},{10,7},{11,8},{12,9},{13... | collective-permute-start | bytes 786440 | tf_op jit(solution)/shard_map/ppermute | solution.py:204
  290.1 14.3 %collective-permute-start.7 = (bf16[512,256]{1,0:T(8,128)(2,1)}, bf16[512,256]{1,0:T(8,128)(2,1)S(1)}, u32[]{:S(2)}, u32[]{:S(2)}) collective-permute-start(bf16[512,256]{1,0:T(8,128)(2,1)} %fusion.38), channel_id=1, source_target_pairs={{4,0},{5,1},{6,2},{7,3},{8,4},{9,5},{10,6},{11,7},{12,8},{13,9},{1... | collective-permute-start | bytes 786440 | tf_op jit(solution)/shard_map/ppermute | solution.py:204
  304.6 7.5 %copy-start.34 = (bf16[1280,256]{1,0:T(8,128)(2,1)}, bf16[1280,256]{1,0:T(8,128)(2,1)S(1)}, u32[]{:S(2)}) copy-start(bf16[1280,256]{1,0:T(8,128)(2,1)S(1)} %get-tuple-element.42) | copy-start | bytes 1966084
  304.6 20.6 %copy-start.36 = (bf16[1280,256]{1,0:T(8,128)(2,1)}, bf16[1280,256]{1,0:T(8,128)(2,1)S(1)}, u32[]{:S(2)}) copy-start(bf16[1280,256]{1,0:T(8,128)(2,1)S(1)} %get-tuple-element.43) | copy-start | bytes 1966084
  317.2 14.5 %copy-start.82 = (bf16[256,12,128]{0,2,1:T(8,128)(2,1)}, bf16[256,12,128]{0,2,1:T(8,128)(2,1)S(1)}, u32[]{:S(2)}) copy-start(bf16[256,12,128]{0,2,1:T(8,128)(2,1)S(1)} %convolution_convert_fusion.10) | copy-start | bytes 2359300
  320.5 6.7 copy-start.4
  320.5 11.3 %slice-start.18 = ((s8[4718592]{0:T(1024)(128)(4,1)}), s8[4194304]{0:T(1024)(128)(4,1)S(1)}, s32[]{:S(2)}) async-start(s8[4718592]{0:T(1024)(128)(4,1)} %bitcast.389), calls=%async_computation.18 | async-start | bytes 8388608
  337.4 23.0 %copy-start.30 = (bf16[512,1536]{1,0:T(8,128)(2,1)}, bf16[512,1536]{1,0:T(8,128)(2,1)S(1)}, u32[]{:S(2)}) copy-start(bf16[512,1536]{1,0:T(8,128)(2,1)S(1)} %multiply_convert_fusion.4) | copy-start | bytes 4718596
  337.4 23.0 %copy-start.48 = (bf16[1536,128]{1,0:T(8,128)(2,1)S(1)}, bf16[1536,128]{1,0:T(8,128)(2,1)}, u32[]{:S(2)}) copy-start(bf16[1536,128]{1,0:T(8,128)(2,1)} %param.38) | copy-start | bytes 1179652
  361.0 12.4 %copy-start.67 = (bf16[512,128]{1,0:T(8,128)(2,1)S(1)}, bf16[512,128]{1,0:T(8,128)(2,1)}, u32[]{:S(2)}) copy-start(bf16[512,128]{1,0:T(8,128)(2,1)} %fusion.44) | copy-start | bytes 393220
  361.0 12.4 %copy-start.80 = (bf16[4608,128]{1,0:T(8,128)(2,1)S(1)}, bf16[4608,128]{1,0:T(8,128)(2,1)}, u32[]{:S(2)}) copy-start(bf16[4608,128]{1,0:T(8,128)(2,1)} %param.40) | copy-start | bytes 3538948
  392.3 6.9 copy-start.84
  392.3 6.9 copy-start.85
  401.7 22.0 %copy-start.49 = (bf16[1536,128]{1,0:T(8,128)(2,1)S(1)}, bf16[1536,128]{1,0:T(8,128)(2,1)}, u32[]{:S(2)}) copy-start(bf16[1536,128]{1,0:T(8,128)(2,1)} %param.38) | copy-start | bytes 1179652
  435.4 13.3 %copy-start.26 = (pred[256,1280]{1,0:T(8,128)(4,1)S(1)}, pred[256,1280]{1,0:T(8,128)(4,1)}, u32[]{:S(2)}) copy-start(pred[256,1280]{1,0:T(8,128)(4,1)} %fusion.37) | copy-start | bytes 983044
  435.4 22.6 %slice-start.4 = ((s8[15728640]{0:T(1024)(128)(4,1)}), s8[4194304]{0:T(1024)(128)(4,1)S(1)}, s32[]{:S(2)}) async-start(s8[15728640]{0:T(1024)(128)(4,1)} %bitcast.332), calls=%async_computation.4 | async-start | bytes 8388608
  435.4 22.6 %slice-start.5 = ((s8[15728640]{0:T(1024)(128)(4,1)}), s8[4194304]{0:T(1024)(128)(4,1)S(1)}, s32[]{:S(2)}) async-start(s8[15728640]{0:T(1024)(128)(4,1)} %bitcast.332), calls=%async_computation.5 | async-start | bytes 8388608
  435.4 22.6 %slice-start.6 = ((s8[15728640]{0:T(1024)(128)(4,1)}), s8[3145728]{0:T(1024)(128)(4,1)S(1)}, s32[]{:S(2)}) async-start(s8[15728640]{0:T(1024)(128)(4,1)} %bitcast.332), calls=%async_computation.6 | async-start | bytes 6291456
  448.6 9.4 %slice-start.7 = ((s8[15728640]{0:T(1024)(128)(4,1)}), s8[4194304]{0:T(1024)(128)(4,1)S(1)}, s32[]{:S(2)}) async-start(s8[15728640]{0:T(1024)(128)(4,1)} %bitcast.332), calls=%async_computation.7 | async-start | bytes 8388608
  458.1 10.7 %copy-start.38 = (bf16[1280,256]{1,0:T(8,128)(2,1)S(1)}, bf16[1280,256]{1,0:T(8,128)(2,1)}, u32[]{:S(2)}) copy-start(bf16[1280,256]{1,0:T(8,128)(2,1)} %copy-done.36) | copy-start | bytes 1966084
  468.8 7.0 copy-start.5
  468.8 7.0 copy-start.21
  478.5 22.8 %slice-start = ((s8[15728640]{0:T(1024)(128)(4,1)}), s8[4194304]{0:T(1024)(128)(4,1)S(1)}, s32[]{:S(2)}) async-start(s8[15728640]{0:T(1024)(128)(4,1)} %bitcast.330), calls=%async_computation | async-start | bytes 8388608
  478.5 22.8 %slice-start.1 = ((s8[15728640]{0:T(1024)(128)(4,1)}), s8[4194304]{0:T(1024)(128)(4,1)S(1)}, s32[]{:S(2)}) async-start(s8[15728640]{0:T(1024)(128)(4,1)} %bitcast.330), calls=%async_computation.1 | async-start | bytes 8388608
  478.5 22.8 %slice-start.2 = ((s8[15728640]{0:T(1024)(128)(4,1)}), s8[3145728]{0:T(1024)(128)(4,1)S(1)}, s32[]{:S(2)}) async-start(s8[15728640]{0:T(1024)(128)(4,1)} %bitcast.330), calls=%async_computation.2 | async-start | bytes 6291456
  491.7 9.5 %slice-start.3 = ((s8[15728640]{0:T(1024)(128)(4,1)}), s8[4194304]{0:T(1024)(128)(4,1)S(1)}, s32[]{:S(2)}) async-start(s8[15728640]{0:T(1024)(128)(4,1)} %bitcast.330), calls=%async_computation.3 | async-start | bytes 8388608
  501.3 10.5 %copy-start.35 = (bf16[1280,256]{1,0:T(8,128)(2,1)S(1)}, bf16[1280,256]{1,0:T(8,128)(2,1)}, u32[]{:S(2)}) copy-start(bf16[1280,256]{1,0:T(8,128)(2,1)} %copy-done.34) | copy-start | bytes 1966084
  511.8 9.1 %slice-start.16 = ((s8[4718592]{0:T(1024)(128)(4,1)}), s8[4194304]{0:T(1024)(128)(4,1)S(1)}, s32[]{:S(2)}) async-start(s8[4718592]{0:T(1024)(128)(4,1)} %bitcast.386), calls=%async_computation.16 | async-start | bytes 8388608
  520.9 16.9 %copy-start.69 = (bf16[512,128]{1,0:T(8,128)(2,1)}, bf16[512,128]{1,0:T(8,128)(2,1)S(1)}, u32[]{:S(2)}) copy-start(bf16[512,128]{1,0:T(8,128)(2,1)S(1)} %fusion.46) | copy-start | bytes 393220
  526.7 10.3 %copy-start.33 = (bf16[16,8,72,128]{3,1,2,0:T(8,128)(2,1)S(1)}, bf16[16,8,72,128]{3,1,2,0:T(8,128)(2,1)}, u32[]{:S(2)}) copy-start(bf16[16,8,72,128]{3,1,2,0:T(8,128)(2,1)} %fusion.33) | copy-start | bytes 7077892
  541.3 24.5 %copy-start.9 = (f32[512,1536]{1,0:T(8,128)S(1)}, f32[512,1536]{1,0:T(8,128)}, u32[]{:S(2)}) copy-start(f32[512,1536]{1,0:T(8,128)} %copy-done.7) | copy-start | bytes 9437188
  541.4 24.5 %copy-start.51 = (bf16[128,1536]{1,0:T(8,128)(2,1)S(1)}, bf16[128,1536]{1,0:T(8,128)(2,1)}, u32[]{:S(2)}) copy-start(bf16[128,1536]{1,0:T(8,128)(2,1)} %param.41) | copy-start | bytes 1179652
  544.4 23.6 %collective-permute-start.10 = (bf16[512,256]{0,1:T(8,128)(2,1)S(1)}, bf16[512,256]{0,1:T(8,128)(2,1)S(1)}, u32[]{:S(2)}, u32[]{:S(2)}) collective-permute-start(bf16[512,256]{0,1:T(8,128)(2,1)S(1)} %get-tuple-element.40), channel_id=1, source_target_pairs={{0,2},{1,3},{2,4},{3,5},{4,6},{5,7},{6,8},{7,9},{8,10},{9,11},{10,... | collective-permute-start | bytes 786440 | tf_op jit(solution)/shard_map/ppermute | solution.py:204
  551.3 18.0 %collective-permute-start.11 = (bf16[512,256]{0,1:T(8,128)(2,1)S(1)}, bf16[512,256]{0,1:T(8,128)(2,1)S(1)}, u32[]{:S(2)}, u32[]{:S(2)}) collective-permute-start(bf16[512,256]{0,1:T(8,128)(2,1)S(1)} %get-tuple-element.39), channel_id=1, source_target_pairs={{2,0},{3,1},{4,2},{5,3},{6,4},{7,5},{8,6},{9,7},{10,8},{11,9},{12,... | collective-permute-start | bytes 786440 | tf_op jit(solution)/shard_map/ppermute | solution.py:204
  552.6 18.9 %collective-permute-start.12 = (bf16[512,256]{0,1:T(8,128)(2,1)S(1)}, bf16[512,256]{0,1:T(8,128)(2,1)S(1)}, u32[]{:S(2)}, u32[]{:S(2)}) collective-permute-start(bf16[512,256]{0,1:T(8,128)(2,1)S(1)} %get-tuple-element.38), channel_id=1, source_target_pairs={{0,3},{1,4},{2,5},{3,6},{4,7},{5,8},{6,9},{7,10},{8,11},{9,12},{10... | collective-permute-start | bytes 786440 | tf_op jit(solution)/shard_map/ppermute | solution.py:204
  556.5 24.1 %collective-permute-start.13 = (bf16[512,256]{0,1:T(8,128)(2,1)}, bf16[512,256]{0,1:T(8,128)(2,1)}, u32[]{:S(2)}, u32[]{:S(2)}) collective-permute-start(bf16[512,256]{0,1:T(8,128)(2,1)} %get-tuple-element.37), channel_id=1, source_target_pairs={{3,0},{4,1},{5,2},{6,3},{7,4},{8,5},{9,6},{10,7},{11,8},{12,9},{13... | collective-permute-start | bytes 786440 | tf_op jit(solution)/shard_map/ppermute | solution.py:204
  557.8 9.8 %copy-start.29 = (bf16[512,1536]{1,0:T(8,128)(2,1)S(1)}, bf16[512,1536]{1,0:T(8,128)(2,1)}, u32[]{:S(2)}) copy-start(bf16[512,1536]{1,0:T(8,128)(2,1)} %param.22) | copy-start | bytes 4718596
  557.9 14.9 %copy-start.66 = (bf16[512,128]{1,0:T(8,128)(2,1)S(1)}, bf16[512,128]{1,0:T(8,128)(2,1)}, u32[]{:S(2)}) copy-start(bf16[512,128]{1,0:T(8,128)(2,1)} %copy-done.65) | copy-start | bytes 393220
  557.9 26.3 %collective-permute-start.14 = (bf16[512,256]{0,1:T(8,128)(2,1)}, bf16[512,256]{0,1:T(8,128)(2,1)}, u32[]{:S(2)}, u32[]{:S(2)}) collective-permute-start(bf16[512,256]{0,1:T(8,128)(2,1)} %get-tuple-element.36), channel_id=1, source_target_pairs={{0,4},{1,5},{2,6},{3,7},{4,8},{5,9},{6,10},{7,11},{8,12},{9,13},{1... | collective-permute-start | bytes 786440 | tf_op jit(solution)/shard_map/ppermute | solution.py:204
  568.0 6.1 copy-start.60
  568.0 16.1 %collective-permute-start.15 = (bf16[512,256]{0,1:T(8,128)(2,1)}, bf16[512,256]{0,1:T(8,128)(2,1)}, u32[]{:S(2)}, u32[]{:S(2)}) collective-permute-start(bf16[512,256]{0,1:T(8,128)(2,1)} %get-tuple-element.35), channel_id=1, source_target_pairs={{4,0},{5,1},{6,2},{7,3},{8,4},{9,5},{10,6},{11,7},{12,8},{13,9},{1... | collective-permute-start | bytes 786440 | tf_op jit(solution)/shard_map/ppermute | solution.py:204
  569.3 14.8 %collective-permute-start.8 = (bf16[512,256]{0,1:T(8,128)(2,1)}, bf16[512,256]{0,1:T(8,128)(2,1)}, u32[]{:S(2)}, u32[]{:S(2)}) collective-permute-start(bf16[512,256]{0,1:T(8,128)(2,1)} %get-tuple-element.34), channel_id=1, source_target_pairs={{0,1},{1,2},{2,3},{3,4},{4,5},{5,6},{6,7},{7,8},{8,9},{9,10},{10,1... | collective-permute-start | bytes 786440 | tf_op jit(solution)/shard_map/ppermute | solution.py:204
  571.4 12.7 %collective-permute-start.9 = (bf16[512,256]{0,1:T(8,128)(2,1)}, bf16[512,256]{0,1:T(8,128)(2,1)}, u32[]{:S(2)}, u32[]{:S(2)}) collective-permute-start(bf16[512,256]{0,1:T(8,128)(2,1)} %get-tuple-element.41), channel_id=1, source_target_pairs={{1,0},{2,1},{3,2},{4,3},{5,4},{6,5},{7,6},{8,7},{9,8},{10,9},{11,1... | collective-permute-start | bytes 786440 | tf_op jit(solution)/shard_map/ppermute | solution.py:204
  578.1 9.2 %copy-start.45 = (bf16[512,128]{1,0:T(8,128)(2,1)S(1)}, bf16[512,128]{1,0:T(8,128)(2,1)}, u32[]{:S(2)}) copy-start(bf16[512,128]{1,0:T(8,128)(2,1)} %copy-done.44) | copy-start | bytes 393220
  580.6 9.1 %copy-start.47 = (bf16[512,128]{1,0:T(8,128)(2,1)S(1)}, bf16[512,128]{1,0:T(8,128)(2,1)}, u32[]{:S(2)}) copy-start(bf16[512,128]{1,0:T(8,128)(2,1)} %copy-done.46) | copy-start | bytes 393220
  587.5 8.9 %slice-start.10 = ((s8[4718592]{0:T(1024)(128)(4,1)}), s8[4194304]{0:T(1024)(128)(4,1)S(1)}, s32[]{:S(2)}) async-start(s8[4718592]{0:T(1024)(128)(4,1)} %bitcast.344), calls=%async_computation.10 | async-start | bytes 8388608
  (60 other events, 186.7 us)

commit v2 on v0

--- a/solution.py
+++ b/solution.py
@@ -1,6 +1,10 @@
+import functools
+
 import jax
 import jax.numpy as jnp
 from jax import lax
+from jax.experimental import pallas as pl
+from jax.experimental.pallas import tpu as pltpu
 from jax.sharding import PartitionSpec as P
 
 HEADS = 12
@@ -13,6 +17,23 @@
 
 NORM_EPS = 1e-06
 MASKED = -1e30
+
+
+MESH = pl.DeviceIdType.MESH
+bf16 = jnp.bfloat16
+f32 = jnp.float32
+NN = (((1,), (0,)), ((), ()))
+NT = (((1,), (1,)), ((), ()))
+TN = (((0,), (0,)), ((), ()))
+VMEM = pl.BlockSpec(memory_space=pltpu.VMEM)
+HBM = pl.BlockSpec(memory_space=pl.ANY)
+ORD_A = (4, 3, 1, 2, 0)
+ORD_A2 = (4, 3, 2, 1, 0)
+ORD_B = (4, 1, 2, 3, 0)
+ORD_B2 = (4, 2, 1, 3, 0)
+ORD_C = (4, 2, 3, 1, 0)
+ORD_C2 = (4, 1, 3, 2, 0)
+LAGS = (0, 1, 2, 4, 6)
 
 
 def shifted(x, axis, by):
@@ -128,7 +149,7 @@
     return (grad_query.reshape(rows, -1), jnp.concatenate([grad_key, grad_value], axis=1))
 
 
-def local(
+def local_native(
     tokens,
     cotangent,
     doc_lengths,
@@ -317,6 +338,517 @@
     )
 
 
+def flip(me, bits, b):
+    return (me+(1-2*bits[b])*(1<<b),)
+def reduce_kernel(rows, in_ref, out_ref, r0, r1, r2, r3, r4, ssem, rsem):
+    rb=(r0,r1,r2,r3,r4)
+    me=lax.axis_index("ctx")
+    bits=[(me//(1<<b))%2 for b in range(5)]
+    bar=pltpu.get_barrier_semaphore()
+    for b in range(5):
+        pl.semaphore_signal(bar,1,device_id=flip(me,bits,b),device_id_type=MESH)
+    pl.semaphore_wait(bar,5)
+    t=rows//16
+    a=round(t*3/7); bb=round(t*3/14)
+    classes=[(0,a*16,ORD_A),(a*16,bb*16,ORD_B),((a+bb)*16,rows-(a+bb)*16,ORD_C)]
+    def rs(cl,s):
+        r0_,n,order=classes[cl]
+        red=order[::-1]
+        bit=red[s]; done=red[:s]
+        rem=[b for b in (4,3,2,1,0) if b not in done]
+        src=in_ref if s==0 else rb[s-1]
+        idx=tuple((1-bits[b]) if b==bit else slice(None) for b in rem)
+        return pltpu.make_async_remote_copy(src.at[idx+(pl.ds(r0_,n),)],rb[s].at[(slice(None),)*(4-s)+(pl.ds(r0_,n),)],ssem.at[cl,s],rsem.at[cl,s],device_id=flip(me,bits,bit),device_id_type=MESH)
+    def add(cl,s):
+        r0_,n,order=classes[cl]
+        red=order[::-1]
+        bit=red[s]; done=red[:s]
+        rem=[b for b in (4,3,2,1,0) if b not in done]
+        src=in_ref if s==0 else rb[s-1]
+        rs_=pl.ds(r0_,n)
+        nd=4-s
+        def body(j,_):
+            ds=[(j//(1<<(nd-1-i)))%2 for i in range(nd)]
+            it=iter(ds)
+            si=tuple(bits[b] if b==bit else next(it) for b in rem)
+            v=src[si+(rs_,)].astype(f32)+rb[s][tuple(ds)+(rs_,)].astype(f32)
+            rb[s][tuple(ds)+(rs_,)]=v.astype(bf16)
+            return 0
+        lax.fori_loop(0,1<<nd,body,0)
+    def ag(cl,k):
+        r0_,n,order=classes[cl]
+        bit=order[k]; have=order[:k]
+        idx=tuple(slice(None) if b in have else bits[b] for b in (4,3,2,1,0))+(pl.ds(r0_,n),)
+        src=out_ref.at[idx] if k else rb[4].at[pl.ds(r0_,n)]
+        return pltpu.make_async_remote_copy(src,out_ref.at[idx],ssem.at[cl,5+k],rsem.at[cl,5+k],device_id=flip(me,bits,bit),device_id_type=MESH)
+    for cl in range(3): rs(cl,0).start()
+    for s in range(5):
+        for cl in range(3):
+            rs(cl,s).wait_recv()
+            add(cl,s)
+            if s<4: rs(cl,s+1).start()
+            else:
+                ag(cl,0).start()
+                r0_,n,_=classes[cl]
+                out_ref[bits[4],bits[3],bits[2],bits[1],bits[0],pl.ds(r0_,n)]=rb[4][pl.ds(r0_,n)]
+    for k in range(1,5):
+        for cl in range(3):
+            ag(cl,k-1).wait_recv()
+            ag(cl,k).start()
+    for cl in range(3): ag(cl,4).wait_recv()
+    for cl in range(3):
+        for s in range(5):
+            rs(cl,s).wait_send(); ag(cl,s).wait_send()
+def reduce_packed(x, cid=1):
+    rows=x.shape[5]
+    return pl.pallas_call(functools.partial(reduce_kernel,rows),
+        out_shape=jax.ShapeDtypeStruct(x.shape,x.dtype),
+        in_specs=[pl.BlockSpec(memory_space=pltpu.VMEM)],out_specs=pl.BlockSpec(memory_space=pltpu.VMEM),
+        scratch_shapes=[pltpu.VMEM((2,)*(4-s)+(rows,128),bf16) for s in range(5)]+[pltpu.SemaphoreType.DMA((3,10)),pltpu.SemaphoreType.DMA((3,10))],
+        compiler_params=pltpu.CompilerParams(collective_id=cid,has_side_effects=True,vmem_limit_bytes=40<<20))(x)
+
+def gather_units():
+    units = [
+        [(0, 0, 6, ORD_A), (0, 6, 5, ORD_C), (0, 11, 1, ORD_B), (1, 0, 2, ORD_B)],
+        [(2, 0, 5, ORD_A), (2, 5, 4, ORD_C), (2, 9, 3, ORD_B)],
+    ]
+    sets = ((ORD_A, ORD_C, ORD_B), (ORD_A2, ORD_C2, ORD_B2))
+    for i in range(3):
+        first, second, third = sets[i % 2]
+        units.append([(3, 4 * i, 2, first), (3, 4 * i + 2, 1, second), (3, 4 * i + 3, 1, third)])
+    return units
+
+
+def gather_kernel(parts, events, *refs):
+    count = (len(refs) - 3) // 3
+    src, dst, held = refs[:count], refs[count : 2 * count], refs[2 * count : 3 * count]
+    send_sem, recv_sem, own_sem = refs[3 * count :]
+    me = lax.axis_index("ctx")
+    bits = [(me // (1 << b)) % 2 for b in range(5)]
+    barrier = pltpu.get_barrier_semaphore()
+    for b in range(5):
+        pl.semaphore_signal(barrier, 1, device_id=flip(me, bits, b), device_id_type=MESH)
+    pl.semaphore_wait(barrier, 5)
+    own = []
+    for w in range(count):
+        copy = pltpu.make_async_copy(src[w], held[w], own_sem.at[w])
+        copy.start()
+        own.append(copy)
+    for w in range(count):
+        own[w].wait()
+        own[w] = copy = pltpu.make_async_copy(
+            held[w], dst[w].at[bits[4], bits[3], bits[2], bits[1], bits[0]], own_sem.at[w]
+        )
+        copy.start()
+
+    def exchange(p, k):
+        w, tile, tiles, order = parts[p]
+        bit, have = order[k], order[:k]
+        where = tuple(pl.ds(0, 2) if b in have else bits[b] for b in (4, 3, 2, 1, 0))
+        cols = pl.ds(tile * 128, tiles * 128)
+        there = dst[w].at[where + (slice(None), cols)]
+        return pltpu.make_async_remote_copy(
+            there if k else src[w].at[:, cols],
+            there,
+            send_sem.at[p, k],
+            recv_sem.at[p, k],
+            device_id=flip(me, bits, bit),
+            device_id_type=MESH,
+        )
+
+    waited = set()
+    for p, k in events:
+        if k:
+            if parts[p][0] not in waited:
+                waited.add(parts[p][0])
+                own[parts[p][0]].wait()
+            exchange(p, k - 1).wait_recv()
+        exchange(p, k).start()
+    for p in range(len(parts)):
+        exchange(p, 4).wait_recv()
+    for p in range(len(parts)):
+        for k in range(5):
+            exchange(p, k).wait_send()
+
+
+def gather_weights(weights):
+    units = gather_units()
+    parts = [part for unit in units for part in unit]
+    unit_of = [i for i, unit in enumerate(units) for part in unit]
+    events = sorted(
+        ((unit_of[p] + LAGS[k], -k, p, k) for p in range(len(parts)) for k in range(5))
+    )
+    events = [(p, k) for _, _, p, k in events]
+    out = pl.pallas_call(
+        functools.partial(gather_kernel, parts, events),
+        out_shape=[jax.ShapeDtypeStruct((2,) * 5 + w.shape, w.dtype) for w in weights],
+        in_specs=[pl.BlockSpec(memory_space=pl.ANY)] * len(weights),
+        out_specs=[pl.BlockSpec(memory_space=pl.ANY)] * len(weights),
+        scratch_shapes=[pltpu.VMEM(w.shape, w.dtype) for w in weights]
+        + [
+            pltpu.SemaphoreType.DMA((len(parts), 5)),
+            pltpu.SemaphoreType.DMA((len(parts), 5)),
+            pltpu.SemaphoreType.DMA((len(weights),)),
+        ],
+        compiler_params=pltpu.CompilerParams(collective_id=0, has_side_effects=True),
+    )(*weights)
+    return [x.reshape(-1, x.shape[-1]) for x in out]
+
+
+SUB = 128
+GROUP = 6
+SCALE = HD ** (-0.5)
+
+
+def heads_down(x):
+    return jnp.concatenate([x[:,i*HD:(i+1)*HD] for i in range(x.shape[1]//HD)],axis=0)
+def heads_across(x):
+    n=x.shape[0]//SUB
+    return jnp.concatenate([x[i*SUB:(i+1)*SUB] for i in range(n)],axis=1)
+def att_fwd_kernel(span, window, q_ref, kv_ref, qseg_ref, kseg_ref, o_ref, p_ref):
+    s=pl.program_id(1)
+    start=pl.multiple_of(s*SUB,SUB)
+    k=kv_ref[0,pl.ds(start,span),:HD]; v=kv_ref[0,pl.ds(start,span),HD:]
+    row=lax.broadcasted_iota(jnp.int32,(SUB,span),0); col=lax.broadcasted_iota(jnp.int32,(SUB,span),1)
+    ok=(col<=row+(span-SUB))&(col>row+(span-SUB-window))&(kseg_ref[0,:,pl.ds(start,span)]==qseg_ref[...])
+    bias=jnp.where(ok,0.0,MASKED)
+    bias=jnp.concatenate([bias]*GROUP,axis=0)
+    def body(g,_):
+        at=pl.multiple_of(g*GROUP*HD,GROUP*HD)
+        q=heads_down(q_ref[:,pl.ds(at,GROUP*HD)])
+        sc=lax.dot_general(q,k,NT,preferred_element_type=f32)*SCALE+bias
+        e=jnp.exp(sc-jnp.max(sc,axis=1,keepdims=True))
+        p=(e*(1.0/jnp.sum(e,axis=1,keepdims=True))).astype(bf16)
+        p_ref[0,0,pl.ds(pl.multiple_of(g*GROUP*SUB,GROUP*SUB),GROUP*SUB),:]=p
+        o=lax.dot_general(p,v,(((1,),(0,)),((),())),preferred_element_type=f32)
+        o_ref[:,pl.ds(at,GROUP*HD)]=heads_across(o).astype(bf16)
+        return 0
+    lax.fori_loop(0,HEADS//GROUP,body,0)
+def att_fwd(q,kv,qseg,kseg,window):
+    rows=q.shape[0]; width=rows//2; subs=width//SUB; keys=kv.shape[1]; span=keys-width+SUB
+    return pl.pallas_call(functools.partial(att_fwd_kernel,span,window),grid=(2,subs),
+      in_specs=[pl.BlockSpec((SUB,q.shape[1]),lambda w,s:(w*subs+s,0)),pl.BlockSpec((1,keys,2*HD),lambda w,s:(w,0,0)),
+        pl.BlockSpec((SUB,1),lambda w,s:(w*subs+s,0)),pl.BlockSpec((1,1,keys),lambda w,s:(w,0,0))],
+      out_specs=[pl.BlockSpec((SUB,q.shape[1]),lambda w,s:(w*subs+s,0)),pl.BlockSpec((1,1,HEADS*SUB,span),lambda w,s:(w,s,0,0))],
+      out_shape=[jax.ShapeDtypeStruct(q.shape,bf16),jax.ShapeDtypeStruct((2,subs,HEADS*SUB,span),bf16)],
+      compiler_params=pltpu.CompilerParams(vmem_limit_bytes=56<<20),name="att_fwd")(q,kv,qseg,kseg)
+def att_bwd_kernel(span, q_ref, kv_ref, att_ref, do_ref, p_ref, dq_ref, dkv_ref):
+    s=pl.program_id(1)
+    start=pl.multiple_of(s*SUB,SUB)
+    k=kv_ref[0,pl.ds(start,span),:HD]; v=kv_ref[0,pl.ds(start,span),HD:]
+    @pl.when(s==0)
+    def _(): dkv_ref[...]=jnp.zeros_like(dkv_ref)
+    def body(g,_):
+        at=pl.multiple_of(g*GROUP*HD,GROUP*HD)
+        q=heads_down(q_ref[:,pl.ds(at,GROUP*HD)])
+        do=heads_down(do_ref[:,pl.ds(at,GROUP*HD)])
+        o=heads_down(att_ref[:,pl.ds(at,GROUP*HD)])
+        delta=jnp.sum(do.astype(f32)*o.astype(f32),axis=1,keepdims=True)
+        dp=lax.dot_general(do,v,NT,preferred_element_type=f32)
+        p=p_ref[0,0,pl.ds(pl.multiple_of(g*GROUP*SUB,GROUP*SUB),GROUP*SUB),:]
+        ds=(p.astype(f32)*(dp-delta)).astype(bf16)
+        dq=lax.dot_general(ds,k,(((1,),(0,)),((),())),preferred_element_type=f32)*SCALE
+        dq_ref[:,pl.ds(at,GROUP*HD)]=heads_across(dq).astype(bf16)
+        dk=jnp.dot(q.T,ds,preferred_element_type=f32)*SCALE
+        dv=jnp.dot(do.T,p,preferred_element_type=f32)
+        dkv_ref[0,:HD,pl.ds(start,span)]+=dk
+        dkv_ref[0,HD:,pl.ds(start,span)]+=dv
+        return 0
+    lax.fori_loop(0,HEADS//GROUP,body,0)
+def att_bwd(q,kv,att,do,p):
+    rows=q.shape[0]; width=rows//2; subs=width//SUB; keys=kv.shape[1]; span=keys-width+SUB
+    rowspec=pl.BlockSpec((SUB,q.shape[1]),lambda w,s:(w*subs+s,0))
+    dsh=(2,2*HD,keys)
+    return pl.pallas_call(functools.partial(att_bwd_kernel,span),grid=(2,subs),
+      in_specs=[rowspec,pl.BlockSpec((1,keys,2*HD),lambda w,s:(w,0,0)),rowspec,rowspec,pl.BlockSpec((1,1,HEADS*SUB,span),lambda w,s:(w,s,0,0))],
+      out_specs=[rowspec,pl.BlockSpec((1,)+dsh[1:],lambda w,s:(w,0,0))],
+      out_shape=[jax.ShapeDtypeStruct(q.shape,bf16),jax.ShapeDtypeStruct(dsh,f32)],
+      compiler_params=pltpu.CompilerParams(vmem_limit_bytes=56<<20),name="att_bwd")(q,kv,att,do,p)
+
+
+def dot(a,b,dims=NN): return lax.dot_general(a,b,dims,preferred_element_type=f32)
+CH=512; UNIT=256
+def mlp_kernel(ff, a2_ref, g_ref, mid_ref, mask_ref, gain_ref, igu_ref, did_ref, ga_ref, gb_ref, da_ref, db_ref, wd_hbm, wgu_own,
+               out_ref, dmid_ref, gga_ref, ggb_ref, gda_ref, gdb_ref, land,
+               own_v, wbuf, dbuf, acc_o, acc_a, gu_s, dh_s, hid_s, dgu_s, wsem, dsem, ownsem, ssem, rsem):
+    me=lax.axis_index("ctx")
+    bits=[(me//(1<<b))%2 for b in range(5)]
+    nu=ff//UNIT; nc=ff//CH; half=ff//128
+    bar=pltpu.get_barrier_semaphore()
+    for b in range(5):
+        pl.semaphore_signal(bar,1,device_id=flip(me,bits,b),device_id_type=MESH)
+    pl.semaphore_wait(bar,5)
+    stage=pltpu.make_async_copy(wgu_own,own_v,ownsem)
+    stage.start(); stage.wait()
+    own=pltpu.make_async_copy(own_v,land.at[bits[4],bits[3],bits[2],bits[1],bits[0]],ownsem)
+    own.start()
+    SETS=(((ORD_A,0,256,0),(ORD_C,ff,128,0),(ORD_B,ff+128,128,0)),((ORD_A2,0,256,0),(ORD_C2,ff,128,0),(ORD_B2,ff+128,128,0)))
+    def ex(v,par,cl,k):
+        order,base,n,_=SETS[par][cl]
+        bit,have=order[k],order[:k]
+        where=tuple(pl.ds(0,2) if b in have else bits[b] for b in (4,3,2,1,0))
+        at=base+v*UNIT
+        cols=pl.ds(pl.multiple_of(at,128) if not isinstance(at,int) else at,n)
+        there=land.at[where+(slice(None),cols)]
+        return pltpu.make_async_remote_copy(there if k else wgu_own.at[:,cols],there,ssem.at[v,cl,k],rsem.at[v,cl,k],device_id=flip(me,bits,bit),device_id_type=MESH)
+    def step(t,par,guard):
+        for k in (4,3,2,1,0):
+            v=t+8-LAGS[k]; vp=(par+8-LAGS[k])%2
+            def go(v=v,vp=vp,k=k):
+                for cl in range(3):
+                    if k: ex(v,vp,cl,k-1).wait_recv()
+                    ex(v,vp,cl,k).start()
+            if guard: pl.when(v<nu)(go)
+            elif 0<=v<nu: go()
+    def fetch(c,slot):
+        n=CH
+        return [pltpu.make_async_copy(land.at[(slice(None),)*6+(pl.ds(pl.multiple_of(base+c*CH,128),n),)],wbuf.at[(slot,)+(slice(None),)*6+(pl.ds(o,n),)],wsem.at[slot,i]) for i,(base,o) in enumerate(((0,0),(ff,CH)))]+\
+               [pltpu.make_async_copy(wd_hbm.at[pl.ds(pl.multiple_of(c*CH,CH),CH)],dbuf.at[slot],dsem.at[slot])]
+    def arrived(c):
+        for j in range(CH//UNIT):
+            for cl in range(3): ex(c*(CH//UNIT)+j,j%2,cl,4).wait_recv()
+    acc_o[...]=jnp.zeros_like(acc_o); acc_a[...]=jnp.zeros_like(acc_a)
+    for t in range(-8,0):
+        if t==-7: own.wait()
+        step(t,t%2,False)
+    arrived(0)
+    for cp in fetch(0,0): cp.start()
+    for cp in fetch(0,0): cp.wait()
+    def body(c,_):
+        slot=c%2
+        step(2*c,0,True)
+        gbc=[gb_ref[:,pl.ds(pl.multiple_of(base+c*CH,128),CH)] for base in (0,ff)]
+        dac=da_ref[pl.ds(pl.multiple_of(c*CH,CH),CH),:]
+        def wx(): return jnp.concatenate([wbuf[slot].reshape(-1,2*CH),jnp.concatenate(gbc,1)],0)
+        def wdx(): return jnp.concatenate([dbuf[slot],dac],1)
+        def ax(): return jnp.concatenate([a2_ref[...],igu_ref[...]],1)
+        def gx(): return jnp.concatenate([g_ref[...],did_ref[...]],1)
+        gu_s[...]=dot(ax(),wx())
+        step(2*c+1,1,True)
+        dh_s[...]=dot(gx(),wdx(),NT)
+        k0=0.7978845608028654
+        def ew(r,_):
+            rows=pl.ds(pl.multiple_of(r*16,16),16)
+            gate=gu_s[rows,:CH]; up=gu_s[rows,CH:]; dh=dh_s[rows,:]
+            sq=gate*gate
+            th=jnp.tanh(gate*(k0+(k0*0.044715)*sq))
+            ht=0.5+0.5*th
+            gl=gate*ht
+            dgl=ht+(gate*(0.5-0.5*th*th))*(k0+(3*k0*0.044715)*sq)
+            hid_s[rows,:]=(gl*up).astype(bf16)
+            dgu_s[rows,:CH]=(dh*up*dgl).astype(bf16)
+            dgu_s[rows,CH:]=(dh*gl).astype(bf16)
+            return 0
+        lax.fori_loop(0,g_ref.shape[0]//16,ew,0)
+        acc_o[...]+=dot(hid_s[...],wdx())
+        gda_ref[pl.ds(pl.multiple_of(c*CH,CH),CH),:]=dot(hid_s[...],did_ref[...],TN).astype(bf16)
+        r=dot(igu_ref[...],dgu_s[...],TN).astype(bf16)
+        for i in range(2):
+            for j in range(CH//128):
+                ggb_ref[pl.ds(c*(CH//128)+(ff//128)*i+j,1)]=r[None,:,(i*(CH//128)+j)*128:(i*(CH//128)+j+1)*128]
+        @pl.when(c+1<nc)
+        def _():
+            arrived(c+1)
+            for cp in fetch(c+1,1-slot): cp.start()
+        acc_a[...]+=dot(dgu_s[...],wx(),NT)
+        @pl.when(c+1<nc)
+        def _():
+            for cp in fetch(c+1,1-slot): cp.wait()
+        return 0
+    lax.fori_loop(0,nc,body,0)
+    mask=mask_ref[...]
+    g=g_ref[...]
+    d=g_ref.shape[1]
+    inner_d=(acc_o[:,d:]*mask).astype(bf16)
+    mid=mid_ref[...]
+    out_ref[...]=(mid+(acc_o[:,:d]+dot(inner_d,db_ref[...]))).astype(bf16)
+    r=dot(inner_d,g,TN).astype(bf16)
+    for j in range(g.shape[1]//128): gdb_ref[j]=r[:,j*128:(j+1)*128]
+    dgu=(acc_a[:,d:]*mask).astype(bf16)
+    gga_ref[...]=dot(a2_ref[...],dgu,TN).astype(bf16)
+    da2=acc_a[:,:d]+dot(dgu,ga_ref[...],NT)
+    e=da2*gain_ref[...]
+    rr=lax.rsqrt(jnp.mean(mid*mid,axis=1,keepdims=True)+1e-6)
+    dmid_ref[...]=g.astype(f32)+rr*e-(rr*rr*rr)*mid*jnp.mean(e*mid,axis=1,keepdims=True)
+    def fin(v,_):
+        for par in range(2):
+            for cl in range(3):
+                for k in range(5): ex(2*v+par,par,cl,k).wait_send()
+        return 0
+    lax.fori_loop(0,nu//2,fin,0)
+def mlp(a2,g,mid,mask,gain,igu,did,ga,gb,da,db,wd,wgu):
+    rows,d=a2.shape; ff=da.shape[0]; nu=ff//UNIT
+    V=pl.BlockSpec(memory_space=pltpu.VMEM); H=pl.BlockSpec(memory_space=pl.ANY)
+    S=jax.ShapeDtypeStruct
+    return pl.pallas_call(functools.partial(mlp_kernel,ff),
+        in_specs=[V]*11+[H,H],
+        out_specs=[V]*6+[H],
+        out_shape=[S((rows,d),bf16),S((rows,d),f32),S((d,128),bf16),S((2*ff//128,128,128),bf16),S((ff,128),bf16),S((d//128,128,128),bf16),S((2,)*5+wgu.shape,bf16)],
+        scratch_shapes=[pltpu.VMEM(wgu.shape,bf16),pltpu.VMEM((2,)+(2,)*5+(wgu.shape[0],2*CH),bf16),pltpu.VMEM((2,CH,d),bf16),pltpu.VMEM((rows,d+128),f32),pltpu.VMEM((rows,d+128),f32),pltpu.VMEM((rows,2*CH),f32),pltpu.VMEM((rows,CH),f32),pltpu.VMEM((rows,CH),bf16),pltpu.VMEM((rows,2*CH),bf16),
+            pltpu.SemaphoreType.DMA((2,2)),pltpu.SemaphoreType.DMA((2,)),pltpu.SemaphoreType.DMA,pltpu.SemaphoreType.DMA((nu,3,5)),pltpu.SemaphoreType.DMA((nu,3,5))],
+        compiler_params=pltpu.CompilerParams(collective_id=2,has_side_effects=True,vmem_limit_bytes=60<<20),name="mlp")(a2,g,mid,mask,gain,igu,did,ga,gb,da,db,wd,wgu)
+
+
+def tiles_out(x):
+    return x.reshape(x.shape[0], -1, 128).transpose(1, 0, 2).reshape(-1, 128)
+
+
+def tiles_in(x, rows):
+    return x.reshape(-1, rows, 128).transpose(1, 0, 2).reshape(rows, -1)
+
+
+def pack(grads):
+    parts = [g.astype(bf16) for g in grads]
+    have = sum(g.shape[0] for g in parts)
+    total = -(-have // 512) * 512
+    if total > have:
+        parts.append(jnp.zeros((total - have, 128), bf16))
+    return jnp.concatenate(parts, axis=0).reshape((2,) * 5 + (total // 32, 128))
+
+
+def local_own(
+    tokens,
+    cotangent,
+    doc_lengths,
+    adapter_ids,
+    w_query,
+    w_keyval,
+    w_output,
+    w_gateup,
+    w_down,
+    gain_attn,
+    gain_mlp,
+    query_a,
+    query_b,
+    keyval_a,
+    keyval_b,
+    output_a,
+    output_b,
+    gateup_a,
+    gateup_b,
+    down_a,
+    down_b,
+):
+    count = lax.axis_size("ctx")
+    device = lax.axis_index("ctx")
+    local_rows = tokens.shape[0]
+    width = local_rows // 2
+    reach = (WINDOW + width - 1) // width
+    key_width = w_keyval.shape[1]
+    half_rows = jnp.arange(width, dtype=jnp.int32)
+    own_blocks = (device, 2 * count - 1 - device)
+    positions = jnp.concatenate(
+        [own_blocks[0] * width + half_rows, own_blocks[1] * width + half_rows]
+    )
+    segment, mask = adapter_mask(doc_lengths, adapter_ids, positions)
+    resid = tokens.astype(f32)
+    act_one = rms_scale(resid, gain_attn).astype(bf16)
+    full_query, full_keyval, full_output, full_down = gather_weights(
+        (w_query, w_keyval, w_output, w_down)
+    )
+    query_full, inner_query = adapted(act_one, full_query, query_a, query_b, mask)
+    keyval_full, inner_keyval = adapted(act_one, full_keyval, keyval_a, keyval_b, mask)
+    query = query_full.astype(bf16)
+    keyval = keyval_full.astype(bf16)
+    stacked = [keyval]
+    for offset in range(1, reach + 1):
+        later = shifted(keyval, "ctx", -offset)
+        prior = shifted(keyval, "ctx", offset)
+        stacked = [prior] + stacked + [later]
+    table = jnp.stack(stacked)
+    first_device = device - reach
+    key_blocks = [[block - reach + step for step in range(reach + 1)] for block in own_blocks]
+    keys = jnp.stack(
+        [
+            jnp.concatenate([key_block(table, first_device, e, count, width) for e in blocks], axis=0)
+            for blocks in key_blocks
+        ]
+    )
+    key_pos = jnp.stack(
+        [jnp.concatenate([e * width + half_rows for e in blocks]) for blocks in key_blocks]
+    )
+    key_seg = segment_of(doc_lengths, key_pos.reshape(-1)).reshape(2, 1, -1)
+    attention, prob = att_fwd(query, keys, segment[:, None], key_seg, WINDOW)
+    branch_one, inner_output = adapted(attention, full_output, output_a, output_b, mask)
+    middle = resid + branch_one
+    act_two = rms_scale(middle, gain_mlp).astype(bf16)
+    inner_gateup = (dot(act_two, gateup_a) * mask).astype(bf16)
+    d_inner_down = (dot(cotangent, down_b, NT) * mask).astype(bf16)
+    result, grad_middle, g_gateup_a, g_gateup_b, g_down_a, g_down_b, unused = mlp(
+        act_two,
+        cotangent,
+        middle,
+        mask,
+        gain_mlp[None, :],
+        inner_gateup,
+        d_inner_down,
+        gateup_a,
+        gateup_b,
+        down_a,
+        down_b,
+        full_down,
+        w_gateup,
+    )
+    grad_branch = grad_middle.astype(bf16)
+    g_output_a, g_output_b, d_inner_output = adapter_back(
+        grad_branch, attention, inner_output, output_b, mask
+    )
+    grad_attention = (by_cols(grad_branch, full_output) + by_cols(d_inner_output, output_a)).astype(
+        bf16
+    )
+    grad_query, grad_keys = att_bwd(query, keys, attention, grad_attention, prob)
+    grad_keys = grad_keys.transpose(0, 2, 1)
+    slots = jnp.zeros((2 * reach + 1, local_rows, key_width), f32)
+    for which in range(2):
+        for step, entry in enumerate(key_blocks[which]):
+            piece = grad_keys[which, step * width : (step + 1) * width]
+            device_of, row_in = owner_of(entry, count, width)
+            at = (device_of - first_device, row_in, jnp.int32(0))
+            current = lax.dynamic_slice(slots, at, (1, width, key_width))
+            slots = lax.dynamic_update_slice(slots, current + piece[None], at)
+    grad_keyval_full = slots[reach]
+    for offset in range(1, reach + 1):
+        from_lower = shifted(slots[reach + offset].astype(bf16), "ctx", offset).astype(f32)
+        from_upper = shifted(slots[reach - offset].astype(bf16), "ctx", -offset).astype(f32)
+        grad_keyval_full = grad_keyval_full + from_lower + from_upper
+    grad_keyval = grad_keyval_full.astype(bf16)
+    g_query_a, g_query_b, d_inner_query = adapter_back(
+        grad_query, act_one, inner_query, query_b, mask
+    )
+    g_keyval_a, g_keyval_b, d_inner_keyval = adapter_back(
+        grad_keyval, act_one, inner_keyval, keyval_b, mask
+    )
+    grad_act_one = (
+        by_cols(grad_query, full_query)
+        + by_cols(grad_keyval, full_keyval)
+        + by_cols(d_inner_query, query_a)
+        + by_cols(d_inner_keyval, keyval_a)
+    )
+    unused, pull_one = jax.vjp(lambda values: rms_scale(values, gain_attn), resid)
+    grad_tokens = (grad_middle + pull_one(grad_act_one)[0]).astype(bf16)
+    parts = [
+        g_query_a,
+        tiles_out(g_query_b),
+        g_keyval_a,
+        tiles_out(g_keyval_b),
+        g_output_a,
+        tiles_out(g_output_b),
+        g_gateup_a,
+        g_gateup_b.reshape(-1, 128),
+        g_down_a,
+        g_down_b.reshape(-1, 128),
+    ]
+    summed = reduce_packed(pack(parts)).reshape(-1, 128)
+    sums = []
+    start = 0
+    for at, part in enumerate(parts):
+        rows = part.shape[0]
+        piece = summed[start : start + rows].astype(f32)
+        sums.append(tiles_in(piece, 128) if at % 2 else piece)
+        start += rows
+    return (result, grad_tokens, *sums)
+
+
 def solution(mesh):
     in_specs = (
         P("ctx", None),
@@ -342,4 +874,5 @@
         P(),
     )
     out_specs = (P("ctx", None), P("ctx", None), P(), P(), P(), P(), P(), P(), P(), P(), P(), P())
+    local = local_own if mesh.shape["ctx"] == 32 else local_native
     return jax.shard_map(local, mesh=mesh, in_specs=in_specs, out_specs=out_specs, check_vma=False)

time: 933 us -> 602 us (0.65)
  waiting for transfers between devices: 515 us -> 11.2 us
  Pallas kernels: 0 us -> 408 us
  matrix products: 234 us -> 54.9 us
  blocking collectives: 46.3 us -> 0 us
  other arithmetic: 41.2 us -> 24 us
  between operations: 15.5 us -> 2.26 us
  local copies, waits for them, and re-layouts: 40.2 us -> 51.9 us
    pallas_call x0 -> x5, Pallas kernels: none -> 408 us  [the longest x1 163 us: mlp(): pl.pallas_call(functools.partial(mlp_kernel, ff), in_specs=[V] * 11 + [H,...]
    all_gather x4 -> x0, waiting for transfers between devices: 265 us -> none  [the longest x1 157 us: local(): lax.all_gather(w_gateup, 'ctx', axis=0, tiled=True)]
    psum x1 -> x0, waiting for transfers between devices: 227 us -> none  [local(): lax.psum((grad_query_a, grad_query_b, grad_keyval_a, grad_keyval_b, grad_...]
    dot_general x15 -> x2, matrix products: 88.3 us -> 3.45 us  [dot(): return lax.dot_general(a, b, dims, preferred_element_type=f32)]
    dot_general x15 -> x9, matrix products: 72.4 us -> 23 us  [by_cols(): lax.dot_general(left, right, (((1,), (1,)), ((), ())), preferred_element_...]
    all_gather x1 -> x0, blocking collectives: 46.3 us -> none  [local(): lax.all_gather(w_keyval, 'ctx', axis=0, tiled=True)]
    dot_general x4 -> x3, matrix products: 34 us -> 11.8 us  [adapted(): jnp.dot(inputs, weight, preferred_element_type=jnp.float32)]
    convert_element_type x6 -> x5, other arithmetic: 24.9 us -> 6.61 us  [the longest x1 1.98 us: local_own(): grad_keyval = grad_keyval_full.astype(bf16)]
  transfers between devices with their start and end apart: 21 -> 16, of which waited for: 9 -> 4; matrix products, arithmetic and copies ran while one was open for 12% -> 6% of each run, Pallas kernels for 0% -> 0%
where the time goes in v2:
time: 602 us; the launch traced here: 593 us
  Pallas kernels  408 us (68%)
  matrix products  54.9 us (9%)
  local copies, waits for them, and re-layouts  51.9 us (9%)
  starting transfers between devices  40.8 us (7%)
  other arithmetic  24 us (4%)
  waiting for transfers between devices  11.2 us (2%)
    pallas_call x1, Pallas kernels, mlp(): pl.pallas_call(functools.partial(mlp_kernel, ff), in_specs=[V] * 11 + [H,...  163 us
    pallas_call x1, Pallas kernels, gather_weights(): pl.pallas_call(functools.partial(gather_kernel, parts, events), out_shape...  113 us
    pallas_call x1, Pallas kernels, reduce_packed(): pl.pallas_call(functools.partial(reduce_kernel, rows), out_shape=jax.Shap...  89.8 us
    ppermute x16, starting transfers between devices, shifted(): return lax.ppermute(x, axis, pairs)  40.8 us
    unnamed x147, local copies, waits for them, and re-layouts  30.6 us
    pallas_call x1, Pallas kernels, att_fwd(): pl.pallas_call(functools.partial(att_fwd_kernel, span, window), grid=(2,...  24.3 us
    dot_general x9, matrix products, by_cols(): lax.dot_general(left, right, (((1,), (1,)), ((), ())), preferred_element_...  23 us
    pallas_call x1, Pallas kernels, att_bwd(): pl.pallas_call(functools.partial(att_bwd_kernel, span), grid=(2, subs), i...  17.9 us
  transfers between devices with their start and end apart: 16, of which 4 were waited for; matrix products, arithmetic and copies ran while one was open for 6% of the time, Pallas kernels for 0%

profile of v2, /device:TPU:0, one launch (start us, length us, event | category | flops | bytes accessed | tf_op | source)
XLA Modules:
  0.0 592.9 jit_solution(16864196840540650311)
XLA Ops:
  3.0 1.9 fusion.3
  6.2 112.8 %shard_map.292 = (bf16[2,2,2,2,2,48,1536]{6,5,4,3,2,1,0:T(8,128)(2,1)}, bf16[2,2,2,2,2,48,256]{6,5,4,3,2,1,0:T(8,128)(2,1)}, bf16[2,2,2,2,2,48,1536]{6,5,4,3,2,1...) custom-call(bf16[48,1536]{1,0:T(8,128)(2,1)} %refs_0_.1, bf16[48,256]{1,0:T(8,128)(2,1)} %refs_1_.1, ...), custom_call_target="tpu_custom_call" | custom-call | tf_op jit(solution)/shard_map/pallas_call | solution.py:482
  119.0 2.4 fusion.47
  123.1 3.0 collective-permute-start
  126.1 3.9 collective-permute-start.1
  130.0 4.4 collective-permute-start.2
  134.4 2.0 collective-permute-start.3
  136.4 1.3 collective-permute-start.4
  138.5 1.3 fusion.14
  139.9 4.3 fusion.50
  145.5 2.2 fusion.18.did_ref
  147.8 3.8 fusion.7.q_ref
  153.9 1.3 collective-permute-start.5
  156.1 1.3 collective-permute-start.6
  158.4 1.5 collective-permute-start.7
  163.8 1.6 collective-permute-done.5
  165.5 2.6 collective-permute-done.6
  168.1 4.5 collective-permute-done.7
  172.8 1.2 pad_maximum_fusion.kv_ref
  174.0 24.3 %att_fwd.1 = (bf16[512,1536]{1,0:T(8,128)(2,1)}, bf16[2,2,1536,1152]{3,2,1,0:T(8,128)(2,1)}) custom-call(bf16[512,1536]{1,0:T(8,128)(2,1)} %fusion.7.q_ref, bf16[2,1280,256]{2,1,0:T(8,128)(2,1)} %pad_maximum_fusion.kv_ref, s32[512,1]{1,0:T(8,128)} %copy.64.qseg_ref, s32[2,1,1280]{2,1,0:T(1,128)} %sub.142.kseg_ref), custom_call_target="tpu_custom_call" | custom-call | tf_op jit(solution)/shard_map/att_fwd/pallas_call | solution.py:529
  198.4 5.1 fusion.53
  206.3 1.2 fusion.17.igu_ref
  207.5 163.1 %mlp.1 = (bf16[512,1536]{1,0:T(8,128)(2,1)}, f32[512,1536]{1,0:T(8,128)}, bf16[1536,128]{1,0:T(8,128)(2,1)}, bf16[72,128,128]{2,1,0:T(8,128)(2,1)}, bf16[4608,12...) custom-call(bf16[512,1536]{1,0:T(8,128)(2,1)} %copy-done.11, ...), custom_call_target="tpu_custom_call" | custom-call | tf_op jit(solution)/shard_map/mlp/pallas_call | solution.py:683
  370.6 5.6 fusion.42
  377.6 1.7 fusion.8.do_ref
  379.3 17.9 %att_bwd.1 = (bf16[512,1536]{1,0:T(8,128)(2,1)}, f32[2,256,1280]{2,1,0:T(8,128)}) custom-call(bf16[512,1536]{1,0:T(8,128)(2,1)} %fusion.7.q_ref, bf16[2,1280,256]{2,1,0:T(8,128)(2,1)} %pad_maximum_fusion.kv_ref, bf16[512,1536]{1,0:T(8,128)(2,1)} %get-tuple-element.28.att_ref, bf16[512,1536]{1,0:T(8,128)(2,1)} %fusion.8.do_ref, ...), custom_call_target="tpu_custom_call" | custom-call | tf_op jit(solution)/shard_map/att_bwd/pallas_call | solution.py:562
  397.2 2.0 fusion.20
  399.2 7.2 %fusion.54 = f32[512,1536]{1,0:T(8,128)} fusion(bf16[512,1536]{1,0:T(8,128)(2,1)} %get-tuple-element.34, bf16[1536,1536]{1,0:T(8,128)(2,1)} %bitcast.210), kind=kOutput, calls=%fused_computation.165 | convolution fusion | flops 2415919104 | bytes 9437184 | tf_op jit(solution)/shard_map/dot_general | solution.py:69
  409.2 1.8 copy-done.3
  412.1 2.8 collective-permute-start.10
  414.9 1.3 collective-permute-start.11
  416.2 2.7 collective-permute-start.12
  418.9 1.3 collective-permute-start.13
  420.2 8.2 %collective-permute-start.14 = (bf16[512,256]{0,1:T(8,128)(2,1)}, bf16[512,256]{0,1:T(8,128)(2,1)}, u32[]{:S(2)}, u32[]{:S(2)}) collective-permute-start(bf16[512,256]{0,1:T(8,128)(2,1)} %get-tuple-element.85), channel_id=1, source_target_pairs={{0,4},{1,5},{2,6},{3,7},{4,8},{5,9},{6,10},{7,11},{8,12},{9,13},{1... | collective-permute-start | bytes 786440 | tf_op jit(solution)/shard_map/ppermute | solution.py:42
  428.4 1.6 fusion.11
  430.0 1.3 collective-permute-start.15
  431.3 3.4 collective-permute-start.8
  434.7 1.3 collective-permute-start.9
  437.2 1.9 copy.65
  439.1 1.9 copy.66
  441.9 1.9 copy.69
  443.9 1.8 constant_dynamic-update-slice_fusion.9
  445.7 2.4 collective-permute-done.14
  448.1 2.0 fusion.29
  450.1 1.6 fusion.13
  452.6 1.5 convert_element_type.224
  455.1 3.1 fusion.10
  458.9 1.4 fusion.9
  461.8 1.5 constant_dynamic-update-slice_fusion.5
  465.9 2.8 copy-done.2
  468.7 89.8 %shard_map.293 = bf16[2,2,2,2,2,784,128]{6,5,4,3,2,1,0:T(8,128)(2,1)S(1)} custom-call(bf16[2,2,2,2,2,784,128]{6,5,4,3,2,1,0:T(8,128)(2,1)S(1)} %bitcast.177), custom_call_target="tpu_custom_call" | custom-call | tf_op jit(solution)/shard_map/pallas_call | solution.py:404
  558.7 2.0 fusion.52
  560.7 1.6 slice_convert_fusion
  562.3 2.6 copy_bitcast_fusion
  565.9 2.3 copy.70
  568.1 2.3 copy.75
  570.4 1.9 convert_bitcast_fusion.2
  572.4 2.3 copy.72
  574.7 2.3 copy.76
  576.9 1.9 convert_bitcast_fusion.1
  578.9 2.3 copy.74
  581.2 2.3 copy.77
  584.1 2.8 convolution_add_fusion.5
  589.4 1.9 fusion.2
  (218 shorter events, 37.3 us)
Async XLA Ops:
  0.6 203.5 %copy-start = (bf16[128,1536]{1,0:T(8,128)(2,1)S(1)}, bf16[128,1536]{1,0:T(8,128)(2,1)}, u32[]{:S(2)}) copy-start(bf16[128,1536]{1,0:T(8,128)(2,1)} %param.37) | copy-start | bytes 1179652
  0.7 137.8 %copy-start.56 = (s32[128]{0:T(128)}, s32[128]{0:T(128)S(1)}, u32[]{:S(2)}) copy-start(s32[128]{0:T(128)S(1)} %and_select_fusion) | copy-start | bytes 1540
  2.3 119.2 %copy-start.58 = (s32[8]{0:T(128)}, s32[8]{0:T(128)S(1)}, u32[]{:S(2)}) copy-start(s32[8]{0:T(128)S(1)} %bitcast_subtract_fusion) | copy-start | bytes 100
  2.9 118.5 %copy-start.47 = (s32[512]{0:T(512)}, s32[512]{0:T(512)S(1)}, u32[]{:S(2)}) copy-start(s32[512]{0:T(512)S(1)} %broadcast_add_fusion.1) | copy-start | bytes 6148
  2.9 118.6 %copy-start.6 = (bf16[512,1536]{1,0:T(8,128)(2,1)S(1)}, bf16[512,1536]{1,0:T(8,128)(2,1)}, u32[]{:S(2)}) copy-start(bf16[512,1536]{1,0:T(8,128)(2,1)} %param.21) | copy-start | bytes 4718596
  2.9 118.6 %copy-start.26 = (bf16[1536,128]{1,0:T(8,128)(2,1)S(1)}, bf16[1536,128]{1,0:T(8,128)(2,1)}, u32[]{:S(2)}) copy-start(bf16[1536,128]{1,0:T(8,128)(2,1)} %param.34) | copy-start | bytes 1179652
  2.9 118.6 %copy-start.51 = (f32[1536]{0:T(1024)S(1)}, f32[1536]{0:T(1024)}, u32[]{:S(2)}) copy-start(f32[1536]{0:T(1024)} %param.30) | copy-start | bytes 18436
  5.5 134.4 %copy-start.54 = (f32[512]{0:T(512)}, f32[512]{0:T(512)S(1)}, u32[]{:S(2)}) copy-start(f32[512]{0:T(512)S(1)} %fusion.39) | copy-start | bytes 6148
  119.0 3.2 copy-start.42
  119.0 20.8 %slice-start = ((s8[4718592]{0:T(1024)(128)(4,1)}), s8[4194304]{0:T(1024)(128)(4,1)S(1)}, s32[]{:S(2)}) async-start(s8[4718592]{0:T(1024)(128)(4,1)} %bitcast.211), calls=%async_computation | async-start | bytes 8388608
  121.5 17.0 %copy-start.34 = (bf16[1536,128]{1,0:T(8,128)(2,1)S(1)}, bf16[1536,128]{1,0:T(8,128)(2,1)}, u32[]{:S(2)}) copy-start(bf16[1536,128]{1,0:T(8,128)(2,1)} %param.32) | copy-start | bytes 1179652
  121.5 18.3 %slice-start.1 = ((s8[4718592]{0:T(1024)(128)(4,1)}), s8[524288]{0:T(1024)(128)(4,1)S(1)}, s32[]{:S(2)}) async-start(s8[4718592]{0:T(1024)(128)(4,1)} %bitcast.211), calls=%async_computation.1 | async-start | bytes 1048576
  122.2 17.6 %copy-start.23 = (bf16[512,128]{1,0:T(8,128)(2,1)}, bf16[512,128]{1,0:T(8,128)(2,1)S(1)}, u32[]{:S(2)}) copy-start(bf16[512,128]{1,0:T(8,128)(2,1)S(1)} %fusion.15) | copy-start | bytes 393220
  122.2 17.6 %copy-start.52 = (f32[1536]{0:T(1024)S(1)}, f32[1536]{0:T(1024)}, u32[]{:S(2)}) copy-start(f32[1536]{0:T(1024)} %param.30) | copy-start | bytes 18436
  123.1 30.7 %collective-permute-start = (bf16[512,256]{1,0:T(8,128)(2,1)}, bf16[512,256]{1,0:T(8,128)(2,1)}, u32[]{:S(2)}, u32[]{:S(2)}) collective-permute-start(bf16[512,256]{1,0:T(8,128)(2,1)} %fusion.12), channel_id=1, source_target_pairs={{0,4},{1,5},{2,6},{3,7},{4,8},{5,9},{6,10},{7,11},{8,12},{9,13},{1... | collective-permute-start | bytes 786440 | tf_op jit(solution)/shard_map/ppermute | solution.py:42
  126.1 30.0 %collective-permute-start.1 = (bf16[512,256]{1,0:T(8,128)(2,1)}, bf16[512,256]{1,0:T(8,128)(2,1)}, u32[]{:S(2)}, u32[]{:S(2)}) collective-permute-start(bf16[512,256]{1,0:T(8,128)(2,1)} %fusion.12), channel_id=1, source_target_pairs={{0,3},{1,4},{2,5},{3,6},{4,7},{5,8},{6,9},{7,10},{8,11},{9,12},{10... | collective-permute-start | bytes 786440 | tf_op jit(solution)/shard_map/ppermute | solution.py:42
  130.0 28.4 %collective-permute-start.2 = (bf16[512,256]{1,0:T(8,128)(2,1)}, bf16[512,256]{1,0:T(8,128)(2,1)}, u32[]{:S(2)}, u32[]{:S(2)}) collective-permute-start(bf16[512,256]{1,0:T(8,128)(2,1)} %fusion.12), channel_id=1, source_target_pairs={{0,2},{1,3},{2,4},{3,5},{4,6},{5,7},{6,8},{7,9},{8,10},{9,11},{10,... | collective-permute-start | bytes 786440 | tf_op jit(solution)/shard_map/ppermute | solution.py:42
  134.4 26.5 %collective-permute-start.3 = (bf16[512,256]{1,0:T(8,128)(2,1)}, bf16[512,256]{1,0:T(8,128)(2,1)}, u32[]{:S(2)}, u32[]{:S(2)}) collective-permute-start(bf16[512,256]{1,0:T(8,128)(2,1)} %fusion.12), channel_id=1, source_target_pairs={{0,1},{1,2},{2,3},{3,4},{4,5},{5,6},{6,7},{7,8},{8,9},{9,10},{10,1... | collective-permute-start | bytes 786440 | tf_op jit(solution)/shard_map/ppermute | solution.py:42
  136.4 26.4 %collective-permute-start.4 = (bf16[512,256]{1,0:T(8,128)(2,1)}, bf16[512,256]{1,0:T(8,128)(2,1)}, u32[]{:S(2)}, u32[]{:S(2)}) collective-permute-start(bf16[512,256]{1,0:T(8,128)(2,1)} %fusion.12), channel_id=1, source_target_pairs={{1,0},{2,1},{3,2},{4,3},{5,4},{6,5},{7,6},{8,7},{9,8},{10,9},{11,1... | collective-permute-start | bytes 786440 | tf_op jit(solution)/shard_map/ppermute | solution.py:42
  139.9 4.3 copy-start.50
  139.9 5.7 copy-start.14
  147.8 3.8 copy-start.59
  147.8 4.0 copy-start.48
  147.8 5.5 copy-start.44
  153.9 11.6 %collective-permute-start.5 = (bf16[512,256]{1,0:T(8,128)(2,1)}, bf16[512,256]{1,0:T(8,128)(2,1)S(1)}, u32[]{:S(2)}, u32[]{:S(2)}) collective-permute-start(bf16[512,256]{1,0:T(8,128)(2,1)} %fusion.12), channel_id=1, source_target_pairs={{2,0},{3,1},{4,2},{5,3},{6,4},{7,5},{8,6},{9,7},{10,8},{11,9},{12,... | collective-permute-start | bytes 786440 | tf_op jit(solution)/shard_map/ppermute | solution.py:42
  156.1 12.0 %collective-permute-start.6 = (bf16[512,256]{1,0:T(8,128)(2,1)}, bf16[512,256]{1,0:T(8,128)(2,1)S(1)}, u32[]{:S(2)}, u32[]{:S(2)}) collective-permute-start(bf16[512,256]{1,0:T(8,128)(2,1)} %fusion.12), channel_id=1, source_target_pairs={{3,0},{4,1},{5,2},{6,3},{7,4},{8,5},{9,6},{10,7},{11,8},{12,9},{13... | collective-permute-start | bytes 786440 | tf_op jit(solution)/shard_map/ppermute | solution.py:42
  158.4 14.2 %collective-permute-start.7 = (bf16[512,256]{1,0:T(8,128)(2,1)}, bf16[512,256]{1,0:T(8,128)(2,1)S(1)}, u32[]{:S(2)}, u32[]{:S(2)}) collective-permute-start(bf16[512,256]{1,0:T(8,128)(2,1)} %fusion.12), channel_id=1, source_target_pairs={{4,0},{5,1},{6,2},{7,3},{8,4},{9,5},{10,6},{11,7},{12,8},{13,9},{1... | collective-permute-start | bytes 786440 | tf_op jit(solution)/shard_map/ppermute | solution.py:42
  198.4 5.1 copy-start.9
  198.4 5.1 copy-start.28
  198.4 5.1 copy-start.57
  205.0 2.5 copy-start.5
  370.6 5.7 copy-start.4
  377.1 2.1 copy-start.18
  379.3 17.9 %copy-start.30 = (bf16[128,1536]{1,0:T(8,128)(2,1)S(1)}, bf16[128,1536]{1,0:T(8,128)(2,1)}, u32[]{:S(2)}) copy-start(bf16[128,1536]{1,0:T(8,128)(2,1)} %param.33) | copy-start | bytes 1179652
  399.2 29.2 %copy-start.40 = (bf16[512,128]{1,0:T(8,128)(2,1)}, bf16[512,128]{1,0:T(8,128)(2,1)S(1)}, u32[]{:S(2)}) copy-start(bf16[512,128]{1,0:T(8,128)(2,1)S(1)} %fusion.20) | copy-start | bytes 393220
  408.8 2.2 copy-start.3
  411.0 17.4 %copy-start.7 = (bf16[512,1536]{1,0:T(8,128)(2,1)S(1)}, bf16[512,1536]{1,0:T(8,128)(2,1)}, u32[]{:S(2)}) copy-start(bf16[512,1536]{1,0:T(8,128)(2,1)} %param.21) | copy-start | bytes 4718596
  411.0 17.4 %copy-start.53 = (f32[1536]{0:T(1024)S(1)}, f32[1536]{0:T(1024)}, u32[]{:S(2)}) copy-start(f32[1536]{0:T(1024)} %param.30) | copy-start | bytes 18436
  411.0 17.4 %copy-start.55 = (f32[512]{0:T(512)S(1)}, f32[512]{0:T(512)}, u32[]{:S(2)}) copy-start(f32[512]{0:T(512)} %copy-done.54) | copy-start | bytes 6148
  411.0 25.0 %copy-start.17 = (bf16[512,1536]{1,0:T(8,128)(2,1)S(1)}, bf16[512,1536]{1,0:T(8,128)(2,1)}, u32[]{:S(2)}) copy-start(bf16[512,1536]{1,0:T(8,128)(2,1)} %get-tuple-element.34) | copy-start | bytes 4718596
  411.0 25.0 %copy-start.25 = (bf16[512,128]{1,0:T(8,128)(2,1)S(1)}, bf16[512,128]{1,0:T(8,128)(2,1)}, u32[]{:S(2)}) copy-start(bf16[512,128]{1,0:T(8,128)(2,1)} %fusion.14) | copy-start | bytes 393220
  412.1 17.9 %collective-permute-start.10 = (bf16[512,256]{0,1:T(8,128)(2,1)S(1)}, bf16[512,256]{0,1:T(8,128)(2,1)S(1)}, u32[]{:S(2)}, u32[]{:S(2)}) collective-permute-start(bf16[512,256]{0,1:T(8,128)(2,1)S(1)} %get-tuple-element.89), channel_id=1, source_target_pairs={{0,2},{1,3},{2,4},{3,5},{4,6},{5,7},{6,8},{7,9},{8,10},{9,11},{10,... | collective-permute-start | bytes 786440 | tf_op jit(solution)/shard_map/ppermute | solution.py:42
  414.9 16.4 %collective-permute-start.11 = (bf16[512,256]{0,1:T(8,128)(2,1)S(1)}, bf16[512,256]{0,1:T(8,128)(2,1)S(1)}, u32[]{:S(2)}, u32[]{:S(2)}) collective-permute-start(bf16[512,256]{0,1:T(8,128)(2,1)S(1)} %get-tuple-element.88), channel_id=1, source_target_pairs={{2,0},{3,1},{4,2},{5,3},{6,4},{7,5},{8,6},{9,7},{10,8},{11,9},{12,... | collective-permute-start | bytes 786440 | tf_op jit(solution)/shard_map/ppermute | solution.py:42
  416.2 18.5 %collective-permute-start.12 = (bf16[512,256]{0,1:T(8,128)(2,1)S(1)}, bf16[512,256]{0,1:T(8,128)(2,1)S(1)}, u32[]{:S(2)}, u32[]{:S(2)}) collective-permute-start(bf16[512,256]{0,1:T(8,128)(2,1)S(1)} %get-tuple-element.87), channel_id=1, source_target_pairs={{0,3},{1,4},{2,5},{3,6},{4,7},{5,8},{6,9},{7,10},{8,11},{9,12},{10... | collective-permute-start | bytes 786440 | tf_op jit(solution)/shard_map/ppermute | solution.py:42
  418.9 26.8 %collective-permute-start.13 = (bf16[512,256]{0,1:T(8,128)(2,1)}, bf16[512,256]{0,1:T(8,128)(2,1)}, u32[]{:S(2)}, u32[]{:S(2)}) collective-permute-start(bf16[512,256]{0,1:T(8,128)(2,1)} %get-tuple-element.86), channel_id=1, source_target_pairs={{3,0},{4,1},{5,2},{6,3},{7,4},{8,5},{9,6},{10,7},{11,8},{12,9},{13... | collective-permute-start | bytes 786440 | tf_op jit(solution)/shard_map/ppermute | solution.py:42
  420.2 27.9 %collective-permute-start.14 = (bf16[512,256]{0,1:T(8,128)(2,1)}, bf16[512,256]{0,1:T(8,128)(2,1)}, u32[]{:S(2)}, u32[]{:S(2)}) collective-permute-start(bf16[512,256]{0,1:T(8,128)(2,1)} %get-tuple-element.85), channel_id=1, source_target_pairs={{0,4},{1,5},{2,6},{3,7},{4,8},{5,9},{6,10},{7,11},{8,12},{9,13},{1... | collective-permute-start | bytes 786440 | tf_op jit(solution)/shard_map/ppermute | solution.py:42
  430.0 4.7 copy-start.36
  430.0 18.1 %collective-permute-start.15 = (bf16[512,256]{0,1:T(8,128)(2,1)}, bf16[512,256]{0,1:T(8,128)(2,1)}, u32[]{:S(2)}, u32[]{:S(2)}) collective-permute-start(bf16[512,256]{0,1:T(8,128)(2,1)} %get-tuple-element.84), channel_id=1, source_target_pairs={{4,0},{5,1},{6,2},{7,3},{8,4},{9,5},{10,6},{11,7},{12,8},{13,9},{1... | collective-permute-start | bytes 786440 | tf_op jit(solution)/shard_map/ppermute | solution.py:42
  431.3 3.4 copy-start.37
  431.3 16.8 %collective-permute-start.8 = (bf16[512,256]{0,1:T(8,128)(2,1)}, bf16[512,256]{0,1:T(8,128)(2,1)}, u32[]{:S(2)}, u32[]{:S(2)}) collective-permute-start(bf16[512,256]{0,1:T(8,128)(2,1)} %get-tuple-element.83), channel_id=1, source_target_pairs={{0,1},{1,2},{2,3},{3,4},{4,5},{5,6},{6,7},{7,8},{8,9},{9,10},{10,1... | collective-permute-start | bytes 786440 | tf_op jit(solution)/shard_map/ppermute | solution.py:42
  434.7 13.4 %collective-permute-start.9 = (bf16[512,256]{0,1:T(8,128)(2,1)}, bf16[512,256]{0,1:T(8,128)(2,1)}, u32[]{:S(2)}, u32[]{:S(2)}) collective-permute-start(bf16[512,256]{0,1:T(8,128)(2,1)} %get-tuple-element.90), channel_id=1, source_target_pairs={{1,0},{2,1},{3,2},{4,3},{5,4},{6,5},{7,6},{8,7},{9,8},{10,9},{11,1... | collective-permute-start | bytes 786440 | tf_op jit(solution)/shard_map/ppermute | solution.py:42
  443.9 6.2 %copy-start.43 = (bf16[128,256]{1,0:T(8,128)(2,1)S(1)}, bf16[128,256]{1,0:T(8,128)(2,1)}, u32[]{:S(2)}) copy-start(bf16[128,256]{1,0:T(8,128)(2,1)} %param.35) | copy-start | bytes 196612
  443.9 7.9 %copy-start.24 = (bf16[512,128]{1,0:T(8,128)(2,1)S(1)}, bf16[512,128]{1,0:T(8,128)(2,1)}, u32[]{:S(2)}) copy-start(bf16[512,128]{1,0:T(8,128)(2,1)} %copy-done.23) | copy-start | bytes 393220
  450.1 8.8 %copy-start.19 = (bf16[512,128]{1,0:T(8,128)(2,1)S(1)}, bf16[512,128]{1,0:T(8,128)(2,1)}, u32[]{:S(2)}) copy-start(bf16[512,128]{1,0:T(8,128)(2,1)} %copy-done.18) | copy-start | bytes 393220
  454.1 4.8 copy-start.10
  454.1 6.1 %copy-start.16 = (bf16[12,128,128]{2,1,0:T(8,128)(2,1)S(1)}, bf16[12,128,128]{2,1,0:T(8,128)(2,1)}, u32[]{:S(2)}) copy-start(bf16[12,128,128]{2,1,0:T(8,128)(2,1)} %copy.69) | copy-start | bytes 1179652
  455.1 6.0 %copy-start.32 = (bf16[1536,128]{1,0:T(8,128)(2,1)S(1)}, bf16[1536,128]{1,0:T(8,128)(2,1)}, u32[]{:S(2)}) copy-start(bf16[1536,128]{1,0:T(8,128)(2,1)} %get-tuple-element.36) | copy-start | bytes 1179652
  455.1 6.7 %copy-start.13 = (bf16[72,128,128]{2,1,0:T(8,128)(2,1)S(1)}, bf16[72,128,128]{2,1,0:T(8,128)(2,1)}, u32[]{:S(2)}) copy-start(bf16[72,128,128]{2,1,0:T(8,128)(2,1)} %get-tuple-element.37) | copy-start | bytes 7077892
  460.3 3.1 copy-start.20
  461.8 2.6 copy-start.31
  465.9 2.8 copy-start.2
  584.1 2.8 copy-start.35
  584.1 2.8 copy-start.41
  589.4 3.1 copy-start.1
  (14 other events, 17.0 us)

commit v3 on v0

--- a/solution.py
+++ b/solution.py
@@ -1,6 +1,10 @@
+import functools
+
 import jax
 import jax.numpy as jnp
 from jax import lax
+from jax.experimental import pallas as pl
+from jax.experimental.pallas import tpu as pltpu
 from jax.sharding import PartitionSpec as P
 
 HEADS = 12
@@ -13,6 +17,22 @@
 
 NORM_EPS = 1e-06
 MASKED = -1e30
+
+
+MESH = pl.DeviceIdType.MESH
+bf16 = jnp.bfloat16
+f32 = jnp.float32
+NN = (((1,), (0,)), ((), ()))
+NT = (((1,), (1,)), ((), ()))
+TN = (((0,), (0,)), ((), ()))
+VMEM = pl.BlockSpec(memory_space=pltpu.VMEM)
+HBM = pl.BlockSpec(memory_space=pl.ANY)
+ORD_A = (4, 3, 1, 2, 0)
+ORD_A2 = (4, 3, 2, 1, 0)
+ORD_B = (4, 1, 2, 3, 0)
+ORD_B2 = (4, 2, 1, 3, 0)
+ORD_C = (4, 2, 3, 1, 0)
+ORD_C2 = (4, 1, 3, 2, 0)
 
 
 def shifted(x, axis, by):
@@ -128,7 +148,7 @@
     return (grad_query.reshape(rows, -1), jnp.concatenate([grad_key, grad_value], axis=1))
 
 
-def local(
+def local_native(
     tokens,
     cotangent,
     doc_lengths,
@@ -317,6 +337,893 @@
     )
 
 
+def flip(me, bits, b):
+    return (me+(1-2*bits[b])*(1<<b),)
+def reduce_kernel(rows, in_ref, out_ref, r0, r1, r2, r3, r4, ssem, rsem):
+    rb=(r0,r1,r2,r3,r4)
+    me=lax.axis_index("ctx")
+    bits=[(me//(1<<b))%2 for b in range(5)]
+    bar=pltpu.get_barrier_semaphore()
+    for b in range(5):
+        pl.semaphore_signal(bar,1,device_id=flip(me,bits,b),device_id_type=MESH)
+    pl.semaphore_wait(bar,5)
+    t=rows//16
+    a=round(t*3/7); bb=round(t*3/14)
+    classes=[(0,a*16,ORD_A),(a*16,bb*16,ORD_B),((a+bb)*16,rows-(a+bb)*16,ORD_C)]
+    def rs(cl,s):
+        r0_,n,order=classes[cl]
+        red=order[::-1]
+        bit=red[s]; done=red[:s]
+        rem=[b for b in (4,3,2,1,0) if b not in done]
+        src=in_ref if s==0 else rb[s-1]
+        idx=tuple((1-bits[b]) if b==bit else slice(None) for b in rem)
+        return pltpu.make_async_remote_copy(src.at[idx+(pl.ds(r0_,n),)],rb[s].at[(slice(None),)*(4-s)+(pl.ds(r0_,n),)],ssem.at[cl,s],rsem.at[cl,s],device_id=flip(me,bits,bit),device_id_type=MESH)
+    def add(cl,s):
+        r0_,n,order=classes[cl]
+        red=order[::-1]
+        bit=red[s]; done=red[:s]
+        rem=[b for b in (4,3,2,1,0) if b not in done]
+        src=in_ref if s==0 else rb[s-1]
+        rs_=pl.ds(r0_,n)
+        nd=4-s
+        def body(j,_):
+            ds=[(j//(1<<(nd-1-i)))%2 for i in range(nd)]
+            it=iter(ds)
+            si=tuple(bits[b] if b==bit else next(it) for b in rem)
+            v=src[si+(rs_,)].astype(f32)+rb[s][tuple(ds)+(rs_,)].astype(f32)
+            rb[s][tuple(ds)+(rs_,)]=v.astype(bf16)
+            return 0
+        lax.fori_loop(0,1<<nd,body,0)
+    def ag(cl,k):
+        r0_,n,order=classes[cl]
+        bit=order[k]; have=order[:k]
+        idx=tuple(slice(None) if b in have else bits[b] for b in (4,3,2,1,0))+(pl.ds(r0_,n),)
+        src=out_ref.at[idx] if k else rb[4].at[pl.ds(r0_,n)]
+        return pltpu.make_async_remote_copy(src,out_ref.at[idx],ssem.at[cl,5+k],rsem.at[cl,5+k],device_id=flip(me,bits,bit),device_id_type=MESH)
+    for cl in range(3): rs(cl,0).start()
+    for s in range(5):
+        for cl in range(3):
+            rs(cl,s).wait_recv()
+            add(cl,s)
+            if s<4: rs(cl,s+1).start()
+            else:
+                ag(cl,0).start()
+                r0_,n,_=classes[cl]
+                out_ref[bits[4],bits[3],bits[2],bits[1],bits[0],pl.ds(r0_,n)]=rb[4][pl.ds(r0_,n)]
+    for k in range(1,5):
+        for cl in range(3):
+            ag(cl,k-1).wait_recv()
+            ag(cl,k).start()
+    for cl in range(3): ag(cl,4).wait_recv()
+    for cl in range(3):
+        for s in range(5):
+            rs(cl,s).wait_send(); ag(cl,s).wait_send()
+def reduce_packed(x, cid=1):
+    rows=x.shape[5]
+    return pl.pallas_call(functools.partial(reduce_kernel,rows),
+        out_shape=jax.ShapeDtypeStruct(x.shape,x.dtype),
+        in_specs=[pl.BlockSpec(memory_space=pltpu.VMEM)],out_specs=pl.BlockSpec(memory_space=pltpu.VMEM),
+        scratch_shapes=[pltpu.VMEM((2,)*(4-s)+(rows,128),bf16) for s in range(5)]+[pltpu.SemaphoreType.DMA((3,10)),pltpu.SemaphoreType.DMA((3,10))],
+        compiler_params=pltpu.CompilerParams(collective_id=cid,has_side_effects=True,vmem_limit_bytes=40<<20))(x)
+
+
+BGROUP = 6
+CHUNK = 512
+UNIT = 256
+SUB = 128
+GROUP = 4
+SCALE = HD ** (-0.5)
+LAGS = (0, 1, 2, 4, 6)
+SOFT_UNROLL = 8
+AHEAD = 24
+
+
+def dot(a, b, dims=NN):
+    return lax.dot_general(a, b, dims, preferred_element_type=f32)
+
+
+def tile_at(i, size):
+    return pl.ds(i * size if isinstance(i, int) else pl.multiple_of(i * size, size), size)
+
+
+def even_odd(par, low, high):
+    if par % 2:
+        return ((low, 2, ORD_A2), (high, 1, ORD_C2), (high + 1, 1, ORD_B2))
+    return ((low, 2, ORD_A), (high, 1, ORD_C), (high + 1, 1, ORD_B))
+
+
+def bits_of(me):
+    return [(me // (1 << b)) % 2 for b in range(5)]
+
+
+def meet_all(count, me):
+    barrier = pltpu.get_barrier_semaphore()
+
+    def greet(k, unused):
+        pl.semaphore_signal(
+            barrier, 1, device_id=(lax.rem(me + k, count),), device_id_type=MESH
+        )
+        return unused
+
+    lax.fori_loop(1, count, greet, 0)
+    pl.semaphore_wait(barrier, count - 1)
+
+
+def heads_down(x):
+    return jnp.concatenate([x[:, i * HD : (i + 1) * HD] for i in range(x.shape[1] // HD)], axis=0)
+
+
+def heads_across(x):
+    return jnp.concatenate([x[i * SUB : (i + 1) * SUB] for i in range(x.shape[0] // SUB)], axis=1)
+
+
+def norm_rows(read, gain_ref, write, rows):
+    def block(r, unused):
+        at = tile_at(r, 16)
+        x = read(at)
+        scale = lax.rsqrt(jnp.mean(x * x, axis=1, keepdims=True) + NORM_EPS)
+        write(at, (x * scale * gain_ref[...]).astype(bf16))
+        return unused
+
+    lax.fori_loop(0, rows // 16, block, 0, unroll=8)
+
+
+def forward_kernel(
+    count,
+    x_ref,
+    g_ref,
+    mask_ref,
+    qseg_ref,
+    kseg_ref,
+    gain1_ref,
+    gain2_ref,
+    qa_ref,
+    qb_ref,
+    ka_ref,
+    kb_ref,
+    oa_ref,
+    ob_ref,
+    ga_ref,
+    gb_ref,
+    da_ref,
+    db_ref,
+    wq_own,
+    wk_own,
+    wo_own,
+    wd_own,
+    wg_own,
+    out_ref,
+    dmid_ref,
+    a1_ref,
+    q_ref,
+    keys_ref,
+    att_ref,
+    iq_ref,
+    ik_ref,
+    io_ref,
+    gga_ref,
+    ggb_ref,
+    gda_ref,
+    gdb_ref,
+    prob_hbm,
+    wq_all,
+    wk_all,
+    wo_all,
+    wd_all,
+    wg_all,
+    held_q,
+    held_k,
+    held_o,
+    held_d,
+    held_g,
+    wbuf,
+    dbuf,
+    pbuf,
+    kv_own,
+    a2_s,
+    igu_s,
+    did_s,
+    acc_o,
+    acc_a,
+    gu_s,
+    dh_s,
+    hid_s,
+    dgu_s,
+    wsem,
+    dsem,
+    psem,
+    own_sem,
+    xsend,
+    xrecv,
+    hsend,
+    hrecv,
+):
+    rows, d = x_ref.shape
+    width = rows // 2
+    reach = WINDOW // width
+    keys = keys_ref.shape[1]
+    span = keys - width + SUB
+    ff = da_ref.shape[0]
+    nu, nc = ff // UNIT, ff // CHUNK
+    me = lax.axis_index("ctx")
+    bits = bits_of(me)
+    meet_all(count, me)
+    here = (bits[4], bits[3], bits[2], bits[1], bits[0])
+    own = (wq_own, wk_own, wo_own, wd_own, wg_own)
+    held = (held_q, held_k, held_o, held_d, held_g)
+    full = (wq_all, wk_all, wo_all, wd_all, wg_all)
+
+    def where(bit_set):
+        return tuple(pl.ds(0, 2) if b in bit_set else bits[b] for b in (4, 3, 2, 1, 0))
+
+    def remote(src, dst, send, recv, bit):
+        return pltpu.make_async_remote_copy(
+            src, dst, send, recv, device_id=flip(me, bits, bit), device_id_type=MESH
+        )
+
+    units = []
+    for u in range(3):
+        units.append((0, 0, even_odd(u, 4 * u, 4 * u + 2)))
+    units.append((1, 0, ((0, 1, ORD_A), (1, 1, ORD_C2))))
+    for u in range(3):
+        units.append((2, 0, even_odd(u, 4 * u, 4 * u + 2)))
+    thick = wd_own.shape[0] // 3
+    for u in range(9):
+        units.append((3, u // 3 * thick, even_odd(u + 1, u % 3 * 4, u % 3 * 4 + 2)))
+    first = len(units)
+
+    def exchange(u, cl, k):
+        w, row, split = units[u]
+        tile, tiles, order = split[cl]
+        lines = pl.ds(row, wq_own.shape[0])
+        cols = pl.ds(tile * 128, tiles * 128)
+        there = full[w].at[where(order[:k]) + (lines, cols)]
+        return remote(
+            there if k else own[w].at[lines, cols],
+            there,
+            xsend.at[u, cl, k],
+            xrecv.at[u, cl, k],
+            order[k],
+        )
+
+    def gate(v, par, cl, k):
+        tile, tiles, order = even_odd(par, 0, ff // 128)[cl]
+        at = tile * 128 + v * UNIT
+        cols = pl.ds(at if isinstance(at, int) else pl.multiple_of(at, 128), tiles * 128)
+        there = wg_all.at[where(order[:k]) + (slice(None), cols)]
+        return remote(
+            there if k else wg_own.at[:, cols],
+            there,
+            xsend.at[first + v, cl, k],
+            xrecv.at[first + v, cl, k],
+            order[k],
+        )
+
+    staged = [pltpu.make_async_copy(own[w], held[w], own_sem.at[w]) for w in range(5)]
+    placed = [pltpu.make_async_copy(held[w], full[w].at[here], own_sem.at[w]) for w in range(5)]
+    for copy in staged:
+        copy.start()
+    state = {"step": 0, "placed": set()}
+
+    def place(w):
+        if w not in state["placed"]:
+            state["placed"].add(w)
+            placed[w].wait()
+
+    def steps(n):
+        while state["step"] < n:
+            t = state["step"]
+            state["step"] += 1
+            for k in (4, 3, 2, 1, 0):
+                u = t - LAGS[k]
+                if not 0 <= u < first + nu:
+                    continue
+                w = units[u][0] if u < first else 4
+                if k:
+                    place(w)
+                for cl in range(2 if w == 1 else 3):
+                    at = (
+                        functools.partial(exchange, u, cl)
+                        if u < first
+                        else functools.partial(gate, u - first, (u - first) % 2, cl)
+                    )
+                    if k:
+                        at(k - 1).wait_recv()
+                    at(k).start()
+
+    def loop_steps(c, point):
+        for i in (2 * point, 2 * point + 1):
+            t, k = i // 5, 4 - i % 5
+            v = 2 * c + t + AHEAD - first - LAGS[k]
+            par = (t + AHEAD - first - LAGS[k]) % 2
+
+            @pl.when(v < nu)
+            def _(v=v, par=par, k=k):
+                for cl in range(3):
+                    if k:
+                        gate(v, par, cl, k - 1).wait_recv()
+                    gate(v, par, cl, k).start()
+
+    def arrived(weight_at):
+        for u, unit in enumerate(units):
+            if unit[0] == weight_at:
+                for cl in range(len(unit[2])):
+                    exchange(u, cl, 4).wait_recv()
+
+    def load(w, lo, n, slot, at, sem):
+        return pltpu.make_async_copy(
+            full[w].at[(slice(None),) * 6 + (pl.ds(lo, n),)],
+            wbuf.at[(slot,) + (slice(None),) * 6 + (pl.ds(at, n),)],
+            wsem.at[slot, sem],
+        )
+
+    def weight(slot, lo, n):
+        return wbuf[slot, :, :, :, :, :, :, lo : lo + n].reshape(-1, n)
+
+    for w in range(5):
+        staged[w].wait()
+        placed[w].start()
+    steps(4)
+    def read_x(at):
+        return x_ref[at, :].astype(f32)
+
+    def write_a1(at, y):
+        a1_ref[at, :] = y
+
+    norm_rows(read_x, gain1_ref, write_a1, rows)
+    iq_ref[...] = (dot(a1_ref[...], qa_ref[...]) * mask_ref[...]).astype(bf16)
+    ik_ref[...] = (dot(a1_ref[...], ka_ref[...]) * mask_ref[...]).astype(bf16)
+    did_s[...] = (dot(g_ref[...], db_ref[...], NT) * mask_ref[...]).astype(bf16)
+    steps(10)
+    arrived(0)
+    arrived(1)
+    loads = [load(0, 0, 1024, 0, 0, 0), load(0, 1024, d - 1024, 1, 0, 0)]
+    loads.append(load(1, 0, 2 * HD, 1, d - 1024, 1))
+    for copy in loads:
+        copy.start()
+    for copy in loads:
+        copy.wait()
+
+    def beside(a, b):
+        return jnp.concatenate([a, b], axis=1)
+
+    def under(a, b):
+        return jnp.concatenate([a, b], axis=0)
+
+    kv_own[...] = dot(
+        beside(a1_ref[...], ik_ref[...]), under(weight(1, d - 1024, 2 * HD), kb_ref[...])
+    ).astype(bf16)
+    keys_ref[0, pl.ds(reach * width, width)] = kv_own[pl.ds(0, width)]
+    keys_ref[1, pl.ds(reach * width, width)] = kv_own[pl.ds(width, width)]
+
+    def low(j):
+        block = me + j
+        upper = block // count
+        target = block + upper * (2 * count - 1 - 2 * block)
+        copy = pltpu.make_async_remote_copy(
+            kv_own.at[pl.ds(0, width)],
+            keys_ref.at[upper, pl.ds((reach - j) * width, width)],
+            hsend.at[0, j],
+            hrecv.at[upper, j],
+            device_id=(target,),
+            device_id_type=MESH,
+        )
+        return copy, target
+
+    def high(j):
+        return pltpu.make_async_remote_copy(
+            kv_own.at[pl.ds(width, width)],
+            keys_ref.at[1, pl.ds((reach - j) * width, width)],
+            hsend.at[1, j],
+            hrecv.at[1, j],
+            device_id=(me - j,),
+            device_id_type=MESH,
+        )
+
+    def incoming(which, j):
+        return pltpu.make_async_remote_copy(
+            kv_own.at[pl.ds(0, width)],
+            keys_ref.at[which, pl.ds((reach - j) * width, width)],
+            hsend.at[0, j],
+            hrecv.at[which, j],
+            device_id=flip(me, bits, 0),
+            device_id_type=MESH,
+        )
+
+    for j in range(1, reach + 1):
+        copy, target = low(j)
+        pl.when(target != me)(copy.start)
+        pl.when(me >= j)(high(j).start)
+
+        @pl.when(target == me)
+        def _(j=j):
+            keys_ref[1, pl.ds((reach - j) * width, width)] = kv_own[pl.ds(0, width)]
+
+        @pl.when(me < j)
+        def _(j=j):
+            keys_ref[0, pl.ds((reach - j) * width, width)] = jnp.zeros((width, 2 * HD), bf16)
+
+    steps(11)
+    q_ref[:, :1024] = dot(
+        beside(a1_ref[...], iq_ref[...]), under(weight(0, 0, 1024), qb_ref[:, :1024])
+    ).astype(bf16)
+    q_ref[:, 1024:] = dot(
+        beside(a1_ref[...], iq_ref[...]), under(weight(1, 0, d - 1024), qb_ref[:, 1024:])
+    ).astype(bf16)
+    for j in range(1, reach + 1):
+        pl.when(me >= j)(incoming(0, j).wait_recv)
+        pl.when(2 * me != 2 * count - 1 - j)(incoming(1, j).wait_recv)
+    steps(12)
+
+    groups = HEADS // GROUP
+    subs = width // SUB
+    turn = 0
+    for which in range(2):
+        for s in range(subs):
+            base = s * SUB
+            lines = slice(which * width + base, which * width + base + SUB)
+            row = lax.broadcasted_iota(jnp.int32, (SUB, span), 0)
+            col = lax.broadcasted_iota(jnp.int32, (SUB, span), 1)
+            ok = (
+                (col <= row + (span - SUB))
+                & (col > row + (span - SUB - WINDOW))
+                & (kseg_ref[which, :, base : base + span] == qseg_ref[lines, :])
+            )
+            acc_a[:SUB, :span] = jnp.where(ok, 0.0, MASKED)
+
+            for g in range(groups):
+                heads = slice(g * GROUP * HD, (g + 1) * GROUP * HD)
+                k = keys_ref[which, base : base + span, :HD]
+                v = keys_ref[which, base : base + span, HD:]
+                acc_o[: GROUP * SUB, :span] = dot(heads_down(q_ref[lines, heads]), k, NT)
+                slot = turn % 2
+                if turn >= 2:
+                    pltpu.make_async_copy(
+                        pbuf.at[slot], prob_hbm.at[0, 0, pl.ds(0, GROUP * SUB)], psem.at[slot]
+                    ).wait()
+
+                def soft(r, unused, slot=slot):
+                    at = tile_at(r, 16)
+                    bias = acc_a[tile_at(r % (SUB // 16), 16), :span]
+                    sc = acc_o[at, :span] * SCALE + bias
+                    e = jnp.exp(sc - jnp.max(sc, axis=1, keepdims=True))
+                    inv = 1.0 / jnp.sum(e, axis=1, keepdims=True)
+                    pbuf[slot, at, :] = (e * inv).astype(bf16)
+                    return unused
+
+                lax.fori_loop(0, GROUP * SUB // 16, soft, 0, unroll=SOFT_UNROLL)
+                pltpu.make_async_copy(
+                    pbuf.at[slot],
+                    prob_hbm.at[which, s, pl.ds(g * GROUP * SUB, GROUP * SUB)],
+                    psem.at[slot],
+                ).start()
+                att_ref[lines, heads] = heads_across(dot(pbuf[slot], v)).astype(bf16)
+                turn += 1
+            steps(13 + which * subs + s)
+    for slot in range(2):
+        pltpu.make_async_copy(
+            pbuf.at[slot], prob_hbm.at[0, 0, pl.ds(0, GROUP * SUB)], psem.at[slot]
+        ).wait()
+    arrived(2)
+    loads = [load(2, 0, 1024, 0, 0, 0), load(2, 1024, d - 1024, 1, 0, 0)]
+    for copy in loads:
+        copy.start()
+    io_ref[...] = (dot(att_ref[...], oa_ref[...]) * mask_ref[...]).astype(bf16)
+    for copy in loads:
+        copy.wait()
+    dmid_ref[:, :1024] = x_ref[:, :1024].astype(f32) + dot(
+        beside(att_ref[...], io_ref[...]), under(weight(0, 0, 1024), ob_ref[:, :1024])
+    )
+    dmid_ref[:, 1024:] = x_ref[:, 1024:].astype(f32) + dot(
+        beside(att_ref[...], io_ref[...]), under(weight(1, 0, d - 1024), ob_ref[:, 1024:])
+    )
+    steps(17)
+
+    def read_mid(at):
+        return dmid_ref[at, :]
+
+    def write_a2(at, y):
+        a2_s[at, :] = y
+
+    norm_rows(read_mid, gain2_ref, write_a2, rows)
+    igu_s[...] = (dot(a2_s[...], ga_ref[...]) * mask_ref[...]).astype(bf16)
+    acc_o[...] = jnp.zeros_like(acc_o)
+    acc_a[...] = jnp.zeros_like(acc_a)
+    steps(AHEAD)
+    arrived(3)
+
+    def arrived_gate(c):
+        for j in range(CHUNK // UNIT):
+            for cl in range(3):
+                gate(c * (CHUNK // UNIT) + j, j % 2, cl, 4).wait_recv()
+
+    def down_rows(c):
+        return wd_rows.at[tile_at(c, CHUNK)]
+
+    wd_rows = wd_all.reshape(ff, d)
+
+    def fetch(c, slot):
+        cps = [
+            pltpu.make_async_copy(
+                wg_all.at[(slice(None),) * 6 + (tile_at_base(base, c),)],
+                wbuf.at[(slot,) + (slice(None),) * 6 + (pl.ds(o, CHUNK),)],
+                wsem.at[slot, i],
+            )
+            for i, (base, o) in enumerate(((0, 0), (ff, CHUNK)))
+        ]
+        cps.append(pltpu.make_async_copy(down_rows(c), dbuf.at[slot], dsem.at[slot]))
+        return cps
+
+    def tile_at_base(base, c):
+        at = base + c * CHUNK
+        return pl.ds(at if isinstance(at, int) else pl.multiple_of(at, 128), CHUNK)
+
+    arrived_gate(0)
+    for copy in fetch(0, 0):
+        copy.start()
+    for copy in fetch(0, 0):
+        copy.wait()
+
+    def chunk(c, unused):
+        slot = c % 2
+        loop_steps(c, 0)
+        gbc = beside(gb_ref[:, tile_at_base(0, c)], gb_ref[:, tile_at_base(ff, c)])
+        dac = da_ref[tile_at(c, CHUNK), :]
+
+        def wx():
+            return under(weight(slot, 0, 2 * CHUNK), gbc)
+
+        def wdx():
+            return beside(dbuf[slot], dac)
+
+        gu_s[...] = dot(beside(a2_s[...], igu_s[...]), wx())
+        loop_steps(c, 1)
+        dh_s[...] = dot(beside(g_ref[...], did_s[...]), wdx(), NT)
+        k0 = 0.7978845608028654
+
+        def glu(r, unused):
+            at = tile_at(r, 16)
+            gate_v, up, dh = gu_s[at, :CHUNK], gu_s[at, CHUNK:], dh_s[at, :]
+            sq = gate_v * gate_v
+            th = jnp.tanh(gate_v * (k0 + (k0 * 0.044715) * sq))
+            ht = 0.5 + 0.5 * th
+            gl = gate_v * ht
+            dgl = ht + (gate_v * (0.5 - 0.5 * th * th)) * (k0 + (3 * k0 * 0.044715) * sq)
+            hid_s[at, :] = (gl * up).astype(bf16)
+            dgu_s[at, :CHUNK] = (dh * up * dgl).astype(bf16)
+            dgu_s[at, CHUNK:] = (dh * gl).astype(bf16)
+            return unused
+
+        loop_steps(c, 2)
+        lax.fori_loop(0, rows // 16, glu, 0)
+        loop_steps(c, 3)
+        acc_o[...] += dot(hid_s[...], wdx())
+        loop_steps(c, 4)
+        gda_ref[tile_at(c, CHUNK), :] = dot(hid_s[...], did_s[...], TN).astype(bf16)
+        r = dot(igu_s[...], dgu_s[...], TN).astype(bf16)
+        for i in range(2):
+            for j in range(CHUNK // 128):
+                lo = i * CHUNK + j * 128
+                ggb_ref[pl.ds(c * (CHUNK // 128) + (ff // 128) * i + j, 1)] = r[
+                    None, :, lo : lo + 128
+                ]
+
+        @pl.when(c + 1 < nc)
+        def _():
+            arrived_gate(c + 1)
+            for copy in fetch(c + 1, 1 - slot):
+                copy.start()
+
+        acc_a[...] += dot(dgu_s[...], wx(), NT)
+
+        @pl.when(c + 1 < nc)
+        def _():
+            for copy in fetch(c + 1, 1 - slot):
+                copy.wait()
+
+        return unused
+
+    lax.fori_loop(0, nc, chunk, 0)
+    inner_d = (acc_o[:, d:] * mask_ref[...]).astype(bf16)
+    acc_o[:, :d] += dot(inner_d, db_ref[...])
+    r = dot(inner_d, g_ref[...], TN).astype(bf16)
+    for j in range(d // 128):
+        gdb_ref[j] = r[:, j * 128 : (j + 1) * 128]
+    dgu = (acc_a[:, d:] * mask_ref[...]).astype(bf16)
+    gga_ref[...] = dot(a2_s[...], dgu, TN).astype(bf16)
+    acc_a[:, :d] += dot(dgu, ga_ref[...], NT)
+
+    def finish(r, unused):
+        at = tile_at(r, 16)
+        mid = dmid_ref[at, :]
+        out_ref[at, :] = (mid + acc_o[at, :d]).astype(bf16)
+        e = acc_a[at, :d] * gain2_ref[...]
+        rr = lax.rsqrt(jnp.mean(mid * mid, axis=1, keepdims=True) + NORM_EPS)
+        pull = (rr * rr * rr) * jnp.mean(e * mid, axis=1, keepdims=True)
+        dmid_ref[at, :] = g_ref[at, :].astype(f32) + rr * e - pull * mid
+        return unused
+
+    lax.fori_loop(0, rows // 16, finish, 0, unroll=8)
+    for j in range(1, reach + 1):
+        copy, target = low(j)
+        pl.when(target != me)(copy.wait_send)
+        pl.when(me >= j)(high(j).wait_send)
+    for u, unit in enumerate(units):
+        for cl in range(len(unit[2])):
+            for k in range(5):
+                exchange(u, cl, k).wait_send()
+
+    def sent(v, unused):
+        for par in range(2):
+            for cl in range(3):
+                for k in range(5):
+                    gate(2 * v + par, par, cl, k).wait_send()
+        return unused
+
+    lax.fori_loop(0, nu // 2, sent, 0)
+
+
+def forward(count, small, weights):
+    x, g = small[0], small[1]
+    rows, d = x.shape
+    ff = weights[3].shape[0] * count
+    width = rows // 2
+    keys = WINDOW + width
+    span = keys - width + SUB
+    nu = ff // UNIT
+    S = jax.ShapeDtypeStruct
+    full = [S((2,) * 5 + w.shape, bf16) for w in weights]
+    outs = [
+        S((rows, d), bf16),
+        S((rows, d), f32),
+        S((rows, d), bf16),
+        S((rows, d), bf16),
+        S((2, keys, 2 * HD), bf16),
+        S((rows, d), bf16),
+        S((rows, 128), bf16),
+        S((rows, 128), bf16),
+        S((rows, 128), bf16),
+        S((d, 128), bf16),
+        S((2 * ff // 128, 128, 128), bf16),
+        S((ff, 128), bf16),
+        S((d // 128, 128, 128), bf16),
+    ]
+    DMA = pltpu.SemaphoreType.DMA
+    return pl.pallas_call(
+        functools.partial(forward_kernel, count),
+        in_specs=[VMEM] * len(small) + [HBM] * 5,
+        out_specs=[VMEM] * len(outs) + [HBM] * 6,
+        out_shape=outs + [S((2, width // SUB, HEADS * SUB, span), bf16)] + full,
+        scratch_shapes=[pltpu.VMEM(w.shape, bf16) for w in weights]
+        + [
+            pltpu.VMEM((2,) * 6 + (weights[0].shape[0], 2 * CHUNK), bf16),
+            pltpu.VMEM((2, CHUNK, d), bf16),
+            pltpu.VMEM((2, GROUP * SUB, span), bf16),
+            pltpu.VMEM((rows, 2 * HD), bf16),
+            pltpu.VMEM((rows, d), bf16),
+            pltpu.VMEM((rows, 128), bf16),
+            pltpu.VMEM((rows, 128), bf16),
+            pltpu.VMEM((rows, d + 128), f32),
+            pltpu.VMEM((rows, d + 128), f32),
+            pltpu.VMEM((rows, 2 * CHUNK), f32),
+            pltpu.VMEM((rows, CHUNK), f32),
+            pltpu.VMEM((rows, CHUNK), bf16),
+            pltpu.VMEM((rows, 2 * CHUNK), bf16),
+            DMA((2, 2)),
+            DMA((2,)),
+            DMA((2,)),
+            DMA((5,)),
+            DMA((16 + nu, 3, 5)),
+            DMA((16 + nu, 3, 5)),
+            DMA((2, 5)),
+            DMA((2, 5)),
+        ],
+        compiler_params=pltpu.CompilerParams(
+            collective_id=0, has_side_effects=True, vmem_limit_bytes=63 << 20
+        ),
+        name="forward",
+    )(*small, *weights)
+
+
+def att_bwd_kernel(span, q_ref, kv_ref, att_ref, do_ref, p_ref, dq_ref, dkv_ref):
+    s=pl.program_id(1)
+    start=pl.multiple_of(s*SUB,SUB)
+    k=kv_ref[0,pl.ds(start,span),:HD]; v=kv_ref[0,pl.ds(start,span),HD:]
+    @pl.when(s==0)
+    def _(): dkv_ref[...]=jnp.zeros_like(dkv_ref)
+    def body(g,_):
+        at=pl.multiple_of(g*BGROUP*HD,BGROUP*HD)
+        q=heads_down(q_ref[:,pl.ds(at,BGROUP*HD)])
+        do=heads_down(do_ref[:,pl.ds(at,BGROUP*HD)])
+        o=heads_down(att_ref[:,pl.ds(at,BGROUP*HD)])
+        delta=jnp.sum(do.astype(f32)*o.astype(f32),axis=1,keepdims=True)
+        dp=lax.dot_general(do,v,NT,preferred_element_type=f32)
+        p=p_ref[0,0,pl.ds(pl.multiple_of(g*BGROUP*SUB,BGROUP*SUB),BGROUP*SUB),:]
+        ds=(p.astype(f32)*(dp-delta)).astype(bf16)
+        dq=lax.dot_general(ds,k,(((1,),(0,)),((),())),preferred_element_type=f32)*SCALE
+        dq_ref[:,pl.ds(at,BGROUP*HD)]=heads_across(dq).astype(bf16)
+        dk=jnp.dot(q.T,ds,preferred_element_type=f32)*SCALE
+        dv=jnp.dot(do.T,p,preferred_element_type=f32)
+        dkv_ref[0,:HD,pl.ds(start,span)]+=dk
+        dkv_ref[0,HD:,pl.ds(start,span)]+=dv
+        return 0
+    lax.fori_loop(0,HEADS//BGROUP,body,0)
+def att_bwd(q,kv,att,do,p):
+    rows=q.shape[0]; width=rows//2; subs=width//SUB; keys=kv.shape[1]; span=keys-width+SUB
+    rowspec=pl.BlockSpec((SUB,q.shape[1]),lambda w,s:(w*subs+s,0))
+    dsh=(2,2*HD,keys)
+    return pl.pallas_call(functools.partial(att_bwd_kernel,span),grid=(2,subs),
+      in_specs=[rowspec,pl.BlockSpec((1,keys,2*HD),lambda w,s:(w,0,0)),rowspec,rowspec,pl.BlockSpec((1,1,HEADS*SUB,span),lambda w,s:(w,s,0,0))],
+      out_specs=[rowspec,pl.BlockSpec((1,)+dsh[1:],lambda w,s:(w,0,0))],
+      out_shape=[jax.ShapeDtypeStruct(q.shape,bf16),jax.ShapeDtypeStruct(dsh,f32)],
+      compiler_params=pltpu.CompilerParams(vmem_limit_bytes=56<<20),name="att_bwd")(q,kv,att,do,p)
+
+
+def tiles_out(x):
+    return x.reshape(x.shape[0], -1, 128).transpose(1, 0, 2).reshape(-1, 128)
+
+
+def tiles_in(x, rows):
+    return x.reshape(-1, rows, 128).transpose(1, 0, 2).reshape(rows, -1)
+
+
+def pack(grads):
+    parts = [g.astype(bf16) for g in grads]
+    have = sum(g.shape[0] for g in parts)
+    total = -(-have // 512) * 512
+    if total > have:
+        parts.append(jnp.zeros((total - have, 128), bf16))
+    return jnp.concatenate(parts, axis=0).reshape((2,) * 5 + (total // 32, 128))
+
+
+def local_own(
+    tokens,
+    cotangent,
+    doc_lengths,
+    adapter_ids,
+    w_query,
+    w_keyval,
+    w_output,
+    w_gateup,
+    w_down,
+    gain_attn,
+    gain_mlp,
+    query_a,
+    query_b,
+    keyval_a,
+    keyval_b,
+    output_a,
+    output_b,
+    gateup_a,
+    gateup_b,
+    down_a,
+    down_b,
+):
+    count = lax.axis_size("ctx")
+    device = lax.axis_index("ctx")
+    local_rows = tokens.shape[0]
+    width = local_rows // 2
+    reach = (WINDOW + width - 1) // width
+    key_width = w_keyval.shape[1]
+    half_rows = jnp.arange(width, dtype=jnp.int32)
+    own_blocks = (device, 2 * count - 1 - device)
+    positions = jnp.concatenate(
+        [own_blocks[0] * width + half_rows, own_blocks[1] * width + half_rows]
+    )
+    segment, mask = adapter_mask(doc_lengths, adapter_ids, positions)
+    resid = tokens.astype(f32)
+    key_blocks = [[block - reach + step for step in range(reach + 1)] for block in own_blocks]
+    key_pos = jnp.stack(
+        [jnp.concatenate([e * width + half_rows for e in blocks]) for blocks in key_blocks]
+    )
+    key_seg = segment_of(doc_lengths, key_pos.reshape(-1)).reshape(2, 1, -1)
+    (
+        result,
+        grad_middle,
+        act_one,
+        query,
+        keys,
+        attention,
+        inner_query,
+        inner_keyval,
+        inner_output,
+        g_gateup_a,
+        g_gateup_b,
+        g_down_a,
+        g_down_b,
+        prob,
+        full_query,
+        full_keyval,
+        full_output,
+        unused_down,
+        unused_gateup,
+    ) = forward(
+        count,
+        (
+            tokens,
+            cotangent,
+            mask,
+            segment[:, None],
+            key_seg,
+            gain_attn[None, :],
+            gain_mlp[None, :],
+            query_a,
+            query_b,
+            keyval_a,
+            keyval_b,
+            output_a,
+            output_b,
+            gateup_a,
+            gateup_b,
+            down_a,
+            down_b,
+        ),
+        (w_query, w_keyval, w_output, w_down, w_gateup),
+    )
+    full_query, full_keyval, full_output = (
+        w.reshape(-1, w.shape[-1]) for w in (full_query, full_keyval, full_output)
+    )
+    grad_branch = grad_middle.astype(bf16)
+    g_output_a, g_output_b, d_inner_output = adapter_back(
+        grad_branch, attention, inner_output, output_b, mask
+    )
+    grad_attention = (by_cols(grad_branch, full_output) + by_cols(d_inner_output, output_a)).astype(
+        bf16
+    )
+    grad_query, grad_keys = att_bwd(query, keys, attention, grad_attention, prob)
+    grad_keys = grad_keys.transpose(0, 2, 1)
+    first_device = device - reach
+    slots = jnp.zeros((2 * reach + 1, local_rows, key_width), f32)
+    for which in range(2):
+        for step, entry in enumerate(key_blocks[which]):
+            piece = grad_keys[which, step * width : (step + 1) * width]
+            device_of, row_in = owner_of(entry, count, width)
+            at = (device_of - first_device, row_in, jnp.int32(0))
+            current = lax.dynamic_slice(slots, at, (1, width, key_width))
+            slots = lax.dynamic_update_slice(slots, current + piece[None], at)
+    grad_keyval_full = slots[reach]
+    for offset in range(1, reach + 1):
+        from_lower = shifted(slots[reach + offset].astype(bf16), "ctx", offset).astype(f32)
+        from_upper = shifted(slots[reach - offset].astype(bf16), "ctx", -offset).astype(f32)
+        grad_keyval_full = grad_keyval_full + from_lower + from_upper
+    grad_keyval = grad_keyval_full.astype(bf16)
+    g_query_a, g_query_b, d_inner_query = adapter_back(
+        grad_query, act_one, inner_query, query_b, mask
+    )
+    g_keyval_a, g_keyval_b, d_inner_keyval = adapter_back(
+        grad_keyval, act_one, inner_keyval, keyval_b, mask
+    )
+    grad_act_one = (
+        by_cols(grad_query, full_query)
+        + by_cols(grad_keyval, full_keyval)
+        + by_cols(d_inner_query, query_a)
+        + by_cols(d_inner_keyval, keyval_a)
+    )
+    unused, pull_one = jax.vjp(lambda values: rms_scale(values, gain_attn), resid)
+    grad_tokens = (grad_middle + pull_one(grad_act_one)[0]).astype(bf16)
+    parts = [
+        g_query_a,
+        tiles_out(g_query_b),
+        g_keyval_a,
+        tiles_out(g_keyval_b),
+        g_output_a,
+        tiles_out(g_output_b),
+        g_gateup_a,
+        g_gateup_b.reshape(-1, 128),
+        g_down_a,
+        g_down_b.reshape(-1, 128),
+    ]
+    summed = reduce_packed(pack(parts)).reshape(-1, 128)
+    sums = []
+    start = 0
+    for at, part in enumerate(parts):
+        rows = part.shape[0]
+        piece = summed[start : start + rows].astype(f32)
+        sums.append(tiles_in(piece, 128) if at % 2 else piece)
+        start += rows
+    return (result, grad_tokens, *sums)
+
+
 def solution(mesh):
     in_specs = (
         P("ctx", None),
@@ -342,4 +1249,5 @@
         P(),
     )
     out_specs = (P("ctx", None), P("ctx", None), P(), P(), P(), P(), P(), P(), P(), P(), P(), P())
+    local = local_own if mesh.shape["ctx"] == 32 else local_native
     return jax.shard_map(local, mesh=mesh, in_specs=in_specs, out_specs=out_specs, check_vma=False)

time: 933 us -> 510 us (0.55)
  waiting for transfers between devices: 515 us -> 2.9 us
  Pallas kernels: 0 us -> 379 us
  matrix products: 234 us -> 28.5 us
  blocking collectives: 46.3 us -> 0 us
  other arithmetic: 41.2 us -> 19.9 us
  between operations: 15.5 us -> 1.78 us
  starting transfers between devices: 35.2 us -> 24.7 us
    pallas_call x0 -> x3, Pallas kernels: none -> 379 us  [the longest x1 277 us: forward(): pl.pallas_call(functools.partial(forward_kernel, count), in_specs=[VMEM]...]
    all_gather x4 -> x0, waiting for transfers between devices: 265 us -> none  [the longest x1 157 us: local(): lax.all_gather(w_gateup, 'ctx', axis=0, tiled=True)]
    psum x1 -> x0, waiting for transfers between devices: 227 us -> none  [local(): lax.psum((grad_query_a, grad_query_b, grad_keyval_a, grad_keyval_b, grad_...]
    dot_general x27 -> x0, matrix products: 141 us -> none  [the longest x4 34 us: adapted(): jnp.dot(inputs, weight, preferred_element_type=jnp.float32)]
    dot_general x15 -> x9, matrix products: 72.4 us -> 19.2 us  [by_cols(): lax.dot_general(left, right, (((1,), (1,)), ((), ())), preferred_element_...]
    all_gather x1 -> x0, blocking collectives: 46.3 us -> none  [local(): lax.all_gather(w_keyval, 'ctx', axis=0, tiled=True)]
    convert_element_type x6 -> x4, other arithmetic: 24.9 us -> 6.28 us  [the longest x1 1.97 us: local_own(): grad_keyval = grad_keyval_full.astype(bf16)]
    ppermute x16 -> x8, waiting for transfers between devices: 20.4 us -> 2.9 us  [shifted(): return lax.ppermute(x, axis, pairs)]
  transfers between devices with their start and end apart: 21 -> 8, of which waited for: 9 -> 1; matrix products, arithmetic and copies ran while one was open for 12% -> 3% of each run, Pallas kernels for 0% -> 0%
where the time goes in v3:
time: 510 us; the launch traced here: 502 us
  Pallas kernels  379 us (74%)
  local copies, waits for them, and re-layouts  45.2 us (9%)
  matrix products  28.5 us (6%)
  starting transfers between devices  24.7 us (5%)
  other arithmetic  19.9 us (4%)
    pallas_call x1, Pallas kernels, forward(): pl.pallas_call(functools.partial(forward_kernel, count), in_specs=[VMEM]...  277 us
    pallas_call x1, Pallas kernels, reduce_packed(): pl.pallas_call(functools.partial(reduce_kernel, rows), out_shape=jax.Shap...  84.6 us
    ppermute x8, starting transfers between devices, shifted(): return lax.ppermute(x, axis, pairs)  24.7 us
    unnamed x77, local copies, waits for them, and re-layouts  22.6 us
    dot_general x9, matrix products, by_cols(): lax.dot_general(left, right, (((1,), (1,)), ((), ())), preferred_element_...  19.2 us
    pallas_call x1, Pallas kernels, att_bwd(): pl.pallas_call(functools.partial(att_bwd_kernel, span), grid=(2, subs), i...  17.9 us
  transfers between devices with their start and end apart: 8, of which 1 were waited for; matrix products, arithmetic and copies ran while one was open for 3% of the time, Pallas kernels for 0%

profile of v3, /device:TPU:0, one launch (start us, length us, event | category | flops | bytes accessed | tf_op | source)
XLA Modules:
  0.0 502.4 jit_solution(5764484916119334439)
XLA Ops:
  0.8 0.8 reduce-window.9
  1.6 0.7 bitcast_subtract_fusion
  2.5 0.7 select_reduce_fusion
  3.3 0.9 copy.64.qseg_ref
  4.9 1.3 broadcast_in_dim.40.gain1_ref
  6.2 1.3 broadcast_in_dim.41.gain2_ref
  7.5 0.8 compare_convert_fusion.mask_ref
  8.3 277.0 %forward.1 = (bf16[512,1536]{1,0:T(8,128)(2,1)}, f32[512,1536]{1,0:T(8,128)}, bf16[512,1536]{1,0:T(8,128)(2,1)}, bf16[512,1536]{1,0:T(8,128)(2,1)}, bf16[2,1280,...) custom-call(bf16[512,1536]{1,0:T(8,128)(2,1)} %x_ref.1, ...), custom_call_target="tpu_custom_call" | custom-call | tf_op jit(solution)/shard_map/forward/pallas_call | solution.py:992
  285.3 2.6 fusion.10
  288.2 4.6 fusion.33
  292.8 1.7 fusion.5.do_ref
  294.5 17.9 %att_bwd.1 = (bf16[512,1536]{1,0:T(8,128)(2,1)}, f32[2,256,1280]{2,1,0:T(8,128)}) custom-call(bf16[512,1536]{1,0:T(8,128)(2,1)} %get-tuple-element.33.q_ref, bf16[2,1280,256]{2,1,0:T(8,128)(2,1)} %get-tuple-element.34.kv_ref, bf16[512,1536]{1,0:T(8,128)(2,1)} %get-tuple-element.35.att_ref, bf16[512,1536]{1,0:T(8,128)(2,1)} %fusion.5.do_ref, ...), custom_call_target="tpu_custom_call" | custom-call | tf_op jit(solution)/shard_map/att_bwd/pallas_call | solution.py:1055
  312.9 1.1 copy-done.4
  315.1 2.0 copy-done.1
  317.2 1.1 slice_bitcast_fusion.8
  318.3 2.1 collective-permute-start
  320.3 1.3 collective-permute-start.1
  321.6 5.2 %collective-permute-start.2 = (bf16[512,256]{0,1:T(8,128)(2,1)S(1)}, bf16[512,256]{0,1:T(8,128)(2,1)S(1)}, u32[]{:S(2)}, u32[]{:S(2)}) collective-permute-start(bf16[512,256]{0,1:T(8,128)(2,1)S(1)} %get-tuple-element.101), channel_id=1, source_target_pairs={{0,2},{1,3},{2,4},{3,5},{4,6},{5,7},{6,8},{7,9},{8,10},{9,11},{10,... | collective-permute-start | bytes 786440 | tf_op jit(solution)/shard_map/ppermute | solution.py:41
  326.8 1.3 collective-permute-start.3
  328.1 4.1 collective-permute-start.4
  333.3 4.3 fusion.36
  337.6 1.1 convolution_convert_fusion.3
  338.8 1.3 collective-permute-start.5
  340.1 7.9 %collective-permute-start.6 = (bf16[512,256]{0,1:T(8,128)(2,1)}, bf16[512,256]{0,1:T(8,128)(2,1)}, u32[]{:S(2)}, u32[]{:S(2)}) collective-permute-start(bf16[512,256]{0,1:T(8,128)(2,1)} %get-tuple-element.97), channel_id=1, source_target_pairs={{0,4},{1,5},{2,6},{3,7},{4,8},{5,9},{6,10},{7,11},{8,12},{9,13},{1... | collective-permute-start | bytes 786440 | tf_op jit(solution)/shard_map/ppermute | solution.py:41
  348.0 1.5 collective-permute-start.7
  349.6 1.4 fusion.8
  350.9 1.9 copy.65
  352.9 1.9 copy.66
  354.8 0.9 copy.68
  355.7 1.9 copy.69
  357.6 1.8 constant_dynamic-update-slice_fusion.8
  359.5 2.9 collective-permute-done.6
  362.3 2.0 fusion.20
  364.3 0.9 fusion.9
  365.3 0.9 convolution_convert_fusion.5
  366.1 1.5 convert_element_type.188
  367.6 1.0 copy.67
  368.6 2.8 fusion.7
  372.0 2.8 fusion.6
  374.8 0.8 constant_dynamic-update-slice_fusion.6
  375.6 0.8 constant_dynamic-update-slice_fusion.5
  376.4 1.5 constant_dynamic-update-slice_fusion.4
  377.9 1.1 constant_dynamic-update-slice_fusion.3
  379.0 0.8 constant_dynamic-update-slice_fusion.2
  380.4 2.8 copy-done
  383.2 84.6 %shard_map.292 = bf16[2,2,2,2,2,784,128]{6,5,4,3,2,1,0:T(8,128)(2,1)S(1)} custom-call(bf16[2,2,2,2,2,784,128]{6,5,4,3,2,1,0:T(8,128)(2,1)S(1)} %bitcast.120), custom_call_target="tpu_custom_call" | custom-call | tf_op jit(solution)/shard_map/pallas_call | solution.py:403
  468.1 2.0 fusion.35
  470.1 1.6 slice_convert_fusion
  471.6 2.6 copy_bitcast_fusion
  474.3 0.9 convert_bitcast_fusion.3
  475.2 2.3 copy.70
  477.5 2.3 copy.75
  479.8 1.9 convert_bitcast_fusion.2
  481.7 2.3 copy.72
  484.0 2.3 copy.76
  486.3 1.9 convert_bitcast_fusion.1
  488.3 2.3 copy.74
  490.5 2.3 copy.77
  492.8 0.7 copy_bitcast_fusion.1
  493.5 2.8 convolution_add_fusion.3
  496.9 0.8 copy-done.3
  497.8 1.1 fusion.1
  498.9 1.9 fusion.4
  500.8 1.1 copy.113
  (113 shorter events, 5.9 us)
Async XLA Ops:
  8.3 277.0 %copy-start.7 = (bf16[128,1536]{1,0:T(8,128)(2,1)S(1)}, bf16[128,1536]{1,0:T(8,128)(2,1)}, u32[]{:S(2)}) copy-start(bf16[128,1536]{1,0:T(8,128)(2,1)} %ob_ref.1) | copy-start | bytes 1179652
  285.3 2.8 copy-start.2
  288.0 4.8 copy-start.14
  288.1 4.6 copy-start.8
  312.3 1.7 copy-start.4
  314.7 2.4 copy-start.1
  314.8 18.5 %slice-start = ((s8[4718592]{0:T(1024)(128)(4,1)}), s8[4194304]{0:T(1024)(128)(4,1)S(1)}, s32[]{:S(2)}) async-start(s8[4718592]{0:T(1024)(128)(4,1)} %bitcast.149), calls=%async_computation | async-start | bytes 8388608
  317.1 15.1 %copy-start.13 = (bf16[512,1536]{1,0:T(8,128)(2,1)S(1)}, bf16[512,1536]{1,0:T(8,128)(2,1)}, u32[]{:S(2)}) copy-start(bf16[512,1536]{1,0:T(8,128)(2,1)} %get-tuple-element.38) | copy-start | bytes 4718596
  317.2 15.1 %copy-start.18 = (bf16[128,1536]{1,0:T(8,128)(2,1)S(1)}, bf16[128,1536]{1,0:T(8,128)(2,1)}, u32[]{:S(2)}) copy-start(bf16[128,1536]{1,0:T(8,128)(2,1)} %qb_ref.1) | copy-start | bytes 1179652
  317.2 15.7 %copy-start.26 = (bf16[512,128]{1,0:T(8,128)(2,1)S(1)}, bf16[512,128]{1,0:T(8,128)(2,1)}, u32[]{:S(2)}) copy-start(bf16[512,128]{1,0:T(8,128)(2,1)} %get-tuple-element.45) | copy-start | bytes 393220
  317.2 16.1 %slice-start.1 = ((s8[4718592]{0:T(1024)(128)(4,1)}), s8[524288]{0:T(1024)(128)(4,1)S(1)}, s32[]{:S(2)}) async-start(s8[4718592]{0:T(1024)(128)(4,1)} %bitcast.149), calls=%async_computation.1 | async-start | bytes 1048576
  318.3 20.5 %collective-permute-start = (bf16[512,256]{0,1:T(8,128)(2,1)S(1)}, bf16[512,256]{0,1:T(8,128)(2,1)S(1)}, u32[]{:S(2)}, u32[]{:S(2)}) collective-permute-start(bf16[512,256]{0,1:T(8,128)(2,1)S(1)} %get-tuple-element.95), channel_id=1, source_target_pairs={{0,1},{1,2},{2,3},{3,4},{4,5},{5,6},{6,7},{7,8},{8,9},{9,10},{10,1... | collective-permute-start | bytes 786440 | tf_op jit(solution)/shard_map/ppermute | solution.py:41
  320.3 19.7 %collective-permute-start.1 = (bf16[512,256]{0,1:T(8,128)(2,1)S(1)}, bf16[512,256]{0,1:T(8,128)(2,1)S(1)}, u32[]{:S(2)}, u32[]{:S(2)}) collective-permute-start(bf16[512,256]{0,1:T(8,128)(2,1)S(1)} %get-tuple-element.102), channel_id=1, source_target_pairs={{1,0},{2,1},{3,2},{4,3},{5,4},{6,5},{7,6},{8,7},{9,8},{10,9},{11,1... | collective-permute-start | bytes 786440 | tf_op jit(solution)/shard_map/ppermute | solution.py:41
  321.6 26.4 %collective-permute-start.2 = (bf16[512,256]{0,1:T(8,128)(2,1)S(1)}, bf16[512,256]{0,1:T(8,128)(2,1)S(1)}, u32[]{:S(2)}, u32[]{:S(2)}) collective-permute-start(bf16[512,256]{0,1:T(8,128)(2,1)S(1)} %get-tuple-element.101), channel_id=1, source_target_pairs={{0,2},{1,3},{2,4},{3,5},{4,6},{5,7},{6,8},{7,9},{8,10},{9,11},{10,... | collective-permute-start | bytes 786440 | tf_op jit(solution)/shard_map/ppermute | solution.py:41
  326.8 32.6 %collective-permute-start.3 = (bf16[512,256]{0,1:T(8,128)(2,1)}, bf16[512,256]{0,1:T(8,128)(2,1)}, u32[]{:S(2)}, u32[]{:S(2)}) collective-permute-start(bf16[512,256]{0,1:T(8,128)(2,1)} %get-tuple-element.100), channel_id=1, source_target_pairs={{2,0},{3,1},{4,2},{5,3},{6,4},{7,5},{8,6},{9,7},{10,8},{11,9},{12,... | collective-permute-start | bytes 786440 | tf_op jit(solution)/shard_map/ppermute | solution.py:41
  328.1 31.3 %collective-permute-start.4 = (bf16[512,256]{0,1:T(8,128)(2,1)}, bf16[512,256]{0,1:T(8,128)(2,1)}, u32[]{:S(2)}, u32[]{:S(2)}) collective-permute-start(bf16[512,256]{0,1:T(8,128)(2,1)} %get-tuple-element.99), channel_id=1, source_target_pairs={{0,3},{1,4},{2,5},{3,6},{4,7},{5,8},{6,9},{7,10},{8,11},{9,12},{10... | collective-permute-start | bytes 786440 | tf_op jit(solution)/shard_map/ppermute | solution.py:41
  332.8 16.8 %copy-start.27 = (bf16[512,128]{1,0:T(8,128)(2,1)}, bf16[512,128]{1,0:T(8,128)(2,1)S(1)}, u32[]{:S(2)}) copy-start(bf16[512,128]{1,0:T(8,128)(2,1)S(1)} %fusion.11) | copy-start | bytes 393220
  333.3 4.3 copy-start.25
  333.3 16.3 %copy-start.12 = (bf16[512,1536]{1,0:T(8,128)(2,1)S(1)}, bf16[512,1536]{1,0:T(8,128)(2,1)}, u32[]{:S(2)}) copy-start(bf16[512,1536]{1,0:T(8,128)(2,1)} %get-tuple-element.42) | copy-start | bytes 4718596
  338.8 9.2 %copy-start.21 = (bf16[512,256]{0,1:T(8,128)(2,1)}, bf16[512,256]{0,1:T(8,128)(2,1)S(1)}, u32[]{:S(2)}) copy-start(bf16[512,256]{0,1:T(8,128)(2,1)S(1)} %collective-permute-done) | copy-start | bytes 786436
  338.8 20.7 %collective-permute-start.5 = (bf16[512,256]{0,1:T(8,128)(2,1)}, bf16[512,256]{0,1:T(8,128)(2,1)}, u32[]{:S(2)}, u32[]{:S(2)}) collective-permute-start(bf16[512,256]{0,1:T(8,128)(2,1)} %get-tuple-element.98), channel_id=1, source_target_pairs={{3,0},{4,1},{5,2},{6,3},{7,4},{8,5},{9,6},{10,7},{11,8},{12,9},{13... | collective-permute-start | bytes 786440 | tf_op jit(solution)/shard_map/ppermute | solution.py:41
  340.1 7.9 %copy-start.22 = (bf16[512,256]{0,1:T(8,128)(2,1)}, bf16[512,256]{0,1:T(8,128)(2,1)S(1)}, u32[]{:S(2)}) copy-start(bf16[512,256]{0,1:T(8,128)(2,1)S(1)} %collective-permute-done.1) | copy-start | bytes 786436
  340.1 22.2 %collective-permute-start.6 = (bf16[512,256]{0,1:T(8,128)(2,1)}, bf16[512,256]{0,1:T(8,128)(2,1)}, u32[]{:S(2)}, u32[]{:S(2)}) collective-permute-start(bf16[512,256]{0,1:T(8,128)(2,1)} %get-tuple-element.97), channel_id=1, source_target_pairs={{0,4},{1,5},{2,6},{3,7},{4,8},{5,9},{6,10},{7,11},{8,12},{9,13},{1... | collective-permute-start | bytes 786440 | tf_op jit(solution)/shard_map/ppermute | solution.py:41
  348.0 1.6 copy-start.23
  348.0 14.3 %collective-permute-start.7 = (bf16[512,256]{0,1:T(8,128)(2,1)}, bf16[512,256]{0,1:T(8,128)(2,1)}, u32[]{:S(2)}, u32[]{:S(2)}) collective-permute-start(bf16[512,256]{0,1:T(8,128)(2,1)} %get-tuple-element.96), channel_id=1, source_target_pairs={{4,0},{5,1},{6,2},{7,3},{8,4},{9,5},{10,6},{11,7},{12,8},{13,9},{1... | collective-permute-start | bytes 786440 | tf_op jit(solution)/shard_map/ppermute | solution.py:41
  357.6 6.7 %copy-start.29 = (bf16[128,256]{1,0:T(8,128)(2,1)S(1)}, bf16[128,256]{1,0:T(8,128)(2,1)}, u32[]{:S(2)}) copy-start(bf16[128,256]{1,0:T(8,128)(2,1)} %kb_ref.1) | copy-start | bytes 196612
  357.6 7.6 %copy-start.24 = (bf16[512,128]{1,0:T(8,128)(2,1)S(1)}, bf16[512,128]{1,0:T(8,128)(2,1)}, u32[]{:S(2)}) copy-start(bf16[512,128]{1,0:T(8,128)(2,1)} %get-tuple-element.44) | copy-start | bytes 393220
  359.4 12.6 %copy-start.15 = (bf16[512,128]{1,0:T(8,128)(2,1)S(1)}, bf16[512,128]{1,0:T(8,128)(2,1)}, u32[]{:S(2)}) copy-start(bf16[512,128]{1,0:T(8,128)(2,1)} %copy-done.14) | copy-start | bytes 393220
  367.6 7.2 %copy-start.11 = (bf16[12,128,128]{2,1,0:T(8,128)(2,1)S(1)}, bf16[12,128,128]{2,1,0:T(8,128)(2,1)}, u32[]{:S(2)}) copy-start(bf16[12,128,128]{2,1,0:T(8,128)(2,1)} %copy.69) | copy-start | bytes 1179652
  367.6 8.0 %copy-start.20 = (bf16[1536,128]{1,0:T(8,128)(2,1)S(1)}, bf16[1536,128]{1,0:T(8,128)(2,1)}, u32[]{:S(2)}) copy-start(bf16[1536,128]{1,0:T(8,128)(2,1)} %get-tuple-element.46) | copy-start | bytes 1179652
  367.6 8.8 %copy-start.5 = (bf16[72,128,128]{2,1,0:T(8,128)(2,1)S(1)}, bf16[72,128,128]{2,1,0:T(8,128)(2,1)}, u32[]{:S(2)}) copy-start(bf16[72,128,128]{2,1,0:T(8,128)(2,1)} %get-tuple-element.47) | copy-start | bytes 7077892
  374.8 3.0 copy-start.16
  376.4 2.6 copy-start.19
  380.4 2.8 copy-start
  493.5 2.8 copy-start.9
  493.5 2.8 copy-start.28
  496.3 1.4 copy-start.3
  496.3 1.5 copy-start.6
  496.3 1.5 copy-start.17
  496.4 1.5 copy-start.30
  498.9 1.9 copy-start.10

commit v4 on v3

--- a/solution.py
+++ b/solution.py
@@ -339,75 +339,6 @@
 
 def flip(me, bits, b):
     return (me+(1-2*bits[b])*(1<<b),)
-def reduce_kernel(rows, in_ref, out_ref, r0, r1, r2, r3, r4, ssem, rsem):
-    rb=(r0,r1,r2,r3,r4)
-    me=lax.axis_index("ctx")
-    bits=[(me//(1<<b))%2 for b in range(5)]
-    bar=pltpu.get_barrier_semaphore()
-    for b in range(5):
-        pl.semaphore_signal(bar,1,device_id=flip(me,bits,b),device_id_type=MESH)
-    pl.semaphore_wait(bar,5)
-    t=rows//16
-    a=round(t*3/7); bb=round(t*3/14)
-    classes=[(0,a*16,ORD_A),(a*16,bb*16,ORD_B),((a+bb)*16,rows-(a+bb)*16,ORD_C)]
-    def rs(cl,s):
-        r0_,n,order=classes[cl]
-        red=order[::-1]
-        bit=red[s]; done=red[:s]
-        rem=[b for b in (4,3,2,1,0) if b not in done]
-        src=in_ref if s==0 else rb[s-1]
-        idx=tuple((1-bits[b]) if b==bit else slice(None) for b in rem)
-        return pltpu.make_async_remote_copy(src.at[idx+(pl.ds(r0_,n),)],rb[s].at[(slice(None),)*(4-s)+(pl.ds(r0_,n),)],ssem.at[cl,s],rsem.at[cl,s],device_id=flip(me,bits,bit),device_id_type=MESH)
-    def add(cl,s):
-        r0_,n,order=classes[cl]
-        red=order[::-1]
-        bit=red[s]; done=red[:s]
-        rem=[b for b in (4,3,2,1,0) if b not in done]
-        src=in_ref if s==0 else rb[s-1]
-        rs_=pl.ds(r0_,n)
-        nd=4-s
-        def body(j,_):
-            ds=[(j//(1<<(nd-1-i)))%2 for i in range(nd)]
-            it=iter(ds)
-            si=tuple(bits[b] if b==bit else next(it) for b in rem)
-            v=src[si+(rs_,)].astype(f32)+rb[s][tuple(ds)+(rs_,)].astype(f32)
-            rb[s][tuple(ds)+(rs_,)]=v.astype(bf16)
-            return 0
-        lax.fori_loop(0,1<<nd,body,0)
-    def ag(cl,k):
-        r0_,n,order=classes[cl]
-        bit=order[k]; have=order[:k]
-        idx=tuple(slice(None) if b in have else bits[b] for b in (4,3,2,1,0))+(pl.ds(r0_,n),)
-        src=out_ref.at[idx] if k else rb[4].at[pl.ds(r0_,n)]
-        return pltpu.make_async_remote_copy(src,out_ref.at[idx],ssem.at[cl,5+k],rsem.at[cl,5+k],device_id=flip(me,bits,bit),device_id_type=MESH)
-    for cl in range(3): rs(cl,0).start()
-    for s in range(5):
-        for cl in range(3):
-            rs(cl,s).wait_recv()
-            add(cl,s)
-            if s<4: rs(cl,s+1).start()
-            else:
-                ag(cl,0).start()
-                r0_,n,_=classes[cl]
-                out_ref[bits[4],bits[3],bits[2],bits[1],bits[0],pl.ds(r0_,n)]=rb[4][pl.ds(r0_,n)]
-    for k in range(1,5):
-        for cl in range(3):
-            ag(cl,k-1).wait_recv()
-            ag(cl,k).start()
-    for cl in range(3): ag(cl,4).wait_recv()
-    for cl in range(3):
-        for s in range(5):
-            rs(cl,s).wait_send(); ag(cl,s).wait_send()
-def reduce_packed(x, cid=1):
-    rows=x.shape[5]
-    return pl.pallas_call(functools.partial(reduce_kernel,rows),
-        out_shape=jax.ShapeDtypeStruct(x.shape,x.dtype),
-        in_specs=[pl.BlockSpec(memory_space=pltpu.VMEM)],out_specs=pl.BlockSpec(memory_space=pltpu.VMEM),
-        scratch_shapes=[pltpu.VMEM((2,)*(4-s)+(rows,128),bf16) for s in range(5)]+[pltpu.SemaphoreType.DMA((3,10)),pltpu.SemaphoreType.DMA((3,10))],
-        compiler_params=pltpu.CompilerParams(collective_id=cid,has_side_effects=True,vmem_limit_bytes=40<<20))(x)
-
-
-BGROUP = 6
 CHUNK = 512
 UNIT = 256
 SUB = 128
@@ -1025,55 +956,433 @@
     )(*small, *weights)
 
 
-def att_bwd_kernel(span, q_ref, kv_ref, att_ref, do_ref, p_ref, dq_ref, dkv_ref):
-    s=pl.program_id(1)
-    start=pl.multiple_of(s*SUB,SUB)
-    k=kv_ref[0,pl.ds(start,span),:HD]; v=kv_ref[0,pl.ds(start,span),HD:]
-    @pl.when(s==0)
-    def _(): dkv_ref[...]=jnp.zeros_like(dkv_ref)
-    def body(g,_):
-        at=pl.multiple_of(g*BGROUP*HD,BGROUP*HD)
-        q=heads_down(q_ref[:,pl.ds(at,BGROUP*HD)])
-        do=heads_down(do_ref[:,pl.ds(at,BGROUP*HD)])
-        o=heads_down(att_ref[:,pl.ds(at,BGROUP*HD)])
-        delta=jnp.sum(do.astype(f32)*o.astype(f32),axis=1,keepdims=True)
-        dp=lax.dot_general(do,v,NT,preferred_element_type=f32)
-        p=p_ref[0,0,pl.ds(pl.multiple_of(g*BGROUP*SUB,BGROUP*SUB),BGROUP*SUB),:]
-        ds=(p.astype(f32)*(dp-delta)).astype(bf16)
-        dq=lax.dot_general(ds,k,(((1,),(0,)),((),())),preferred_element_type=f32)*SCALE
-        dq_ref[:,pl.ds(at,BGROUP*HD)]=heads_across(dq).astype(bf16)
-        dk=jnp.dot(q.T,ds,preferred_element_type=f32)*SCALE
-        dv=jnp.dot(do.T,p,preferred_element_type=f32)
-        dkv_ref[0,:HD,pl.ds(start,span)]+=dk
-        dkv_ref[0,HD:,pl.ds(start,span)]+=dv
-        return 0
-    lax.fori_loop(0,HEADS//BGROUP,body,0)
-def att_bwd(q,kv,att,do,p):
-    rows=q.shape[0]; width=rows//2; subs=width//SUB; keys=kv.shape[1]; span=keys-width+SUB
-    rowspec=pl.BlockSpec((SUB,q.shape[1]),lambda w,s:(w*subs+s,0))
-    dsh=(2,2*HD,keys)
-    return pl.pallas_call(functools.partial(att_bwd_kernel,span),grid=(2,subs),
-      in_specs=[rowspec,pl.BlockSpec((1,keys,2*HD),lambda w,s:(w,0,0)),rowspec,rowspec,pl.BlockSpec((1,1,HEADS*SUB,span),lambda w,s:(w,s,0,0))],
-      out_specs=[rowspec,pl.BlockSpec((1,)+dsh[1:],lambda w,s:(w,0,0))],
-      out_shape=[jax.ShapeDtypeStruct(q.shape,bf16),jax.ShapeDtypeStruct(dsh,f32)],
-      compiler_params=pltpu.CompilerParams(vmem_limit_bytes=56<<20),name="att_bwd")(q,kv,att,do,p)
-
-
-def tiles_out(x):
-    return x.reshape(x.shape[0], -1, 128).transpose(1, 0, 2).reshape(-1, 128)
-
-
-def tiles_in(x, rows):
-    return x.reshape(-1, rows, 128).transpose(1, 0, 2).reshape(rows, -1)
-
-
-def pack(grads):
-    parts = [g.astype(bf16) for g in grads]
-    have = sum(g.shape[0] for g in parts)
-    total = -(-have // 512) * 512
-    if total > have:
-        parts.append(jnp.zeros((total - have, 128), bf16))
-    return jnp.concatenate(parts, axis=0).reshape((2,) * 5 + (total // 32, 128))
+class Sum:
+    def __init__(self, me, buf, parts, send, recv):
+        self.me, self.bits = me, bits_of(me)
+        self.buf, self.parts, self.send, self.recv = buf, parts, send, recv
+        tiles = buf.shape[5] // 16
+        a, b = round(tiles * 3 / 7), round(tiles * 3 / 14)
+        self.split = (
+            (0, a * 16, ORD_A),
+            (a * 16, b * 16, ORD_B),
+            ((a + b) * 16, (tiles - a - b) * 16, ORD_C),
+        )
+        self.queue = [(s, cl) for s in range(1, 11) for cl in range(3)]
+
+    def copy(self, cl, s):
+        row, n, order = self.split[cl]
+        lines = pl.ds(row, n)
+        bits = self.bits
+        if s < 5:
+            red = order[::-1]
+            bit = red[s]
+            rem = [b for b in (4, 3, 2, 1, 0) if b not in red[:s]]
+            src = self.buf if s == 0 else self.parts[s - 1]
+            idx = tuple((1 - bits[b]) if b == bit else pl.ds(0, 2) for b in rem)
+            src = src.at[idx + (lines,)]
+            dst = self.parts[s].at[(pl.ds(0, 2),) * (4 - s) + (lines,)]
+        else:
+            bit, have = order[s - 5], order[: s - 5]
+            idx = tuple(pl.ds(0, 2) if b in have else bits[b] for b in (4, 3, 2, 1, 0))
+            src = dst = self.buf.at[idx + (lines,)]
+        return pltpu.make_async_remote_copy(
+            src,
+            dst,
+            self.send.at[cl, s],
+            self.recv.at[cl, s],
+            device_id=flip(self.me, bits, bit),
+            device_id_type=MESH,
+        )
+
+    def add(self, cl, s):
+        row, n, order = self.split[cl]
+        red = order[::-1]
+        rem = [b for b in (4, 3, 2, 1, 0) if b not in red[:s]]
+        src, dst = (self.buf if s == 0 else self.parts[s - 1]), self.parts[s]
+        lines = pl.ds(row, n)
+        free = 4 - s
+
+        def one(j, unused):
+            at = [(j // (1 << (free - 1 - i))) % 2 for i in range(free)]
+            rest = iter(at)
+            idx = tuple(self.bits[b] if b == red[s] else next(rest) for b in rem)
+            total = src[idx + (lines,)].astype(f32) + dst[tuple(at) + (lines,)].astype(f32)
+            dst[tuple(at) + (lines,)] = total.astype(bf16)
+            return unused
+
+        lax.fori_loop(0, 1 << free, one, 0)
+
+    def begin(self):
+        for cl in range(3):
+            self.copy(cl, 0).start()
+
+    def advance(self, n=1):
+        for unused in range(n):
+            if not self.queue:
+                return
+            s, cl = self.queue.pop(0)
+            before = self.copy(cl, s - 1)
+            before.wait_recv()
+            before.wait_send()
+            if s <= 5:
+                self.add(cl, s - 1)
+            if s == 5:
+                row, n_, unused_order = self.split[cl]
+                b = self.bits
+                self.buf[b[4], b[3], b[2], b[1], b[0], pl.ds(row, n_)] = self.parts[4][
+                    pl.ds(row, n_)
+                ]
+            if s < 10:
+                self.copy(cl, s).start()
+
+
+def backward_kernel(
+    count,
+    dmid_ref,
+    x_ref,
+    mask_ref,
+    gain_ref,
+    a1_ref,
+    q_ref,
+    keys_ref,
+    att_ref,
+    iq_ref,
+    ik_ref,
+    io_ref,
+    qa_ref,
+    qb_ref,
+    ka_ref,
+    kb_ref,
+    oa_ref,
+    ob_ref,
+    gga_hbm,
+    ggb_hbm,
+    gda_hbm,
+    gdb_hbm,
+    prob_hbm,
+    wq_all,
+    wk_all,
+    wo_all,
+    dx_ref,
+    oqa_ref,
+    oqb_ref,
+    oka_ref,
+    okb_ref,
+    ooa_ref,
+    oob_ref,
+    oga_ref,
+    ogb_ref,
+    oda_ref,
+    odb_ref,
+    one,
+    two,
+    pa0,
+    pa1,
+    pa2,
+    pa3,
+    pa4,
+    pb0,
+    pb1,
+    pb2,
+    pb3,
+    pb4,
+    wbuf,
+    pbuf,
+    grad_s,
+    small_s,
+    dkv_s,
+    acc,
+    hout,
+    hin,
+    wsem,
+    psem,
+    gsem,
+    send1,
+    recv1,
+    send2,
+    recv2,
+    hsend,
+    hrecv,
+):
+    rows, d = x_ref.shape
+    width = rows // 2
+    reach = WINDOW // width
+    keys = keys_ref.shape[1]
+    span = keys - width + SUB
+    me = lax.axis_index("ctx")
+    bits = bits_of(me)
+    meet_all(count, me)
+    flat_one = one.reshape(-1, 128)
+    flat_two = two.reshape(-1, 128)
+    hid_rows = gda_hbm.shape[0]
+    gates = ggb_hbm.shape[0] * 128
+    at_ggb = d
+    at_gda = at_ggb + gates
+    at_gdb = at_gda + hid_rows
+    at_goa = at_gdb + d
+    at_gob = at_goa + d
+    at_qb, at_ka, at_kb = d, 2 * d, 3 * d
+
+    def whole(ref):
+        return ref.at[(slice(None),) * 7]
+
+    loads = [
+        pltpu.make_async_copy(wo_all, wbuf.at[(slice(None),) * 6 + (pl.ds(0, d),)], wsem.at[0])
+    ]
+    grads = [
+        pltpu.make_async_copy(src.reshape(-1, 128), flat_one.at[pl.ds(at, n)], gsem.at[i])
+        for i, (src, at, n) in enumerate(
+            (
+                (gga_hbm, 0, d),
+                (ggb_hbm, at_ggb, gates),
+                (gda_hbm, at_gda, hid_rows),
+                (gdb_hbm, at_gdb, d),
+            )
+        )
+    ]
+    groups = HEADS // GROUP
+    subs = width // SUB
+    turns = [(w, s, g) for w in range(2) for s in range(subs) for g in range(groups)]
+
+    def prob(n):
+        w, s, g = turns[n]
+        return pltpu.make_async_copy(
+            prob_hbm.at[w, s, pl.ds(g * GROUP * SUB, GROUP * SUB)], pbuf.at[n % 2], psem.at[n % 2]
+        )
+
+    for copy in loads + grads + [prob(0), prob(1)]:
+        copy.start()
+
+    def beside(*xs):
+        return jnp.concatenate(xs, axis=1)
+
+    def weight(lo, n):
+        return wbuf[:, :, :, :, :, :, lo : lo + n].reshape(-1, n)
+
+    def store_tiles(flat, at, x):
+        for j in range(x.shape[1] // 128):
+            flat[pl.ds(at + j * 128, 128)] = x[:, j * 128 : (j + 1) * 128].astype(bf16)
+
+    grad_s[...] = dmid_ref[...].astype(bf16)
+    small_s[:, :128] = (dot(grad_s[...], ob_ref[...], NT) * mask_ref[...]).astype(bf16)
+    flat_one[pl.ds(at_goa, d)] = dot(att_ref[...], small_s[:, :128], TN).astype(bf16)
+    store_tiles(flat_one, at_gob, dot(io_ref[...], grad_s[...], TN))
+    for copy in grads:
+        copy.wait()
+    first = Sum(me, one, (pa0, pa1, pa2, pa3, pa4), send1, recv1)
+    second = Sum(me, two, (pb0, pb1, pb2, pb3, pb4), send2, recv2)
+    first.begin()
+    for copy in loads:
+        copy.wait()
+    acc[:, :d] = dot(
+        beside(grad_s[...], small_s[:, :128]), beside(weight(0, d), oa_ref[...]), NT
+    )
+    grad_s[...] = acc[:, :d].astype(bf16)
+    loads = [
+        pltpu.make_async_copy(wq_all, wbuf.at[(slice(None),) * 6 + (pl.ds(0, d),)], wsem.at[0]),
+        pltpu.make_async_copy(
+            wk_all, wbuf.at[(slice(None),) * 6 + (pl.ds(d, 2 * HD),)], wsem.at[1]
+        ),
+    ]
+    for copy in loads:
+        copy.start()
+    dkv_s[...] = jnp.zeros_like(dkv_s)
+    first.advance(1)
+
+    for n, (which, s, g) in enumerate(turns):
+        base = s * SUB
+        lines = slice(which * width + base, which * width + base + SUB)
+        heads = slice(g * GROUP * HD, (g + 1) * GROUP * HD)
+        k = keys_ref[which, base : base + span, :HD]
+        v = keys_ref[which, base : base + span, HD:]
+        q = heads_down(q_ref[lines, heads])
+        do = heads_down(grad_s[lines, heads])
+        o = heads_down(att_ref[lines, heads])
+        delta = jnp.sum(do.astype(f32) * o.astype(f32), axis=1, keepdims=True)
+        prob(n).wait()
+        p = pbuf[n % 2]
+        ds = (p.astype(f32) * (dot(do, v, NT) - delta)).astype(bf16)
+        dkv_s[which, HD:, base : base + span] += dot(do.T, p)
+        dkv_s[which, :HD, base : base + span] += dot(q.T, ds) * SCALE
+        grad_s[lines, heads] = heads_across(dot(ds, k) * SCALE).astype(bf16)
+        if n + 2 < len(turns):
+            prob(n + 2).start()
+        first.advance(1)
+
+    def piece(which, j):
+        lo = (reach - j) * width
+        return dkv_s[which, :, lo : lo + width].T
+
+    for j in range(1, reach + 1):
+        for which in range(2):
+            hout[which, j - 1] = piece(which, j).astype(bf16)
+
+    def low(j):
+        return pltpu.make_async_remote_copy(
+            hout.at[0, j - 1],
+            hin.at[0, j - 1],
+            hsend.at[0, j],
+            hrecv.at[0, j],
+            device_id=(me - j,),
+            device_id_type=MESH,
+        )
+
+    def high(j):
+        block = 2 * count - 1 - me - j
+        upper = block // count
+        target = block + upper * (2 * count - 1 - 2 * block)
+        copy = pltpu.make_async_remote_copy(
+            hout.at[1, j - 1],
+            hin.at[upper, j - 1],
+            hsend.at[1, j],
+            hrecv.at[upper, j],
+            device_id=(target,),
+            device_id_type=MESH,
+        )
+        return copy, target
+
+    def incoming(half, j):
+        return pltpu.make_async_remote_copy(
+            hout.at[0, j - 1],
+            hin.at[half, j - 1],
+            hsend.at[0, j],
+            hrecv.at[half, j],
+            device_id=flip(me, bits, 0),
+            device_id_type=MESH,
+        )
+
+    for j in range(1, reach + 1):
+        pl.when(me >= j)(low(j).start)
+        copy, target = high(j)
+        pl.when(target != me)(copy.start)
+    first.advance(1)
+    small_s[:, :128] = (dot(grad_s[...], qb_ref[...], NT) * mask_ref[...]).astype(bf16)
+    flat_two[pl.ds(0, d)] = dot(a1_ref[...], small_s[:, :128], TN).astype(bf16)
+    store_tiles(flat_two, at_qb, dot(iq_ref[...], grad_s[...], TN))
+    used = 3 * d + 2 * HD
+    spare = flat_two.shape[0] - used
+    flat_two[pl.ds(used, spare)] = jnp.zeros((spare, 128), bf16)
+    first.advance(2)
+    for half in range(2):
+        own = dkv_s[half, :, reach * width :].T
+        acc[half * width : (half + 1) * width, : 2 * HD] = own
+    for j in range(1, reach + 1):
+        lower_self = 2 * me == 2 * count - 1 - j
+
+        @pl.when(jnp.logical_not(lower_self))
+        def _(j=j):
+            incoming(0, j).wait_recv()
+            acc[:width, : 2 * HD] += hin[0, j - 1].astype(f32)
+
+        @pl.when(lower_self)
+        def _(j=j):
+            acc[:width, : 2 * HD] += hout[1, j - 1].astype(f32)
+
+        @pl.when(me >= j)
+        def _(j=j):
+            incoming(1, j).wait_recv()
+            acc[width:, : 2 * HD] += hin[1, j - 1].astype(f32)
+
+    small_s[:, 128 : 128 + 2 * HD] = acc[:, : 2 * HD].astype(bf16)
+    dkv = small_s[:, 128 : 128 + 2 * HD]
+    small_s[:, 128 + 2 * HD :] = (dot(dkv, kb_ref[...], NT) * mask_ref[...]).astype(bf16)
+    flat_two[pl.ds(at_ka, d)] = dot(a1_ref[...], small_s[:, 128 + 2 * HD :], TN).astype(bf16)
+    store_tiles(flat_two, at_kb, dot(ik_ref[...], small_s[:, 128 : 128 + 2 * HD], TN))
+    second.begin()
+    first.advance(3)
+    for copy in loads:
+        copy.wait()
+    acc[:, :d] = dot(
+        beside(grad_s[...], small_s[...]),
+        beside(weight(0, d), qa_ref[...], weight(d, 2 * HD), ka_ref[...]),
+        NT,
+    )
+    first.advance(3)
+    second.advance(3)
+
+    def finish(r, unused):
+        at = tile_at(r, 16)
+        x = x_ref[at, :].astype(f32)
+        e = acc[at, :d] * gain_ref[...]
+        rr = lax.rsqrt(jnp.mean(x * x, axis=1, keepdims=True) + NORM_EPS)
+        pull = (rr * rr * rr) * jnp.mean(e * x, axis=1, keepdims=True)
+        dx_ref[at, :] = (dmid_ref[at, :] + rr * e - pull * x).astype(bf16)
+        return unused
+
+    lax.fori_loop(0, rows // 16, finish, 0, unroll=8)
+    while first.queue or second.queue:
+        second.advance(3)
+        first.advance(3)
+
+    def take(out, flat, at, tiles):
+        if tiles:
+            for j in range(out.shape[1] // 128):
+                out[:, j * 128 : (j + 1) * 128] = flat[pl.ds(at + j * 128, 128)].astype(f32)
+        else:
+            out[...] = flat[pl.ds(at, out.shape[0])].astype(f32)
+
+    take(oga_ref, flat_one, 0, False)
+    take(ogb_ref, flat_one, at_ggb, True)
+    take(oda_ref, flat_one, at_gda, False)
+    take(odb_ref, flat_one, at_gdb, True)
+    take(ooa_ref, flat_one, at_goa, False)
+    take(oob_ref, flat_one, at_gob, True)
+    take(oqa_ref, flat_two, 0, False)
+    take(oqb_ref, flat_two, at_qb, True)
+    take(oka_ref, flat_two, at_ka, False)
+    take(okb_ref, flat_two, at_kb, True)
+    for j in range(1, reach + 1):
+        pl.when(me >= j)(low(j).wait_send)
+        copy, target = high(j)
+        pl.when(target != me)(copy.wait_send)
+
+
+def backward(count, small, large):
+    rows, d = small[0].shape
+    gates, hid = large[1].shape[0] * 128, large[2].shape[0]
+    keys = small[6].shape[1]
+    span = keys - rows // 2 + SUB
+    one = (2 * d + gates + hid + 2 * d) // 32
+    two = -(-(3 * d + 2 * HD) // 512) * 16
+    S = jax.ShapeDtypeStruct
+    V = pltpu.VMEM
+    DMA = pltpu.SemaphoreType.DMA
+    five = (2,) * 5
+    outs = [S((rows, d), bf16)]
+    for a, b in ((d, d), (d, 2 * HD), (d, d), (d, gates), (hid, d)):
+        outs += [S((a, 128), f32), S((128, b), f32)]
+    return pl.pallas_call(
+        functools.partial(backward_kernel, count),
+        in_specs=[VMEM] * len(small) + [HBM] * len(large),
+        out_specs=[VMEM] * len(outs),
+        out_shape=outs,
+        scratch_shapes=[V(five + (one, 128), bf16), V(five + (two, 128), bf16)]
+        + [V((2,) * (4 - s) + (one, 128), bf16) for s in range(5)]
+        + [V((2,) * (4 - s) + (two, 128), bf16) for s in range(5)]
+        + [
+            V(five + (d // 32, d + 2 * HD), bf16),
+            V((2, GROUP * SUB, span), bf16),
+            V((rows, d), bf16),
+            V((rows, 256 + 2 * HD), bf16),
+            V((2, 2 * HD, keys), f32),
+            V((rows, d), f32),
+            V((2, 4, rows // 2, 2 * HD), bf16),
+            V((2, 4, rows // 2, 2 * HD), bf16),
+            DMA((2,)),
+            DMA((2,)),
+            DMA((4,)),
+            DMA((3, 10)),
+            DMA((3, 10)),
+            DMA((3, 10)),
+            DMA((3, 10)),
+            DMA((2, 5)),
+            DMA((2, 5)),
+        ],
+        compiler_params=pltpu.CompilerParams(
+            collective_id=1, has_side_effects=True, vmem_limit_bytes=63 << 20
+        ),
+        name="backward",
+    )(*small, *large)
 
 
 def local_own(
@@ -1104,14 +1413,12 @@
     local_rows = tokens.shape[0]
     width = local_rows // 2
     reach = (WINDOW + width - 1) // width
-    key_width = w_keyval.shape[1]
     half_rows = jnp.arange(width, dtype=jnp.int32)
     own_blocks = (device, 2 * count - 1 - device)
     positions = jnp.concatenate(
         [own_blocks[0] * width + half_rows, own_blocks[1] * width + half_rows]
     )
     segment, mask = adapter_mask(doc_lengths, adapter_ids, positions)
-    resid = tokens.astype(f32)
     key_blocks = [[block - reach + step for step in range(reach + 1)] for block in own_blocks]
     key_pos = jnp.stack(
         [jnp.concatenate([e * width + half_rows for e in blocks]) for blocks in key_blocks]
@@ -1160,67 +1467,38 @@
         ),
         (w_query, w_keyval, w_output, w_down, w_gateup),
     )
-    full_query, full_keyval, full_output = (
-        w.reshape(-1, w.shape[-1]) for w in (full_query, full_keyval, full_output)
-    )
-    grad_branch = grad_middle.astype(bf16)
-    g_output_a, g_output_b, d_inner_output = adapter_back(
-        grad_branch, attention, inner_output, output_b, mask
-    )
-    grad_attention = (by_cols(grad_branch, full_output) + by_cols(d_inner_output, output_a)).astype(
-        bf16
-    )
-    grad_query, grad_keys = att_bwd(query, keys, attention, grad_attention, prob)
-    grad_keys = grad_keys.transpose(0, 2, 1)
-    first_device = device - reach
-    slots = jnp.zeros((2 * reach + 1, local_rows, key_width), f32)
-    for which in range(2):
-        for step, entry in enumerate(key_blocks[which]):
-            piece = grad_keys[which, step * width : (step + 1) * width]
-            device_of, row_in = owner_of(entry, count, width)
-            at = (device_of - first_device, row_in, jnp.int32(0))
-            current = lax.dynamic_slice(slots, at, (1, width, key_width))
-            slots = lax.dynamic_update_slice(slots, current + piece[None], at)
-    grad_keyval_full = slots[reach]
-    for offset in range(1, reach + 1):
-        from_lower = shifted(slots[reach + offset].astype(bf16), "ctx", offset).astype(f32)
-        from_upper = shifted(slots[reach - offset].astype(bf16), "ctx", -offset).astype(f32)
-        grad_keyval_full = grad_keyval_full + from_lower + from_upper
-    grad_keyval = grad_keyval_full.astype(bf16)
-    g_query_a, g_query_b, d_inner_query = adapter_back(
-        grad_query, act_one, inner_query, query_b, mask
-    )
-    g_keyval_a, g_keyval_b, d_inner_keyval = adapter_back(
-        grad_keyval, act_one, inner_keyval, keyval_b, mask
-    )
-    grad_act_one = (
-        by_cols(grad_query, full_query)
-        + by_cols(grad_keyval, full_keyval)
-        + by_cols(d_inner_query, query_a)
-        + by_cols(d_inner_keyval, keyval_a)
-    )
-    unused, pull_one = jax.vjp(lambda values: rms_scale(values, gain_attn), resid)
-    grad_tokens = (grad_middle + pull_one(grad_act_one)[0]).astype(bf16)
-    parts = [
-        g_query_a,
-        tiles_out(g_query_b),
-        g_keyval_a,
-        tiles_out(g_keyval_b),
-        g_output_a,
-        tiles_out(g_output_b),
-        g_gateup_a,
-        g_gateup_b.reshape(-1, 128),
-        g_down_a,
-        g_down_b.reshape(-1, 128),
-    ]
-    summed = reduce_packed(pack(parts)).reshape(-1, 128)
-    sums = []
-    start = 0
-    for at, part in enumerate(parts):
-        rows = part.shape[0]
-        piece = summed[start : start + rows].astype(f32)
-        sums.append(tiles_in(piece, 128) if at % 2 else piece)
-        start += rows
+    grad_tokens, *sums = backward(
+        count,
+        (
+            grad_middle,
+            tokens,
+            mask,
+            gain_attn[None, :],
+            act_one,
+            query,
+            keys,
+            attention,
+            inner_query,
+            inner_keyval,
+            inner_output,
+            query_a,
+            query_b,
+            keyval_a,
+            keyval_b,
+            output_a,
+            output_b,
+        ),
+        (
+            g_gateup_a,
+            g_gateup_b,
+            g_down_a,
+            g_down_b,
+            prob,
+            full_query,
+            full_keyval,
+            full_output,
+        ),
+    )
     return (result, grad_tokens, *sums)
 
 

time: 510 us -> 438 us (0.86)
  Pallas kernels: 379 us -> 409 us
  matrix products: 28.5 us -> 0 us
  local copies, waits for them, and re-layouts: 45.2 us -> 19.9 us
  starting transfers between devices: 24.7 us -> 0 us
  other arithmetic: 19.9 us -> 3.35 us
    pallas_call x2 -> x1, Pallas kernels: 103 us -> 132 us  [backward(): pl.pallas_call(functools.partial(backward_kernel, count), in_specs=[VMEM]...]
    dot_general x15 -> x0, matrix products: 28.5 us -> none  [the longest x9 19.2 us: by_cols(): lax.dot_general(left, right, (((1,), (1,)), ((), ())), preferred_element_...]
    ppermute x8 -> x0, starting transfers between devices: 24.7 us -> none  [shifted(): return lax.ppermute(x, axis, pairs)]
    convert_element_type x7 -> x0, local copies, waits for them, and re-layouts: 10.2 us -> none  [the longest x6 9.14 us: pack(): parts = [g.astype(bf16) for g in grads]]
    reshape x5 -> x0, other arithmetic: 8.15 us -> none  [tiles_in(): return x.reshape(-1, rows, 128).transpose(1, 0, 2).reshape(rows, -1)]
    reshape x3 -> x0, local copies, waits for them, and re-layouts: 6.84 us -> none  [tiles_in(): return x.reshape(-1, rows, 128).transpose(1, 0, 2).reshape(rows, -1)]
    unnamed x77 -> x36, local copies, waits for them, and re-layouts: 22.6 us -> 15.8 us
    convert_element_type x3 -> x0, other arithmetic: 5.44 us -> none  [the longest x1 1.97 us: local_own(): grad_keyval = grad_keyval_full.astype(bf16)]
  transfers between devices with their start and end apart: 8 -> 0, of which waited for: 1 -> 0; matrix products, arithmetic and copies ran while one was open for 3% -> 0% of each run, Pallas kernels for 0% -> 0%
where the time goes in v4:
time: 438 us; the launch traced here: 434 us
  Pallas kernels  409 us (93%)
  local copies, waits for them, and re-layouts  19.9 us (5%)
    pallas_call x1, Pallas kernels, forward(): pl.pallas_call(functools.partial(forward_kernel, count), in_specs=[VMEM]...  277 us
    pallas_call x1, Pallas kernels, backward(): pl.pallas_call(functools.partial(backward_kernel, count), in_specs=[VMEM]...  132 us
    unnamed x36, local copies, waits for them, and re-layouts  15.8 us

profile of v4, /device:TPU:0, one launch (start us, length us, event | category | flops | bytes accessed | tf_op | source)
XLA Modules:
  0.0 433.7 jit_solution(9132849660865800132)
XLA Ops:
  0.7 0.8 reduce-window.9
  1.5 0.7 bitcast_subtract_fusion
  2.2 1.3 broadcast_in_dim.18.gain1_ref.gain_ref
  3.5 1.3 broadcast_in_dim.19.gain2_ref
  5.0 0.1 convert_reduce_fusion.1
  5.1 0.7 select_reduce_fusion
  5.8 0.1 convert_reduce_fusion
  5.9 0.6 sub.47.kseg_ref
  6.5 0.8 compare_convert_fusion.mask_ref
  7.4 0.9 copy.34.qseg_ref
  8.2 277.1 %forward.1 = (bf16[512,1536]{1,0:T(8,128)(2,1)}, f32[512,1536]{1,0:T(8,128)}, bf16[512,1536]{1,0:T(8,128)(2,1)}, bf16[512,1536]{1,0:T(8,128)(2,1)}, bf16[2,1280,...) custom-call(bf16[512,1536]{1,0:T(8,128)(2,1)} %x_ref.3, ...), custom_call_target="tpu_custom_call" | custom-call | tf_op jit(solution)/shard_map/forward/pallas_call | solution.py:923
  285.3 132.3 %backward.1 = (bf16[512,1536]{1,0:T(8,128)(2,1)}, f32[1536,128]{1,0:T(8,128)}, f32[128,1536]{1,0:T(8,128)}, f32[1536,128]{1,0:T(8,128)}, f32[128,256]{1,0:T(8,12...) custom-call(f32[512,1536]{1,0:T(8,128)} %get-tuple-element.41.dmid_r, ...), custom_call_target="tpu_custom_call" | custom-call | tf_op jit(solution)/shard_map/backward/pallas_call | solution.py:1354
  417.7 0.0 copy-start.1
  417.7 0.0 copy-start.8
  417.7 0.0 slice-start
  417.7 2.8 copy.57
  420.5 0.0 copy-done.1
  420.5 0.0 copy-start.7
  420.5 1.1 copy.58
  421.6 0.0 copy-done.8
  421.6 0.0 copy-start.6
  421.6 0.0 copy-start.9
  421.6 0.0 copy-start.5
  421.6 0.9 copy.59
  422.5 0.0 copy-done.7
  422.5 0.0 copy-start.4
  422.5 0.0 slice-start.1
  422.5 0.9 copy.60
  423.4 0.0 copy-done.6
  423.4 0.0 copy-start.3
  423.4 0.9 copy.61
  424.3 0.0 copy-done.9
  424.3 0.7 copy.62
  425.0 0.0 copy-done.5
  425.0 0.9 copy.63
  425.8 0.0 copy-done.4
  425.8 0.9 copy.64
  426.7 0.0 copy-done.3
  426.7 0.9 copy.65
  427.6 0.0 slice-done
  427.6 0.0 slice-done.1
  427.6 0.0 copy-start
  427.6 2.4 copy.66
  430.0 1.0 copy-done
  431.0 0.0 copy-start.2
  431.0 1.4 copy.67
  432.4 0.3 copy-done.2
  432.7 0.9 copy.68
  (21 shorter events, 0.1 us)
Async XLA Ops:
  417.7 2.8 copy-start.1
  417.7 4.0 copy-start.8
  417.7 9.9 %slice-start = ((s8[4718592]{0:T(1024)(128)(4,1)}), s8[4194304]{0:T(1024)(128)(4,1)S(1)}, s32[]{:S(2)}) async-start(s8[4718592]{0:T(1024)(128)(4,1)} %bitcast.4), calls=%async_computation | async-start | bytes 8388608
  420.5 2.0 copy-start.7
  421.6 1.8 copy-start.6
  421.6 2.7 copy-start.9
  421.6 3.3 copy-start.5
  422.5 3.3 copy-start.4
  422.5 5.1 %slice-start.1 = ((s8[4718592]{0:T(1024)(128)(4,1)}), s8[524288]{0:T(1024)(128)(4,1)S(1)}, s32[]{:S(2)}) async-start(s8[4718592]{0:T(1024)(128)(4,1)} %bitcast.4), calls=%async_computation.1 | async-start | bytes 1048576
  423.4 3.3 copy-start.3
  427.6 3.4 copy-start
  431.0 1.7 copy-start.2

commit v5 on v4

--- a/solution.py
+++ b/solution.py
@@ -344,9 +344,11 @@
 SUB = 128
 GROUP = 4
 SCALE = HD ** (-0.5)
-LAGS = (0, 1, 2, 4, 6)
+LAGS = (0, 2, 4, 6, 8)
 SOFT_UNROLL = 8
-AHEAD = 24
+AHEAD = 18 + LAGS[4]
+KEYS_AT = 4 + LAGS[4]
+ATT_STEPS = 8
 
 
 def dot(a, b, dims=NN):
@@ -534,33 +536,35 @@
     placed = [pltpu.make_async_copy(held[w], full[w].at[here], own_sem.at[w]) for w in range(5)]
     for copy in staged:
         copy.start()
-    state = {"step": 0, "placed": set()}
+    done_place = set()
 
     def place(w):
-        if w not in state["placed"]:
-            state["placed"].add(w)
+        if w not in done_place:
+            done_place.add(w)
             placed[w].wait()
 
+    order = []
+    for t in range(AHEAD):
+        for k in (4, 3, 2, 1, 0):
+            u = t - LAGS[k]
+            if 0 <= u < first + nu:
+                order.append((t + (4 - k) / 5, u, k))
+
     def steps(n):
-        while state["step"] < n:
-            t = state["step"]
-            state["step"] += 1
-            for k in (4, 3, 2, 1, 0):
-                u = t - LAGS[k]
-                if not 0 <= u < first + nu:
-                    continue
-                w = units[u][0] if u < first else 4
+        while order and order[0][0] < n:
+            unused, u, k = order.pop(0)
+            w = units[u][0] if u < first else 4
+            if k:
+                place(w)
+            for cl in range(2 if w == 1 else 3):
+                at = (
+                    functools.partial(exchange, u, cl)
+                    if u < first
+                    else functools.partial(gate, u - first, (u - first) % 2, cl)
+                )
                 if k:
-                    place(w)
-                for cl in range(2 if w == 1 else 3):
-                    at = (
-                        functools.partial(exchange, u, cl)
-                        if u < first
-                        else functools.partial(gate, u - first, (u - first) % 2, cl)
-                    )
-                    if k:
-                        at(k - 1).wait_recv()
-                    at(k).start()
+                    at(k - 1).wait_recv()
+                at(k).start()
 
     def loop_steps(c, point):
         for i in (2 * point, 2 * point + 1):
@@ -605,7 +609,7 @@
     iq_ref[...] = (dot(a1_ref[...], qa_ref[...]) * mask_ref[...]).astype(bf16)
     ik_ref[...] = (dot(a1_ref[...], ka_ref[...]) * mask_ref[...]).astype(bf16)
     did_s[...] = (dot(g_ref[...], db_ref[...], NT) * mask_ref[...]).astype(bf16)
-    steps(10)
+    steps(KEYS_AT)
     arrived(0)
     arrived(1)
     loads = [load(0, 0, 1024, 0, 0, 0), load(0, 1024, d - 1024, 1, 0, 0)]
@@ -674,7 +678,7 @@
         def _(j=j):
             keys_ref[0, pl.ds((reach - j) * width, width)] = jnp.zeros((width, 2 * HD), bf16)
 
-    steps(11)
+    steps(KEYS_AT + 1)
     q_ref[:, :1024] = dot(
         beside(a1_ref[...], iq_ref[...]), under(weight(0, 0, 1024), qb_ref[:, :1024])
     ).astype(bf16)
@@ -684,7 +688,7 @@
     for j in range(1, reach + 1):
         pl.when(me >= j)(incoming(0, j).wait_recv)
         pl.when(2 * me != 2 * count - 1 - j)(incoming(1, j).wait_recv)
-    steps(12)
+    steps(KEYS_AT + 2)
 
     groups = HEADS // GROUP
     subs = width // SUB
@@ -730,7 +734,7 @@
                 ).start()
                 att_ref[lines, heads] = heads_across(dot(pbuf[slot], v)).astype(bf16)
                 turn += 1
-            steps(13 + which * subs + s)
+                steps(KEYS_AT + 2 + ATT_STEPS * turn / (2 * subs * groups))
     for slot in range(2):
         pltpu.make_async_copy(
             pbuf.at[slot], prob_hbm.at[0, 0, pl.ds(0, GROUP * SUB)], psem.at[slot]
@@ -748,7 +752,7 @@
     dmid_ref[:, 1024:] = x_ref[:, 1024:].astype(f32) + dot(
         beside(att_ref[...], io_ref[...]), under(weight(1, 0, d - 1024), ob_ref[:, 1024:])
     )
-    steps(17)
+    steps(KEYS_AT + 2 + ATT_STEPS + 1)
 
     def read_mid(at):
         return dmid_ref[at, :]
@@ -956,18 +960,21 @@
     )(*small, *weights)
 
 
+ADVANCE = (6, 11)
+
+
 class Sum:
     def __init__(self, me, buf, parts, send, recv):
         self.me, self.bits = me, bits_of(me)
         self.buf, self.parts, self.send, self.recv = buf, parts, send, recv
         tiles = buf.shape[5] // 16
-        a, b = round(tiles * 3 / 7), round(tiles * 3 / 14)
-        self.split = (
-            (0, a * 16, ORD_A),
-            (a * 16, b * 16, ORD_B),
-            ((a + b) * 16, (tiles - a - b) * 16, ORD_C),
-        )
-        self.queue = [(s, cl) for s in range(1, 11) for cl in range(3)]
+        third, sixth = round(tiles / 3), round(tiles / 6)
+        sizes = (third, third, sixth, tiles - 2 * third - sixth)
+        self.split, row = [], 0
+        for n, order in zip(sizes, (ORD_A, ORD_A2, ORD_B, ORD_B2)):
+            self.split.append((row, n * 16, order))
+            row += n * 16
+        self.queue = [(s, cl) for s in range(1, 11) for cl in range(4)]
 
     def copy(self, cl, s):
         row, n, order = self.split[cl]
@@ -1013,10 +1020,10 @@
         lax.fori_loop(0, 1 << free, one, 0)
 
     def begin(self):
-        for cl in range(3):
+        for cl in range(4):
             self.copy(cl, 0).start()
 
-    def advance(self, n=1):
+    def advance(self, n=4):
         for unused in range(n):
             if not self.queue:
                 return
@@ -1187,7 +1194,7 @@
     for copy in loads:
         copy.start()
     dkv_s[...] = jnp.zeros_like(dkv_s)
-    first.advance(1)
+    first.advance()
 
     for n, (which, s, g) in enumerate(turns):
         base = s * SUB
@@ -1207,7 +1214,8 @@
         grad_s[lines, heads] = heads_across(dot(ds, k) * SCALE).astype(bf16)
         if n + 2 < len(turns):
             prob(n + 2).start()
-        first.advance(1)
+        if n in ADVANCE:
+            first.advance()
 
     def piece(which, j):
         lo = (reach - j) * width
@@ -1255,14 +1263,13 @@
         pl.when(me >= j)(low(j).start)
         copy, target = high(j)
         pl.when(target != me)(copy.start)
-    first.advance(1)
     small_s[:, :128] = (dot(grad_s[...], qb_ref[...], NT) * mask_ref[...]).astype(bf16)
     flat_two[pl.ds(0, d)] = dot(a1_ref[...], small_s[:, :128], TN).astype(bf16)
     store_tiles(flat_two, at_qb, dot(iq_ref[...], grad_s[...], TN))
     used = 3 * d + 2 * HD
     spare = flat_two.shape[0] - used
     flat_two[pl.ds(used, spare)] = jnp.zeros((spare, 128), bf16)
-    first.advance(2)
+    first.advance()
     for half in range(2):
         own = dkv_s[half, :, reach * width :].T
         acc[half * width : (half + 1) * width, : 2 * HD] = own
@@ -1289,7 +1296,7 @@
     flat_two[pl.ds(at_ka, d)] = dot(a1_ref[...], small_s[:, 128 + 2 * HD :], TN).astype(bf16)
     store_tiles(flat_two, at_kb, dot(ik_ref[...], small_s[:, 128 : 128 + 2 * HD], TN))
     second.begin()
-    first.advance(3)
+    first.advance()
     for copy in loads:
         copy.wait()
     acc[:, :d] = dot(
@@ -1297,8 +1304,8 @@
         beside(weight(0, d), qa_ref[...], weight(d, 2 * HD), ka_ref[...]),
         NT,
     )
-    first.advance(3)
-    second.advance(3)
+    second.advance()
+    first.advance()
 
     def finish(r, unused):
         at = tile_at(r, 16)
@@ -1310,16 +1317,16 @@
         return unused
 
     lax.fori_loop(0, rows // 16, finish, 0, unroll=8)
-    while first.queue or second.queue:
-        second.advance(3)
-        first.advance(3)
+    while first.queue:
+        second.advance()
+        first.advance()
 
     def take(out, flat, at, tiles):
         if tiles:
             for j in range(out.shape[1] // 128):
-                out[:, j * 128 : (j + 1) * 128] = flat[pl.ds(at + j * 128, 128)].astype(f32)
+                out[:, j * 128 : (j + 1) * 128] = flat[pl.ds(at + j * 128, 128)]
         else:
-            out[...] = flat[pl.ds(at, out.shape[0])].astype(f32)
+            out[...] = flat[pl.ds(at, out.shape[0])]
 
     take(oga_ref, flat_one, 0, False)
     take(ogb_ref, flat_one, at_ggb, True)
@@ -1327,6 +1334,7 @@
     take(odb_ref, flat_one, at_gdb, True)
     take(ooa_ref, flat_one, at_goa, False)
     take(oob_ref, flat_one, at_gob, True)
+    second.advance(40)
     take(oqa_ref, flat_two, 0, False)
     take(oqb_ref, flat_two, at_qb, True)
     take(oka_ref, flat_two, at_ka, False)
@@ -1350,7 +1358,7 @@
     five = (2,) * 5
     outs = [S((rows, d), bf16)]
     for a, b in ((d, d), (d, 2 * HD), (d, d), (d, gates), (hid, d)):
-        outs += [S((a, 128), f32), S((128, b), f32)]
+        outs += [S((a, 128), bf16), S((128, b), bf16)]
     return pl.pallas_call(
         functools.partial(backward_kernel, count),
         in_specs=[VMEM] * len(small) + [HBM] * len(large),
@@ -1371,10 +1379,10 @@
             DMA((2,)),
             DMA((2,)),
             DMA((4,)),
-            DMA((3, 10)),
-            DMA((3, 10)),
-            DMA((3, 10)),
-            DMA((3, 10)),
+            DMA((4, 10)),
+            DMA((4, 10)),
+            DMA((4, 10)),
+            DMA((4, 10)),
             DMA((2, 5)),
             DMA((2, 5)),
         ],
@@ -1499,7 +1507,7 @@
             full_output,
         ),
     )
-    return (result, grad_tokens, *sums)
+    return (result, grad_tokens, *(s.astype(f32) for s in sums))
 
 
 def solution(mesh):

time: 438 us -> 394 us (0.90)
  Pallas kernels: 409 us -> 363 us
  other arithmetic: 3.35 us -> 16.8 us
  local copies, waits for them, and re-layouts: 19.9 us -> 8.19 us
    pallas_call x1, Pallas kernels: 277 us -> 251 us  [forward(): pl.pallas_call(functools.partial(forward_kernel, count), in_specs=[VMEM]...]
    pallas_call x1, Pallas kernels: 132 us -> 112 us  [backward(): pl.pallas_call(functools.partial(backward_kernel, count), in_specs=[VMEM]...]
    convert_element_type x0 -> x10, other arithmetic: none -> 13.4 us  [local_own(): return (result, grad_tokens, *(s.astype(f32) for s in sums))]
    unnamed x36 -> x22, local copies, waits for them, and re-layouts: 15.8 us -> 4.11 us
where the time goes in v5:
time: 394 us; the launch traced here: 390 us
  Pallas kernels  363 us (92%)
  other arithmetic  16.8 us (4%)
  local copies, waits for them, and re-layouts  8.19 us (2%)
    pallas_call x1, Pallas kernels, forward(): pl.pallas_call(functools.partial(forward_kernel, count), in_specs=[VMEM]...  251 us
    pallas_call x1, Pallas kernels, backward(): pl.pallas_call(functools.partial(backward_kernel, count), in_specs=[VMEM]...  112 us
    convert_element_type x10, other arithmetic, local_own(): return (result, grad_tokens, *(s.astype(f32) for s in sums))  13.4 us

profile of v5, /device:TPU:0, one launch (start us, length us, event | category | flops | bytes accessed | tf_op | source)
XLA Modules:
  0.0 389.5 jit_solution(12451827235772585372)
XLA Ops:
  0.7 0.8 reduce-window.9
  1.5 0.7 bitcast_subtract_fusion
  2.2 1.3 broadcast_in_dim.18.gain1_ref.gain_ref
  3.5 1.3 broadcast_in_dim.19.gain2_ref
  5.0 0.1 convert_reduce_fusion.1
  5.1 0.7 select_reduce_fusion
  5.8 0.1 convert_reduce_fusion
  5.9 0.6 sub.47.kseg_ref
  6.5 0.8 compare_convert_fusion.mask_ref
  7.4 0.9 copy.34.qseg_ref
  8.2 250.8 %forward.1 = (bf16[512,1536]{1,0:T(8,128)(2,1)}, f32[512,1536]{1,0:T(8,128)}, bf16[512,1536]{1,0:T(8,128)(2,1)}, bf16[512,1536]{1,0:T(8,128)(2,1)}, bf16[2,1280,...) custom-call(bf16[512,1536]{1,0:T(8,128)(2,1)} %x_ref.3, ...), custom_call_target="tpu_custom_call" | custom-call | tf_op jit(solution)/shard_map/forward/pallas_call | solution.py:927
  259.0 112.5 %backward.1 = (bf16[512,1536]{1,0:T(8,128)(2,1)}, bf16[1536,128]{1,0:T(8,128)(2,1)}, bf16[128,1536]{1,0:T(8,128)(2,1)}, bf16[1536,128]{1,0:T(8,128)(2,1)}, bf16[...) custom-call(f32[512,1536]{1,0:T(8,128)} %get-tuple-element.41.dmid_r, ...), custom_call_target="tpu_custom_call" | custom-call | tf_op jit(solution)/shard_map/backward/pallas_call | solution.py:1362
  371.4 0.0 copy-start.9
  371.5 0.0 copy-start.8
  371.5 1.6 convert_element_type.45
  373.0 0.0 copy-start.7
  373.0 2.0 convert_element_type.42
  375.0 0.0 copy-done.9
  375.0 0.0 copy-start.6
  375.0 1.0 convert_element_type.43
  376.0 0.0 copy-done.8
  376.0 0.0 copy-start.5
  376.0 0.9 convert_element_type.44
  376.9 0.0 copy-done.7
  376.9 0.0 copy-start.4
  376.9 0.9 convert_element_type.46
  377.9 0.0 copy-done.6
  377.9 0.0 copy-start.3
  377.9 1.0 convert_element_type.47
  378.8 0.0 copy-done.5
  378.8 0.9 convert_element_type.48
  379.8 0.0 copy-done.4
  379.8 1.0 convert_element_type.51
  380.7 0.0 copy-done.3
  380.7 0.0 copy-start
  380.7 1.6 convert_element_type.50
  382.3 1.0 copy-done
  383.2 0.0 copy-start.1
  383.2 2.7 convert_element_type.49
  385.9 0.0 copy-done.1
  385.9 0.0 copy-start.2
  385.9 1.1 copy.47
  387.0 0.8 copy-done.2
  387.9 1.1 copy.48
  (20 shorter events, 0.1 us)
Async XLA Ops:
  371.4 3.6 copy-start.9
  371.5 4.5 %copy-start.8 = (bf16[1536,128]{1,0:T(8,128)(2,1)S(1)}, bf16[1536,128]{1,0:T(8,128)(2,1)}, u32[]{:S(2)}) copy-start(bf16[1536,128]{1,0:T(8,128)(2,1)} %get-tuple-element.60) | copy-start | bytes 1179652
  373.0 3.9 copy-start.7
  375.0 2.8 copy-start.6
  376.0 2.8 copy-start.5
  376.9 2.8 copy-start.4
  377.9 2.9 copy-start.3
  380.7 2.5 copy-start
  383.2 2.7 copy-start.1
  385.9 2.0 copy-start.2

commit v6 on v5

--- a/solution.py
+++ b/solution.py
@@ -27,6 +27,7 @@
 TN = (((0,), (0,)), ((), ()))
 VMEM = pl.BlockSpec(memory_space=pltpu.VMEM)
 HBM = pl.BlockSpec(memory_space=pl.ANY)
+SMEM = pl.BlockSpec(memory_space=pltpu.SMEM)
 ORD_A = (4, 3, 1, 2, 0)
 ORD_A2 = (4, 3, 2, 1, 0)
 ORD_B = (4, 1, 2, 3, 0)
@@ -348,7 +349,7 @@
 SOFT_UNROLL = 8
 AHEAD = 18 + LAGS[4]
 KEYS_AT = 4 + LAGS[4]
-ATT_STEPS = 8
+ATT_STEPS = 11
 
 
 def dot(a, b, dims=NN):
@@ -367,6 +368,27 @@
 
 def bits_of(me):
     return [(me // (1 << b)) % 2 for b in range(5)]
+
+
+def segment_at(lens_ref, pos):
+    start = jnp.int32(0)
+    seg = jnp.full(pos.shape, -1, jnp.int32)
+    for i in range(lens_ref.shape[0]):
+        seg += jnp.where(pos >= start, 1, 0)
+        start += lens_ref[i]
+    return seg
+
+
+def mask_at(lens_ref, ids_ref, count, me, rows):
+    width = rows // 2
+    row = lax.broadcasted_iota(jnp.int32, (rows, ADAPTERS * RANK), 0)
+    col = lax.broadcasted_iota(jnp.int32, (rows, ADAPTERS * RANK), 1)
+    pos = row + jnp.where(row < width, me * width, (2 * count - 2 - me) * width)
+    seg = segment_at(lens_ref, pos)
+    chosen = jnp.zeros(pos.shape, jnp.int32)
+    for i in range(ids_ref.shape[0]):
+        chosen = jnp.where(seg == i, ids_ref[i], chosen)
+    return jnp.where(col // RANK == chosen, 1.0, 0.0)
 
 
 def meet_all(count, me):
@@ -395,7 +417,7 @@
         at = tile_at(r, 16)
         x = read(at)
         scale = lax.rsqrt(jnp.mean(x * x, axis=1, keepdims=True) + NORM_EPS)
-        write(at, (x * scale * gain_ref[...]).astype(bf16))
+        write(at, (x * scale * gain_ref[...][None, :]).astype(bf16))
         return unused
 
     lax.fori_loop(0, rows // 16, block, 0, unroll=8)
@@ -405,9 +427,8 @@
     count,
     x_ref,
     g_ref,
-    mask_ref,
-    qseg_ref,
-    kseg_ref,
+    lens_ref,
+    ids_ref,
     gain1_ref,
     gain2_ref,
     qa_ref,
@@ -456,6 +477,7 @@
     a2_s,
     igu_s,
     did_s,
+    mask_ref,
     acc_o,
     acc_a,
     gu_s,
@@ -599,6 +621,8 @@
         staged[w].wait()
         placed[w].start()
     steps(4)
+    mask_ref[...] = mask_at(lens_ref, ids_ref, count, me, rows)
+
     def read_x(at):
         return x_ref[at, :].astype(f32)
 
@@ -695,6 +719,7 @@
     turn = 0
     for which in range(2):
         for s in range(subs):
+            block = me if which == 0 else 2 * count - 1 - me
             base = s * SUB
             lines = slice(which * width + base, which * width + base + SUB)
             row = lax.broadcasted_iota(jnp.int32, (SUB, span), 0)
@@ -702,7 +727,10 @@
             ok = (
                 (col <= row + (span - SUB))
                 & (col > row + (span - SUB - WINDOW))
-                & (kseg_ref[which, :, base : base + span] == qseg_ref[lines, :])
+                & (
+                    segment_at(lens_ref, block * width + base + col[:1] - reach * width)
+                    == segment_at(lens_ref, block * width + base + row[:, :1])
+                )
             )
             acc_a[:SUB, :span] = jnp.where(ok, 0.0, MASKED)
 
@@ -872,7 +900,7 @@
         at = tile_at(r, 16)
         mid = dmid_ref[at, :]
         out_ref[at, :] = (mid + acc_o[at, :d]).astype(bf16)
-        e = acc_a[at, :d] * gain2_ref[...]
+        e = acc_a[at, :d] * gain2_ref[...][None, :]
         rr = lax.rsqrt(jnp.mean(mid * mid, axis=1, keepdims=True) + NORM_EPS)
         pull = (rr * rr * rr) * jnp.mean(e * mid, axis=1, keepdims=True)
         dmid_ref[at, :] = g_ref[at, :].astype(f32) + rr * e - pull * mid
@@ -926,7 +954,7 @@
     DMA = pltpu.SemaphoreType.DMA
     return pl.pallas_call(
         functools.partial(forward_kernel, count),
-        in_specs=[VMEM] * len(small) + [HBM] * 5,
+        in_specs=[VMEM] * 2 + [SMEM] * 2 + [VMEM] * (len(small) - 4) + [HBM] * 5,
         out_specs=[VMEM] * len(outs) + [HBM] * 6,
         out_shape=outs + [S((2, width // SUB, HEADS * SUB, span), bf16)] + full,
         scratch_shapes=[pltpu.VMEM(w.shape, bf16) for w in weights]
@@ -938,6 +966,7 @@
             pltpu.VMEM((rows, d), bf16),
             pltpu.VMEM((rows, 128), bf16),
             pltpu.VMEM((rows, 128), bf16),
+            pltpu.VMEM((rows, 128), f32),
             pltpu.VMEM((rows, d + 128), f32),
             pltpu.VMEM((rows, d + 128), f32),
             pltpu.VMEM((rows, 2 * CHUNK), f32),
@@ -961,6 +990,7 @@
 
 
 ADVANCE = (6, 11)
+POINTS = ()
 
 
 class Sum:
@@ -1047,7 +1077,8 @@
     count,
     dmid_ref,
     x_ref,
-    mask_ref,
+    lens_ref,
+    ids_ref,
     gain_ref,
     a1_ref,
     q_ref,
@@ -1071,16 +1102,6 @@
     wk_all,
     wo_all,
     dx_ref,
-    oqa_ref,
-    oqb_ref,
-    oka_ref,
-    okb_ref,
-    ooa_ref,
-    oob_ref,
-    oga_ref,
-    ogb_ref,
-    oda_ref,
-    odb_ref,
     one,
     two,
     pa0,
@@ -1093,6 +1114,7 @@
     pb2,
     pb3,
     pb4,
+    mask_ref,
     wbuf,
     pbuf,
     grad_s,
@@ -1170,6 +1192,7 @@
         for j in range(x.shape[1] // 128):
             flat[pl.ds(at + j * 128, 128)] = x[:, j * 128 : (j + 1) * 128].astype(bf16)
 
+    mask_ref[...] = mask_at(lens_ref, ids_ref, count, me, rows)
     grad_s[...] = dmid_ref[...].astype(bf16)
     small_s[:, :128] = (dot(grad_s[...], ob_ref[...], NT) * mask_ref[...]).astype(bf16)
     flat_one[pl.ds(at_goa, d)] = dot(att_ref[...], small_s[:, :128], TN).astype(bf16)
@@ -1263,6 +1286,8 @@
         pl.when(me >= j)(low(j).start)
         copy, target = high(j)
         pl.when(target != me)(copy.start)
+    if 1 in POINTS:
+        first.advance()
     small_s[:, :128] = (dot(grad_s[...], qb_ref[...], NT) * mask_ref[...]).astype(bf16)
     flat_two[pl.ds(0, d)] = dot(a1_ref[...], small_s[:, :128], TN).astype(bf16)
     store_tiles(flat_two, at_qb, dot(iq_ref[...], grad_s[...], TN))
@@ -1290,6 +1315,8 @@
             incoming(1, j).wait_recv()
             acc[width:, : 2 * HD] += hin[1, j - 1].astype(f32)
 
+    if 2 in POINTS:
+        first.advance()
     small_s[:, 128 : 128 + 2 * HD] = acc[:, : 2 * HD].astype(bf16)
     dkv = small_s[:, 128 : 128 + 2 * HD]
     small_s[:, 128 + 2 * HD :] = (dot(dkv, kb_ref[...], NT) * mask_ref[...]).astype(bf16)
@@ -1310,7 +1337,7 @@
     def finish(r, unused):
         at = tile_at(r, 16)
         x = x_ref[at, :].astype(f32)
-        e = acc[at, :d] * gain_ref[...]
+        e = acc[at, :d] * gain_ref[...][None, :]
         rr = lax.rsqrt(jnp.mean(x * x, axis=1, keepdims=True) + NORM_EPS)
         pull = (rr * rr * rr) * jnp.mean(e * x, axis=1, keepdims=True)
         dx_ref[at, :] = (dmid_ref[at, :] + rr * e - pull * x).astype(bf16)
@@ -1321,24 +1348,7 @@
         second.advance()
         first.advance()
 
-    def take(out, flat, at, tiles):
-        if tiles:
-            for j in range(out.shape[1] // 128):
-                out[:, j * 128 : (j + 1) * 128] = flat[pl.ds(at + j * 128, 128)]
-        else:
-            out[...] = flat[pl.ds(at, out.shape[0])]
-
-    take(oga_ref, flat_one, 0, False)
-    take(ogb_ref, flat_one, at_ggb, True)
-    take(oda_ref, flat_one, at_gda, False)
-    take(odb_ref, flat_one, at_gdb, True)
-    take(ooa_ref, flat_one, at_goa, False)
-    take(oob_ref, flat_one, at_gob, True)
     second.advance(40)
-    take(oqa_ref, flat_two, 0, False)
-    take(oqb_ref, flat_two, at_qb, True)
-    take(oka_ref, flat_two, at_ka, False)
-    take(okb_ref, flat_two, at_kb, True)
     for j in range(1, reach + 1):
         pl.when(me >= j)(low(j).wait_send)
         copy, target = high(j)
@@ -1348,7 +1358,7 @@
 def backward(count, small, large):
     rows, d = small[0].shape
     gates, hid = large[1].shape[0] * 128, large[2].shape[0]
-    keys = small[6].shape[1]
+    keys = small[7].shape[1]
     span = keys - rows // 2 + SUB
     one = (2 * d + gates + hid + 2 * d) // 32
     two = -(-(3 * d + 2 * HD) // 512) * 16
@@ -1356,18 +1366,16 @@
     V = pltpu.VMEM
     DMA = pltpu.SemaphoreType.DMA
     five = (2,) * 5
-    outs = [S((rows, d), bf16)]
-    for a, b in ((d, d), (d, 2 * HD), (d, d), (d, gates), (hid, d)):
-        outs += [S((a, 128), bf16), S((128, b), bf16)]
+    outs = [S((rows, d), bf16), S(five + (one, 128), bf16), S(five + (two, 128), bf16)]
     return pl.pallas_call(
         functools.partial(backward_kernel, count),
-        in_specs=[VMEM] * len(small) + [HBM] * len(large),
+        in_specs=[VMEM] * 2 + [SMEM] * 2 + [VMEM] * (len(small) - 4) + [HBM] * len(large),
         out_specs=[VMEM] * len(outs),
         out_shape=outs,
-        scratch_shapes=[V(five + (one, 128), bf16), V(five + (two, 128), bf16)]
-        + [V((2,) * (4 - s) + (one, 128), bf16) for s in range(5)]
+        scratch_shapes=[V((2,) * (4 - s) + (one, 128), bf16) for s in range(5)]
         + [V((2,) * (4 - s) + (two, 128), bf16) for s in range(5)]
         + [
+            V((rows, 128), f32),
             V(five + (d // 32, d + 2 * HD), bf16),
             V((2, GROUP * SUB, span), bf16),
             V((rows, d), bf16),
@@ -1391,6 +1399,46 @@
         ),
         name="backward",
     )(*small, *large)
+
+
+def unpack_kernel(places, one_hbm, two_hbm, *refs):
+    n = len(places)
+    outs, ins, wide = refs[:n], refs[n : 2 * n], refs[2 * n : 3 * n]
+    in_sem, out_sem = refs[3 * n :]
+    flat = [one_hbm.reshape(-1, 128), two_hbm.reshape(-1, 128)]
+    reads = [
+        pltpu.make_async_copy(flat[w].at[pl.ds(at, ins[i].shape[0])], ins[i], in_sem.at[i])
+        for i, (w, at, tiled) in enumerate(places)
+    ]
+    writes = [pltpu.make_async_copy(wide[i], outs[i], out_sem.at[i]) for i in range(n)]
+    for copy in reads:
+        copy.start()
+    for i, (w, at, tiled) in enumerate(places):
+        reads[i].wait()
+        if tiled:
+            for j in range(wide[i].shape[1] // 128):
+                wide[i][:, j * 128 : (j + 1) * 128] = ins[i][pl.ds(j * 128, 128)].astype(f32)
+        else:
+            wide[i][...] = ins[i][...].astype(f32)
+        writes[i].start()
+    for copy in writes:
+        copy.wait()
+
+
+def unpack(one, two, shapes, places):
+    rows = [a * b // 128 for a, b in shapes]
+    n = len(shapes)
+    return pl.pallas_call(
+        functools.partial(unpack_kernel, places),
+        in_specs=[HBM] * 2,
+        out_specs=[HBM] * n,
+        out_shape=[jax.ShapeDtypeStruct(s, f32) for s in shapes],
+        scratch_shapes=[pltpu.VMEM((r, 128), bf16) for r in rows]
+        + [pltpu.VMEM(s, f32) for s in shapes]
+        + [pltpu.SemaphoreType.DMA((n,)), pltpu.SemaphoreType.DMA((n,))],
+        compiler_params=pltpu.CompilerParams(vmem_limit_bytes=40 << 20),
+        name="unpack",
+    )(one, two)
 
 
 def local_own(
@@ -1417,21 +1465,6 @@
     down_b,
 ):
     count = lax.axis_size("ctx")
-    device = lax.axis_index("ctx")
-    local_rows = tokens.shape[0]
-    width = local_rows // 2
-    reach = (WINDOW + width - 1) // width
-    half_rows = jnp.arange(width, dtype=jnp.int32)
-    own_blocks = (device, 2 * count - 1 - device)
-    positions = jnp.concatenate(
-        [own_blocks[0] * width + half_rows, own_blocks[1] * width + half_rows]
-    )
-    segment, mask = adapter_mask(doc_lengths, adapter_ids, positions)
-    key_blocks = [[block - reach + step for step in range(reach + 1)] for block in own_blocks]
-    key_pos = jnp.stack(
-        [jnp.concatenate([e * width + half_rows for e in blocks]) for blocks in key_blocks]
-    )
-    key_seg = segment_of(doc_lengths, key_pos.reshape(-1)).reshape(2, 1, -1)
     (
         result,
         grad_middle,
@@ -1457,11 +1490,10 @@
         (
             tokens,
             cotangent,
-            mask,
-            segment[:, None],
-            key_seg,
-            gain_attn[None, :],
-            gain_mlp[None, :],
+            doc_lengths,
+            adapter_ids,
+            gain_attn,
+            gain_mlp,
             query_a,
             query_b,
             keyval_a,
@@ -1475,13 +1507,14 @@
         ),
         (w_query, w_keyval, w_output, w_down, w_gateup),
     )
-    grad_tokens, *sums = backward(
+    grad_tokens, first, second = backward(
         count,
         (
             grad_middle,
             tokens,
-            mask,
-            gain_attn[None, :],
+            doc_lengths,
+            adapter_ids,
+            gain_attn,
             act_one,
             query,
             keys,
@@ -1507,7 +1540,24 @@
             full_output,
         ),
     )
-    return (result, grad_tokens, *(s.astype(f32) for s in sums))
+    d, hid, gates = w_output.shape[1], down_a.shape[0], gateup_b.shape[1]
+    kv = w_keyval.shape[1]
+    shapes = [(d, 128), (128, d), (d, 128), (128, kv), (d, 128), (128, d)]
+    shapes += [(d, 128), (128, gates), (hid, 128), (128, d)]
+    places = [
+        (1, 0, False),
+        (1, d, True),
+        (1, 2 * d, False),
+        (1, 3 * d, True),
+        (0, 2 * d + gates + hid, False),
+        (0, 3 * d + gates + hid, True),
+        (0, 0, False),
+        (0, d, True),
+        (0, d + gates, False),
+        (0, d + gates + hid, True),
+    ]
+    sums = unpack(first, second, shapes, places)
+    return (result, grad_tokens, *sums)
 
 
 def solution(mesh):

time: 394 us -> 385 us (0.977)
  other arithmetic: 16.8 us -> 0 us
  Pallas kernels: 363 us -> 372 us
    convert_element_type x11 -> x0, other arithmetic: 14.3 us -> none  [the longest x10 13.4 us: local_own(): return (result, grad_tokens, *(s.astype(f32) for s in sums))]
    pallas_call x0 -> x1, Pallas kernels: none -> 6.61 us  [unpack(): pl.pallas_call(functools.partial(unpack_kernel, places), in_specs=[HBM] *...]
where the time goes in v6:
time: 385 us; the launch traced here: 380 us
  Pallas kernels  372 us (97%)
  local copies, waits for them, and re-layouts  6.87 us (2%)
    pallas_call x1, Pallas kernels, forward(): pl.pallas_call(functools.partial(forward_kernel, count), in_specs=[VMEM]...  250 us
    pallas_call x1, Pallas kernels, backward(): pl.pallas_call(functools.partial(backward_kernel, count), in_specs=[VMEM]...  115 us

profile of v6, /device:TPU:0, one launch (start us, length us, event | category | flops | bytes accessed | tf_op | source)
XLA Modules:
  0.0 380.2 jit_solution(1986269456562617660)
XLA Ops:
  0.6 250.1 %forward.1 = (bf16[512,1536]{1,0:T(8,128)(2,1)}, f32[512,1536]{1,0:T(8,128)}, bf16[512,1536]{1,0:T(8,128)(2,1)}, bf16[512,1536]{1,0:T(8,128)(2,1)}, bf16[2,1280,...) custom-call(bf16[512,1536]{1,0:T(8,128)(2,1)} %x_ref.3, ...), custom_call_target="tpu_custom_call" | custom-call | tf_op jit(solution)/shard_map/forward/pallas_call | solution.py:955
  250.7 115.4 %backward.1 = (bf16[512,1536]{1,0:T(8,128)(2,1)}, bf16[2,2,2,2,2,624,128]{6,5,4,3,2,1,0:T(8,128)(2,1)}, bf16[2,2,2,2,2,160,128]{6,5,4,3,2,1,0:T(8,128)(2,1)}) custom-call(f32[512,1536]{1,0:T(8,128)} %get-tuple-element.43.dmid_ref, bf16[512,1536]{1,0:T(8,128)(2,1)} %x_ref.3, s32[8]{0:T(128)} %lens_ref.3, s32[8]{0:T(128)} %ids_ref.3, f32[1536]{0:T(1024)} %gain_ref.1, ...), custom_call_target="tpu_custom_call" | custom-call | tf_op jit(solution)/shard_map/backward/pallas_call | solution.py:1370
  366.2 0.0 copy-start
  366.2 2.4 copy-done
  368.6 0.0 copy-start.1
  368.6 1.3 copy-done.1
  369.9 0.0 copy-start.2
  369.9 6.6 %unpack.1 = (f32[1536,128]{1,0:T(8,128)}, f32[128,1536]{1,0:T(8,128)}, f32[1536,128]{1,0:T(8,128)}, f32[128,256]{1,0:T(8,128)}, f32[1536,128]{1,0:T(8,128)}, /*i...) custom-call(bf16[2,2,2,2,2,624,128]{6,5,4,3,2,1,0:T(8,128)(2,1)S(1)}, ...), custom_call_target="tpu_custom_call" | custom-call | tf_op jit(solution)/shard_map/unpack/pallas_call | solution.py:1431
  376.5 0.0 copy-done.2
  376.6 0.0 copy-start.3
  376.6 1.1 copy.35
  377.7 0.8 copy-done.3
  378.5 1.1 copy.36
Async XLA Ops:
  366.2 2.5 copy-start
  368.6 1.3 copy-start.1
  369.9 6.6 %copy-start.2 = (bf16[512,1536]{1,0:T(8,128)(2,1)S(1)}, bf16[512,1536]{1,0:T(8,128)(2,1)}, u32[]{:S(2)}) copy-start(bf16[512,1536]{1,0:T(8,128)(2,1)} %get-tuple-element.84) | copy-start | bytes 4718596
  376.6 2.0 copy-start.3

commit v7 on v6

--- a/solution.py
+++ b/solution.py
@@ -438,8 +438,8 @@
     oa_ref,
     ob_ref,
     ga_ref,
-    gb_ref,
-    da_ref,
+    gb_hbm,
+    da_hbm,
     db_ref,
     wq_own,
     wk_own,
@@ -448,10 +448,10 @@
     wg_own,
     out_ref,
     dmid_ref,
-    a1_ref,
-    q_ref,
-    keys_ref,
-    att_ref,
+    a1_hbm,
+    q_hbm,
+    keys_hbm,
+    att_hbm,
     iq_ref,
     ik_ref,
     io_ref,
@@ -477,6 +477,12 @@
     a2_s,
     igu_s,
     did_s,
+    a1_ref,
+    q_ref,
+    keys_ref,
+    att_ref,
+    gb_ref,
+    da_ref,
     mask_ref,
     acc_o,
     acc_a,
@@ -492,13 +498,14 @@
     xrecv,
     hsend,
     hrecv,
+    late_sem,
 ):
     rows, d = x_ref.shape
     width = rows // 2
     reach = WINDOW // width
     keys = keys_ref.shape[1]
     span = keys - width + SUB
-    ff = da_ref.shape[0]
+    ff = da_hbm.shape[0]
     nu, nc = ff // UNIT, ff // CHUNK
     me = lax.axis_index("ctx")
     bits = bits_of(me)
@@ -558,6 +565,21 @@
     placed = [pltpu.make_async_copy(held[w], full[w].at[here], own_sem.at[w]) for w in range(5)]
     for copy in staged:
         copy.start()
+    late = [
+        pltpu.make_async_copy(src, dst, late_sem.at[i])
+        for i, (src, dst) in enumerate(
+            (
+                (gb_hbm, gb_ref),
+                (da_hbm, da_ref),
+                (a1_ref, a1_hbm),
+                (q_ref, q_hbm),
+                (keys_ref, keys_hbm),
+                (att_ref, att_hbm),
+            )
+        )
+    ]
+    late[0].start()
+    late[1].start()
     done_place = set()
 
     def place(w):
@@ -633,6 +655,7 @@
     iq_ref[...] = (dot(a1_ref[...], qa_ref[...]) * mask_ref[...]).astype(bf16)
     ik_ref[...] = (dot(a1_ref[...], ka_ref[...]) * mask_ref[...]).astype(bf16)
     did_s[...] = (dot(g_ref[...], db_ref[...], NT) * mask_ref[...]).astype(bf16)
+    late[2].start()
     steps(KEYS_AT)
     arrived(0)
     arrived(1)
@@ -712,6 +735,8 @@
     for j in range(1, reach + 1):
         pl.when(me >= j)(incoming(0, j).wait_recv)
         pl.when(2 * me != 2 * count - 1 - j)(incoming(1, j).wait_recv)
+    late[3].start()
+    late[4].start()
     steps(KEYS_AT + 2)
 
     groups = HEADS // GROUP
@@ -767,6 +792,7 @@
         pltpu.make_async_copy(
             pbuf.at[slot], prob_hbm.at[0, 0, pl.ds(0, GROUP * SUB)], psem.at[slot]
         ).wait()
+    late[5].start()
     arrived(2)
     loads = [load(2, 0, 1024, 0, 0, 0), load(2, 1024, d - 1024, 1, 0, 0)]
     for copy in loads:
@@ -821,6 +847,8 @@
         at = base + c * CHUNK
         return pl.ds(at if isinstance(at, int) else pl.multiple_of(at, 128), CHUNK)
 
+    late[0].wait()
+    late[1].wait()
     arrived_gate(0)
     for copy in fetch(0, 0):
         copy.start()
@@ -911,6 +939,8 @@
         copy, target = low(j)
         pl.when(target != me)(copy.wait_send)
         pl.when(me >= j)(high(j).wait_send)
+    for copy in late[2:]:
+        copy.wait()
     for u, unit in enumerate(units):
         for cl in range(len(unit[2])):
             for k in range(5):
@@ -954,8 +984,13 @@
     DMA = pltpu.SemaphoreType.DMA
     return pl.pallas_call(
         functools.partial(forward_kernel, count),
-        in_specs=[VMEM] * 2 + [SMEM] * 2 + [VMEM] * (len(small) - 4) + [HBM] * 5,
-        out_specs=[VMEM] * len(outs) + [HBM] * 6,
+        in_specs=[VMEM] * 2
+        + [SMEM] * 2
+        + [VMEM] * (len(small) - 7)
+        + [HBM] * 2
+        + [VMEM]
+        + [HBM] * 5,
+        out_specs=[VMEM] * 2 + [HBM] * 4 + [VMEM] * (len(outs) - 6) + [HBM] * 6,
         out_shape=outs + [S((2, width // SUB, HEADS * SUB, span), bf16)] + full,
         scratch_shapes=[pltpu.VMEM(w.shape, bf16) for w in weights]
         + [
@@ -966,6 +1001,12 @@
             pltpu.VMEM((rows, d), bf16),
             pltpu.VMEM((rows, 128), bf16),
             pltpu.VMEM((rows, 128), bf16),
+            pltpu.VMEM((rows, d), bf16),
+            pltpu.VMEM((rows, d), bf16),
+            pltpu.VMEM((2, keys, 2 * HD), bf16),
+            pltpu.VMEM((rows, d), bf16),
+            pltpu.VMEM((128, 2 * ff), bf16),
+            pltpu.VMEM((ff, 128), bf16),
             pltpu.VMEM((rows, 128), f32),
             pltpu.VMEM((rows, d + 128), f32),
             pltpu.VMEM((rows, d + 128), f32),
@@ -981,6 +1022,7 @@
             DMA((16 + nu, 3, 5)),
             DMA((2, 5)),
             DMA((2, 5)),
+            DMA((6,)),
         ],
         compiler_params=pltpu.CompilerParams(
             collective_id=0, has_side_effects=True, vmem_limit_bytes=63 << 20

time: 385 us -> 383 us (level)
  no operation moved by 1% of the time
where the time goes in v7:
time: 383 us; the launch traced here: 379 us
  Pallas kernels  371 us (97%)
  local copies, waits for them, and re-layouts  6.87 us (2%)
    pallas_call x1, Pallas kernels, forward(): pl.pallas_call(functools.partial(forward_kernel, count), in_specs=[VMEM]...  249 us
    pallas_call x1, Pallas kernels, backward(): pl.pallas_call(functools.partial(backward_kernel, count), in_specs=[VMEM]...  115 us

profile of v7, /device:TPU:0, one launch (start us, length us, event | category | flops | bytes accessed | tf_op | source)
XLA Modules:
  0.0 378.9 jit_solution(9705743227436380672)
XLA Ops:
  0.6 248.9 %forward.1 = (bf16[512,1536]{1,0:T(8,128)(2,1)}, f32[512,1536]{1,0:T(8,128)}, bf16[512,1536]{1,0:T(8,128)(2,1)}, bf16[512,1536]{1,0:T(8,128)(2,1)}, bf16[2,1280,...) custom-call(bf16[512,1536]{1,0:T(8,128)(2,1)} %x_ref.3, ...), custom_call_target="tpu_custom_call" | custom-call | tf_op jit(solution)/shard_map/forward/pallas_call | solution.py:985
  249.5 115.3 %backward.1 = (bf16[512,1536]{1,0:T(8,128)(2,1)}, bf16[2,2,2,2,2,624,128]{6,5,4,3,2,1,0:T(8,128)(2,1)}, bf16[2,2,2,2,2,160,128]{6,5,4,3,2,1,0:T(8,128)(2,1)}) custom-call(f32[512,1536]{1,0:T(8,128)} %get-tuple-element.43.dmid_ref, bf16[512,1536]{1,0:T(8,128)(2,1)} %x_ref.3, s32[8]{0:T(128)} %lens_ref.3, s32[8]{0:T(128)} %ids_ref.3, f32[1536]{0:T(1024)} %gain_ref.1, ...), custom_call_target="tpu_custom_call" | custom-call | tf_op jit(solution)/shard_map/backward/pallas_call | solution.py:1412
  364.9 0.0 copy-start
  364.9 2.4 copy-done
  367.3 0.0 copy-start.1
  367.3 1.3 copy-done.1
  368.6 0.0 copy-start.2
  368.7 6.6 %unpack.1 = (f32[1536,128]{1,0:T(8,128)}, f32[128,1536]{1,0:T(8,128)}, f32[1536,128]{1,0:T(8,128)}, f32[128,256]{1,0:T(8,128)}, f32[1536,128]{1,0:T(8,128)}, /*i...) custom-call(bf16[2,2,2,2,2,624,128]{6,5,4,3,2,1,0:T(8,128)(2,1)S(1)}, ...), custom_call_target="tpu_custom_call" | custom-call | tf_op jit(solution)/shard_map/unpack/pallas_call | solution.py:1473
  375.3 0.0 copy-done.2
  375.3 0.0 copy-start.3
  375.3 1.1 copy.35
  376.4 0.8 copy-done.3
  377.3 1.1 copy.36
Async XLA Ops:
  364.9 2.5 copy-start
  367.3 1.3 copy-start.1
  368.6 6.6 %copy-start.2 = (bf16[512,1536]{1,0:T(8,128)(2,1)S(1)}, bf16[512,1536]{1,0:T(8,128)(2,1)}, u32[]{:S(2)}) copy-start(bf16[512,1536]{1,0:T(8,128)(2,1)} %get-tuple-element.84) | copy-start | bytes 4718596
  375.3 2.0 copy-start.3
